TPU v7x, 32 devices: a whole 2x2x4 slice. The times are simulated.
32 devices in a mesh: rows: 8 (over z, y), blk: 4 (over x, core).
Axes of the slice: x: 2, y: 2, z: 4, core: 2. Of those that a mesh axis runs over, the one named last changes fastest.
Arguments:
- block_input: bfloat16 [16, 256, 1536], P('rows', 'blk'), may hold values from -6 to 6
- cotangent: bfloat16 [16, 256, 1536], P('rows', 'blk'), may hold values from -6 to 6
- query_w: float32 [1536, 768], P(('rows', 'blk')), may hold values from -0.0390625 to 0.0390625
- key_w: float32 [1536, 768], P(('rows', 'blk')), may hold values from -0.15625 to 0.15625
- value_w: float32 [1536, 768], P(('rows', 'blk')), may hold values from -0.15625 to 0.15625
- output_w: float32 [768, 1536], P(None, ('rows', 'blk')), may hold values from -1.25 to 1.25
- gate_w: float32 [1536, 3968], P(('rows', 'blk')), may hold values from -0.15625 to 0.15625
- up_w: float32 [1536, 3968], P(('rows', 'blk')), may hold values from -0.15625 to 0.15625
- down_w: float32 [3968, 1536], P(None, ('rows', 'blk')), may hold values from -0.09375 to 0.09375
- first_gain: float32 [1536], P(('rows', 'blk')), may hold values from 0.5 to 1.5
- second_gain: float32 [1536], P(('rows', 'blk')), may hold values from 0.5 to 1.5
- bias_table: float32 [32, 12], replicated, may hold values from -4 to 4
- rel_bucket: int32 [512], replicated, may hold values from 0 to 31
- doc_ids: int32 [16, 256], P('rows'), may hold values from 0 to 1, as said below
Outputs:
- block_output: bfloat16 [16, 256, 1536], P('rows', 'blk')
- input_grad: float32 [16, 256, 1536], P('rows', 'blk')
- query_grad: float32 [1536, 768], P(('rows', 'blk'))
- key_grad: float32 [1536, 768], P(('rows', 'blk'))
- value_grad: float32 [1536, 768], P(('rows', 'blk'))
- output_grad: float32 [768, 1536], P(None, ('rows', 'blk'))
- gate_grad: float32 [1536, 3968], P(('rows', 'blk'))
- up_grad: float32 [1536, 3968], P(('rows', 'blk'))
- down_grad: float32 [3968, 1536], P(None, ('rows', 'blk'))
- first_grad: float32 [1536], P(('rows', 'blk'))
- second_grad: float32 [1536], P(('rows', 'blk'))
- table_grad: float32 [32, 12], replicated
Inputs may be any that keep to these rules, and one draw needn't show every extreme that they name: `doc_ids`: each row is either one document of 256 positions (all ids 0) or 2 documents of 128 positions with ids rising from 0; the first row is of the second kind and the second row of the first.
All inputs are finite; a program needn't handle non-finite values.
Results may differ from a plain program's by a relative error of at most 0.024.
Values may be sent and summed in bfloat16 or wider, within the bound.
No kernel may reach another device: no remote copies, remote signals or barrier semaphores. Data moves between devices by JAX's collectives and lax.ppermute only.
A program may use at most 256 MiB of HBM per device.

v0:
```python
import math

import jax
import jax.numpy as jnp
from jax import lax
from jax.experimental import pallas as pl
from jax.experimental.pallas import tpu as pltpu
from jax.sharding import Mesh, PartitionSpec as P

EPSILON = 1e-06
BF = jnp.bfloat16
F32 = jnp.float32
HIGHEST = lax.Precision.HIGHEST
RING = ("rows", "seq")
MAX_RING = 8
EXTRA = 16
PADS = (8, 6, 4)
RPADS = (8, 4, 8)
CUTS = (2, 1)
FREE = pl.CostEstimate(flops=0, transcendentals=0, bytes_accessed=0)


def dot(left, right, dims, out=F32):
    return lax.dot_general(left, right, (dims, ((), ())), preferred_element_type=out)


NN = ((1,), (0,))
NT = ((1,), (1,))
TN = ((0,), (0,))


def ring_order(count):
    return list(range(0, count, 2)) + list(range(count - 1, 0, -2))


def ring_places(count):
    half = count // 2
    group = lax.axis_index(RING)
    place = jnp.where(group % 2 == 0, group // 2, count - 1 - group // 2)
    places = []
    for k in range(count):
        at = place - k
        at = jnp.where(at < 0, at + count, at)
        places.append(jnp.where(at < half, 2 * at, 2 * (count - 1 - at) + 1))
    return places


def ring_ok(count):
    return count <= MAX_RING and count % 2 == 0


class Lanes:
    def __init__(self, count, ways):
        order = ring_order(count)
        self.pairs = {
            step: [(order[i], order[(i + step) % count]) for i in range(count)] for step in (1, -1)
        }
        self.count, self.ways, self.last = count, ways, None

    def pin(self, *values):
        if self.last is not None:
            values = lax.optimization_barrier((*values, self.last))[:-1]
        self.last = values[0]
        return values if len(values) > 1 else values[0]

    def shift(self, value, step):
        return lax.ppermute(value, RING, self.pairs[step])

    def partner(self, value, bit):
        return lax.ppermute(value, "tp", [(i, i ^ bit) for i in range(self.ways)])


class Task:
    def __init__(self, steps):
        self.steps, self.value = steps, None

    def step(self):
        if self.steps is not None:
            try:
                next(self.steps)
            except StopIteration as stop:
                self.value, self.steps = stop.value, None

    def result(self):
        while self.steps is not None:
            self.step()
        return self.value


def gather_ring(lanes, chunk, keep, lead):
    count = lanes.count
    if not ring_ok(count):
        got = lax.all_gather(chunk, RING, axis=0) if count > 1 else chunk[None]
        return got[:, :keep].reshape(-1, chunk.shape[1]), [got[i] for i in range(count)]
    chunk = lanes.pin(chunk)
    moving = {lead: chunk, -lead: chunk}
    got = [chunk]
    for k in range(1, count // 2):
        moving = {step: lanes.shift(value, step) for step, value in moving.items()}
        yield
        moving = dict(zip(moving, lanes.pin(*moving.values())))
        got += [moving[1], moving[-1]]
    last = lanes.shift(moving[lead], lead)
    yield
    got.append(lanes.pin(last))
    return place_rows(got, count, keep), got


def chunk_order(count):
    order = [0]
    for k in range(1, count // 2):
        order += [k, count - k]
    return order + [count // 2]


def place_rows(got, count, keep):
    def body(*refs):
        places = ring_places(count)
        for ref, k in zip(refs, chunk_order(count)):
            refs[-1][pl.ds(pl.multiple_of(places[k] * keep, keep), keep), :] = ref[:keep]

    return near(body, got, [((count * keep, got[0].shape[1]), BF)])[0]


def scatter_ring(lanes, blocks, lead, rows):
    count, size, _ = blocks.shape
    if count == 1:
        return blocks[0]
    if not ring_ok(count):
        return lax.psum_scatter(blocks, RING, scatter_dimension=0, tiled=True)[0]
    (far,) = add_blocks(blocks, [(count // 2, None)], rows)
    moving = {lead: lanes.shift(lanes.pin(far), lead)}
    yield
    for j in range(count // 2 - 1, 0, -1):
        arrived = dict(zip(moving, lanes.pin(*moving.values()) if len(moving) > 1 else (lanes.pin(moving[lead]),)))
        sums = add_blocks(blocks, [(-j * step, arrived.get(step)) for step in (1, -1)], rows)
        moving = {step: lanes.shift(value, step) for step, value in zip((1, -1), lanes.pin(*sums))}
        yield
    came, back = lanes.pin(*moving.values())
    return add_blocks(blocks, [(0, came)], size, back)[0]


def add_blocks(blocks, terms, rows, more=None):
    count, size, width = blocks.shape
    came = [c for _, c in terms if c is not None] + ([] if more is None else [more])

    def body(blocks_ref, *refs):
        places = ring_places(count)
        given, outs = list(refs[: len(came)]), refs[len(came) :]
        for (k, c), out in zip(terms, outs):
            total = blocks_ref[places[k % count]].astype(F32)
            if c is not None:
                total = total + given.pop(0)[:size].astype(F32)
            if more is not None:
                total = total + given.pop(0)[:size].astype(F32)
            out[:size] = total.astype(BF)
            if rows > size:
                out[size:] = jnp.zeros((rows - size, width), BF)

    return near(body, [blocks, *came], [((rows, width), BF)] * len(terms))


def block_of(index):
    return index % 2 * 2 + index // 2


def gather_tokens(lanes, value, cuts):
    value = lanes.pin(value)
    got = lanes.partner(value, 2)
    yield
    value = jnp.concatenate([value, lanes.pin(got)], axis=0)
    got = yield from over_core(lanes, value, cuts)
    return jnp.concatenate([value, *got], axis=0)


def over_core(lanes, give, cuts):
    rows, pieces, first = give.shape[0], [], 0
    for n in range(cuts):
        last = rows * (n + 1) // cuts // 16 * 16 if n + 1 < cuts else rows
        got = lanes.partner(lanes.pin(give[first:last]), 1)
        yield
        pieces.append(lanes.pin(got))
        first = last
    return pieces


def sum_tokens(lanes, keep, give, cuts):
    got = yield from over_core(lanes, give, cuts)
    low = lanes.pin(add_halves(keep, got, False))
    got = lanes.partner(low, 2)
    yield
    low = lanes.pin(add_halves(low, [lanes.pin(got)], True))
    got = yield from over_core(lanes, low, cuts)
    return low, got


def add_halves(left, pieces, swapped):
    rows = left.shape[0]
    half = rows // 2

    def body(left_ref, *refs):
        first = 0
        for ref in refs[:-1]:
            for at in range(0, ref.shape[0], half if swapped else ref.shape[0]):
                count = half if swapped else ref.shape[0]
                to = half - at if swapped else first + at
                total = left_ref[to : to + count].astype(F32) + ref[at : at + count].astype(F32)
                refs[-1][to : to + count] = total.astype(BF)
            first += ref.shape[0]

    return near(body, [left, *pieces], [(left.shape, BF)])[0]


def scatter_tokens(lanes, keep, give, cuts):
    got = yield from over_core(lanes, give, cuts)
    low = lanes.pin(add_halves(keep, got, False))
    mine = low.shape[0] // 2
    got = lanes.partner(low[mine:], 2)
    yield
    return low[:mine], lanes.pin(got)


def exchange(lanes, blocks, at_once=True):
    pieces = [blocks[0]] + [None] * 3
    for k in (2, 3, 1):
        pieces[k] = lanes.partner(lanes.pin(blocks[k]), k)
        if not at_once:
            yield
    if at_once:
        yield
    pieces[1:] = lanes.pin(*pieces[1:])
    return pieces


def by_member(pieces):
    own, chosen = lax.axis_index("tp"), []
    for a in range(4):
        piece = pieces[a]
        for mine in range(1, 4):
            piece = jnp.where(own == mine, pieces[a ^ mine], piece)
        chosen.append(piece)
    return chosen


def stack_members(pieces, widths, pads):
    depth = pieces[0].shape[0]
    if depth % 16:
        pieces = jnp.concatenate(by_member(pieces), axis=0)
        starts = [sum(widths[:i]) for i in range(len(widths))]
        return [jnp.pad(pieces[:, a : a + w], ((0, p), (0, 0))) for a, w, p in zip(starts, widths, pads)]

    def body(*refs):
        own = lax.axis_index("tp")
        at = 0
        for width, pad, out in zip(widths, pads, refs[4:]):
            for k in range(4):
                out[pl.ds(pl.multiple_of((own ^ k) * depth, depth), depth), :] = refs[k][:, at : at + width]
            if pad:
                out[4 * depth :] = jnp.zeros((pad, width), BF)
            at += width

    return near(body, pieces, [((4 * depth + pad, width), BF) for width, pad in zip(widths, pads)])


def stack_attn(pieces, chunk):
    depth, width = chunk // 4, pieces[0].shape[1]
    if depth % 16:
        pieces = by_member(pieces)
        gains = jnp.concatenate([p[depth : depth + 2, :depth] for p in pieces], axis=1)
        gains = jnp.pad(gains, ((0, EXTRA - 2), (0, width - chunk)))
        return jnp.concatenate([p[:depth] for p in pieces] + [gains], axis=0)

    def body(*refs):
        own, out, gains_ref = lax.axis_index("tp"), refs[4], refs[5]
        for k in range(4):
            out[pl.ds(pl.multiple_of((own ^ k) * depth, depth), depth), :] = refs[k][:depth]
            gains_ref[own ^ k] = refs[k][depth:, :depth].astype(F32)
        gains = [gains_ref[a] for a in range(4)] + [jnp.zeros((EXTRA, width - chunk), F32)]
        out[chunk:] = jnp.concatenate(gains, axis=1).astype(BF)

    return near(body, pieces, [((chunk + EXTRA, width), BF)], [pltpu.VMEM((4, EXTRA, depth), F32)])[0]


def split_attn(total, depth, width):
    chunk = 4 * depth
    if depth % 16:
        tables = jnp.pad(total[chunk + 2 : chunk + 3], ((2, EXTRA - 3), (0, 0)))
        blocks = []
        for large, pair in zip(rows_of([total], depth), rows_of([total[chunk : chunk + 2, :chunk].T], depth)):
            pair = jnp.pad(pair.T, ((0, EXTRA - 2), (0, 4 * width - depth)))
            blocks.append(jnp.concatenate([large, pair + tables], axis=0))
        return blocks

    def body(total_ref, *refs):
        own, small_ref = lax.axis_index("tp"), refs[4]
        fill = jnp.zeros((2, 4 * width - depth), F32)
        small = total_ref[chunk : chunk + EXTRA].astype(F32)
        below = jnp.concatenate([small[2:3], jnp.zeros((EXTRA - 3, 4 * width), F32)], axis=0)
        for a in range(4):
            pair = jnp.concatenate([small[0:2, a * depth : (a + 1) * depth], fill], axis=1)
            small_ref[a] = jnp.concatenate([pair, below], axis=0)
        for k in range(4):
            refs[k][:depth] = total_ref[pl.ds(pl.multiple_of((own ^ k) * depth, depth), depth), :]
            refs[k][depth:] = small_ref[own ^ k].astype(BF)

    return near(
        body, [total], [((depth + EXTRA, 4 * width), BF)] * 4, [pltpu.VMEM((4, EXTRA, 4 * width), F32)]
    )


def run(body, grid, ins, outs, scratch=(), vmem=24):
    def spec(block, index_map):
        return pl.BlockSpec(block, index_map)

    arrays, in_specs = [], []
    for item in ins:
        array, block, index_map = item if isinstance(item, tuple) else (item, item.shape, None)
        if index_map is None:
            index_map = lambda *_, n=array.ndim: (0,) * n
        arrays.append(array)
        in_specs.append(spec(block, index_map))
    out_specs = [
        spec(block or shape, index_map or (lambda *_, n=len(shape): (0,) * n)) for shape, _, block, index_map in outs
    ]
    return pl.pallas_call(
        body, grid=grid, in_specs=in_specs, out_specs=out_specs,
        out_shape=[jax.ShapeDtypeStruct(shape, dtype) for shape, dtype, _, _ in outs],
        scratch_shapes=list(scratch),
        compiler_params=pltpu.CompilerParams(
            dimension_semantics=("arbitrary",) * len(grid), vmem_limit_bytes=vmem << 20
        ),
        cost_estimate=FREE,
    )(*arrays)


def near(body, arrays, outs, scratch=(), vmem=16):
    spec = pl.BlockSpec(memory_space=pltpu.VMEM)
    return pl.pallas_call(
        body, in_specs=[spec] * len(arrays), out_specs=[spec] * len(outs),
        out_shape=[jax.ShapeDtypeStruct(shape, dtype) for shape, dtype in outs],
        scratch_shapes=list(scratch),
        compiler_params=pltpu.CompilerParams(vmem_limit_bytes=vmem << 20),
        cost_estimate=FREE,
    )(*arrays)


def far(arrays):
    return [pltpu.with_memory_space_constraint(a, pltpu.HBM) for a in arrays]


def whole(shape, dtype):
    return (shape, dtype, None, None)


def pack_attn(weights, gains, width):
    depth, inner = weights[0].shape

    def body(q_ref, k_ref, v_ref, o_ref, first_ref, second_ref, *rest):
        outs, out_ref = rest[:4], rest[4]
        own = lax.axis_index("tp")
        extra = jnp.concatenate([first_ref[...], second_ref[...], jnp.zeros((EXTRA - 2, depth), F32)], axis=0)
        extra = jnp.concatenate([extra, jnp.zeros((EXTRA, 4 * width - depth), F32)], axis=1).astype(BF)
        for a in range(4):
            parts = [r[:, a * width : (a + 1) * width] for r in (q_ref, k_ref, v_ref, o_ref)]
            out_ref[a ^ own, :depth] = jnp.concatenate(parts, axis=1).astype(BF)
            out_ref[a ^ own, depth:] = extra
        for k in range(4):
            outs[k][...] = out_ref[k]

    shape = (depth + EXTRA, 4 * width)
    return run(body, (1,), far([*weights, *gains]), [whole(shape, BF)] * 4, [pltpu.VMEM((4, *shape), BF)])


def pack_mlp(weights, ff):
    depth, count = weights[0].shape

    def body(*refs):
        own, out_ref = lax.axis_index("tp"), refs[-1]
        for a in range(4):
            parts = []
            for ref in refs[: len(weights)]:
                last = min(count, (a + 1) * ff)
                parts.append(ref[:, a * ff : last])
                if last < (a + 1) * ff:
                    parts.append(jnp.zeros((depth, (a + 1) * ff - last), F32))
            out_ref[a ^ own] = jnp.concatenate(parts, axis=1).astype(BF)
        for k in range(4):
            refs[len(weights) + k][...] = out_ref[k]

    shape = (depth, len(weights) * ff)
    return run(body, (1,), far(weights), [whole(shape, BF)] * 4, [pltpu.VMEM((4, *shape), BF)])


def pack_plain(weights, width, extra):
    own = lax.axis_index("tp")
    weights = [jnp.pad(w.astype(BF), ((0, 0), (0, 4 * width - w.shape[1]))) for w in weights]
    blocks = []
    for k in range(4):
        block = jnp.concatenate([lax.dynamic_slice_in_dim(w, (own ^ k) * width, width, 1) for w in weights], axis=1)
        blocks.append(block if extra is None else jnp.concatenate([block, extra], axis=0))
    return blocks


def spread_gains(chunks, chunk):
    count = len(chunks)
    ring = ring_ok(count)

    def body(*refs):
        one_ref, two_ref, rows_ref = refs[-3:]
        places = ring_places(count) if ring else None
        for ref, k in zip(refs, chunk_order(count) if ring else range(count)):
            rows_ref[places[k] if ring else k] = ref[chunk : chunk + 2, :chunk].astype(F32)
        both = jnp.concatenate([rows_ref[r] for r in range(count)], axis=1)
        one_ref[...], two_ref[...] = both[0:1], both[1:2]

    return near(body, chunks, [((1, count * chunk), F32)] * 2, [pltpu.VMEM((count, 2, chunk), F32)])


def tiles(total, tile, work):
    lax.fori_loop(0, total // tile, lambda i, _: work(pl.multiple_of(i * tile, tile)), None)


def rsq_of(value):
    return lax.rsqrt(jnp.mean(value * value, axis=1, keepdims=True) + EPSILON)


def project(inputs, gain, weights, width):
    tokens, model = inputs.shape
    tile = tokens // 2

    def body(x_ref, gain_ref, w_ref, normed_ref, rsq_ref, q_ref, k_ref, v_ref):
        for at in range(0, tokens, tile):
            rows = slice(at, at + tile)
            x = x_ref[rows].astype(F32)
            rsq = rsq_of(x)
            normed = (x * rsq * gain_ref[...]).astype(BF)
            normed_ref[rows] = normed
            rsq_ref[rows] = jnp.broadcast_to(rsq, (tile, 128))
            three = dot(normed, w_ref[:, : 3 * width], NN).astype(BF)
            for i, ref in enumerate((q_ref, k_ref, v_ref)):
                ref[rows] = three[:, i * width : (i + 1) * width]

    return near(
        body, [inputs, gain, weights],
        [((tokens, model), BF), ((tokens, 128), F32)] + [((tokens, width), BF)] * 3,
    )


def head_scores(own, row, head, dim, rows, length, q_ref, k_ref, w_ref, qd_ref, kd_ref):
    lanes = slice(head * dim, (head + 1) * dim)
    starts = [pl.multiple_of((block_of(own ^ a) * rows + row) * length, length) for a in range(4)]
    queries = jnp.concatenate([q_ref[pl.ds(s, length), lanes] for s in starts], axis=0)
    keys = take_keys(k_ref, starts, length, lanes)
    q_len, k_len = queries.shape[0], keys.shape[0]
    scores = dot(queries, keys, NT)
    bias = jnp.broadcast_to(w_ref[pl.ds(head, 1), :], (q_len, q_len + k_len))
    bias = pltpu.roll(bias, k_len, 1, stride=1, stride_axis=0)[:, :k_len]
    same = qd_ref[row] == kd_ref[row]
    expo = jnp.where(same, jnp.exp(scores + bias), 0.0)
    return queries, keys, expo, starts, lanes


def take_keys(ref, starts, length, lanes):
    return jnp.concatenate(
        [ref[g, pl.ds(s, length), lanes] for g in range(ref.shape[0]) for s in starts], axis=0
    )


def attn_forward(q, k, v, by_distance, query_doc, key_doc, attn_w, heads, dim, rows, length):
    tokens, width = q.shape
    model = attn_w.shape[0]
    half = tokens // 2

    def body(q_ref, k_ref, v_ref, w_ref, qd_ref, kd_ref, o_ref, attn_ref, keep_ref, give_ref, part_ref):
        def one_row(row):
            forward_row(row, q_ref, k_ref, v_ref, w_ref, qd_ref, kd_ref, o_ref, attn_ref, part_ref)

        lax.fori_loop(0, rows, lambda row, _: one_row(row), None)
        keep_ref[...] = part_ref[:half]
        give_ref[...] = part_ref[half:].astype(BF)

    def forward_row(row, q_ref, k_ref, v_ref, w_ref, qd_ref, kd_ref, o_ref, attn_ref, part_ref):
        own, out = lax.axis_index("tp"), []
        for head in range(heads):
            _, _, expo, starts, lanes = head_scores(
                own, row, head, dim, rows, length, q_ref, k_ref, w_ref, qd_ref, kd_ref
            )
            values = take_keys(v_ref, starts, length, lanes)
            low = expo.astype(BF)
            totals = jnp.sum(low.astype(F32), axis=1, keepdims=True)
            out.append(dot(low, values, NN) / totals)
        out = jnp.concatenate(out, axis=1)
        part = dot(out.astype(BF), o_ref[:, 3 * width :], NT)
        for a, s in enumerate(starts):
            attn_ref[pl.ds(s, length), :] = out[a * length : (a + 1) * length]
            part_ref[pl.ds(s, length), :] = part[a * length : (a + 1) * length]

    return near(
        body, [q, k, v, by_distance, query_doc, key_doc, attn_w],
        [((tokens, width), F32), ((half, model), F32), ((half, model), BF)],
        [pltpu.VMEM((tokens, model), F32)],
    )


def attn_backward(q, k, v, by_distance, query_doc, key_doc, attn, grad, one_hot, heads, dim, rows, length, columns):
    buckets = one_hot.shape[1]

    def body(
        q_ref, k_ref, v_ref, w_ref, qd_ref, kd_ref, attn_ref, grad_ref, hot_ref,
        gq_ref, gk_ref, gv_ref, table_ref, diag_ref,
    ):
        diag_ref[...] = jnp.zeros(diag_ref.shape, F32)

        def one_row(row):
            backward_row(
                row, q_ref, k_ref, v_ref, w_ref, qd_ref, kd_ref, attn_ref, grad_ref, gq_ref, gk_ref, gv_ref, diag_ref
            )

        lax.fori_loop(0, rows, lambda row, _: one_row(row), None)
        table = lax.dot_general(
            diag_ref[...], hot_ref[...], (NN, ((), ())), precision=HIGHEST, preferred_element_type=F32
        )
        table = [table[h : h + 1] for h in range(heads)]
        table_ref[...] = jnp.concatenate(table + [jnp.zeros((1, columns - heads * buckets), F32)], axis=1)

    def backward_row(
        row, q_ref, k_ref, v_ref, w_ref, qd_ref, kd_ref, attn_ref, grad_ref, gq_ref, gk_ref, gv_ref, diag_ref
    ):
        own = lax.axis_index("tp")
        grads_q, grads_k, grads_v, diags = [], [], [], []
        for head in range(heads):
            queries, keys, expo, starts, lanes = head_scores(
                own, row, head, dim, rows, length, q_ref, k_ref, w_ref, qd_ref, kd_ref
            )
            values = take_keys(v_ref, starts, length, lanes)
            grads = jnp.concatenate([grad_ref[pl.ds(s, length), lanes] for s in starts], axis=0)
            outs = jnp.concatenate([attn_ref[pl.ds(s, length), lanes] for s in starts], axis=0)
            low = expo.astype(BF)
            totals = jnp.sum(low.astype(F32), axis=1, keepdims=True)
            grad_low = (grads / totals).astype(BF)
            grad_total = -jnp.sum(grads * outs, axis=1, keepdims=True) / totals
            grad_score = (expo * (dot(grad_low, values, NT) + grad_total)).astype(BF)
            grads_q.append(dot(grad_score, keys, NN))
            grads_k.append(dot(grad_score, queries, TN))
            grads_v.append(dot(low, grad_low, TN))
            q_len, k_len = grad_score.shape
            row_at = lax.broadcasted_iota(jnp.int32, (q_len, q_len), 0)
            column_at = lax.broadcasted_iota(jnp.int32, (q_len, q_len), 1)
            flip = jnp.where(row_at + column_at == q_len - 1, 1.0, 0.0).astype(BF)
            turned = dot(flip, grad_score, NN)
            turned = jnp.concatenate([turned, jnp.zeros((q_len, q_len), F32)], axis=1)
            turned = pltpu.roll(turned, 1, 1, stride=1, stride_axis=0)
            diags.append(jnp.sum(turned, axis=0, keepdims=True))
        joined = jnp.concatenate(grads_q, axis=1).astype(BF)
        for a, s in enumerate(starts):
            gq_ref[pl.ds(s, length), :] = joined[a * length : (a + 1) * length]
        for parts, ref in ((grads_k, gk_ref), (grads_v, gv_ref)):
            joined = jnp.concatenate(parts, axis=1).astype(BF)
            for g in range(ref.shape[0]):
                for a, s in enumerate(starts):
                    at = (g * 4 + a) * length
                    ref[g, pl.ds(s, length), :] = joined[at : at + length]
        diag_ref[...] += jnp.concatenate(diags, axis=0)

    return near(
        body, [q, k, v, by_distance, query_doc, key_doc, attn, grad, one_hot],
        [(q.shape, BF), (k.shape, BF), (v.shape, BF), ((1, columns), F32)],
        [pltpu.VMEM(by_distance.shape, F32)],
    )


def in_halves(low, others, tile):
    places = []
    for ref in (low, *others):
        places += [(ref, at) for at in range(0, ref.shape[0], tile)]
    return lambda i: places[i][0][places[i][1] : places[i][1] + tile].astype(F32)


def norm_again(inputs, low, others, gain):
    tokens, model = inputs.shape
    tile = tokens // 4

    def body(x_ref, gain_ref, low_ref, *refs):
        middle_ref, normed_ref = refs[-2:]
        read = in_halves(low_ref, refs[:-2], tile)
        for i in range(tokens // tile):
            rows = slice(i * tile, (i + 1) * tile)
            middle = x_ref[rows].astype(F32) + read(i)
            middle_ref[rows] = middle
            normed_ref[rows] = (middle * rsq_of(middle) * gain_ref[...]).astype(BF)

    return near(body, [inputs, gain, low, *others], [((tokens, model), F32), ((tokens, model), BF)])


def norm_back(middle, cot, low, others, gain, attn_w, width):
    tokens, model = middle.shape
    tile = tokens // 4

    def body(m_ref, cot_ref, gain_ref, w_ref, low_ref, *refs):
        mid_ref, branch_ref, gain_out_ref, attn_ref = refs[-4:]
        read = in_halves(low_ref, refs[:-4], tile)
        gain_sum = jnp.zeros((1, model), F32)
        for i in range(tokens // tile):
            rows = slice(i * tile, (i + 1) * tile)
            grad = read(i)
            middle = m_ref[rows]
            rsq = rsq_of(middle)
            unit = middle * rsq
            scaled = grad * gain_ref[...]
            back = cot_ref[rows].astype(F32) + rsq * (scaled - unit * jnp.mean(scaled * unit, axis=1, keepdims=True))
            mid_ref[rows] = back
            branch_ref[rows] = back.astype(BF)
            gain_sum += jnp.sum(grad * unit, axis=0, keepdims=True)
        gain_out_ref[...] = gain_sum
        attn_ref[...] = dot(branch_ref[...], w_ref[:, 3 * width :], NN)

    return near(
        body, [middle, cot, gain, attn_w, low, *others],
        [((tokens, model), F32), ((tokens, model), BF), ((1, model), F32), ((tokens, width), F32)],
    )


def gated(normed, gate_b, up_b):
    tokens, ff = normed.shape[0], gate_b.shape[1]
    tile = 256
    scale = math.sqrt(2.0 / math.pi)

    def body(x_ref, gate_ref, up_ref, hidden_ref, slopes_ref):
        def work(at):
            columns = pl.ds(at, tile)
            gate, up = dot(x_ref[...], gate_ref[:, columns], NN), dot(x_ref[...], up_ref[:, columns], NN)
            square = gate * gate
            tanh = jnp.tanh(scale * gate * (1.0 + 0.044715 * square))
            curve = 0.5 * (1.0 + tanh)
            slope = curve + 0.5 * gate * (1.0 - tanh * tanh) * (scale * (1.0 + 3 * 0.044715 * square))
            activated = gate * curve
            hidden_ref[:, columns] = (activated * up).astype(BF)
            slopes_ref[:, columns] = up * slope
            slopes_ref[:, pl.ds(pl.multiple_of(ff + at, tile), tile)] = activated

        tiles(ff, tile, work)

    return near(body, [normed, gate_b, up_b], [((tokens, ff), BF), ((tokens, 2 * ff), F32)])


def gated_back(cot, down_b, slopes):
    tokens, ff = cot.shape[0], down_b.shape[1]
    tile = 256

    def body(cot_ref, down_ref, slopes_ref, pair_ref):
        def work(at):
            grad = dot(cot_ref[...], down_ref[:, pl.ds(at, tile)], NN)
            for columns in (pl.ds(at, tile), pl.ds(pl.multiple_of(ff + at, tile), tile)):
                pair_ref[:, columns] = (grad * slopes_ref[:, columns]).astype(BF)

        tiles(ff, tile, work)

    return near(body, [cot, down_b, slopes], [((tokens, 2 * ff), BF)])[0]


def weight_grad(left, right, count, first=0, last=None):
    model = left.shape[1]
    last = last or right.shape[1]
    tile, chunk = 384, model // count

    def body(left_ref, right_ref, out_ref):
        def work(at):
            part = dot(left_ref[:, pl.ds(at, tile)], right_ref[:, first:last], TN).astype(BF)
            for c in range(tile // chunk):
                out_ref[at // chunk + c] = part[c * chunk : (c + 1) * chunk]

        tiles(model, tile, work)

    return near(body, [left, right], [((count, chunk, last - first), BF)])[0]


def back_through(left, rights):
    tokens, model = left.shape[0], rights[0].shape[0]
    half, tile = tokens // 2, 384

    def body(left_ref, *refs):
        keep_ref, give_ref = refs[-2:]

        def work(at):
            columns = pl.ds(at, tile)
            total, first = None, 0
            for ref in refs[:-2]:
                last = first + ref.shape[1]
                term = dot(left_ref[:, first:last], ref[columns, :], NT)
                total, first = term if total is None else total + term, last
            keep_ref[:, columns] = total[:half]
            give_ref[:, columns] = total[half:].astype(BF)

        tiles(model, tile, work)

    return near(body, [left, *rights], [((half, model), F32), ((half, model), BF)])


def attn_weight_grads(normed, inputs, rsq, branch, attn, grads, attn_w, second_part, table, chunk):
    tokens, model = normed.shape
    width = attn.shape[1]
    half, tile = tokens // 2, 384
    each = tile // chunk

    def body(n_ref, x_ref, rsq_ref, b_ref, attn_ref, q_ref, k_ref, v_ref, w_ref, second_ref, table_ref, out_ref, keep_ref, give_ref):
        three = jnp.concatenate([q_ref[...], k_ref[...], v_ref[...]], axis=1)
        attended = attn_ref[...].astype(BF)
        fill = jnp.zeros((1, 4 * width - chunk), F32)

        def work(at):
            columns = pl.ds(at, tile)
            back = dot(three, w_ref[columns, : 3 * width], NT)
            keep_ref[:, columns] = back[:half]
            give_ref[:, columns] = back[half:].astype(BF)
            first = jnp.sum(back * x_ref[:, columns].astype(F32) * rsq_ref[:, 0:1], axis=0, keepdims=True)
            second = second_ref[:, columns]
            wide = dot(n_ref[:, columns], three, TN).astype(BF)
            last = dot(b_ref[:, columns], attended, TN).astype(BF)
            for c in range(each):
                rows, block = slice(c * chunk, (c + 1) * chunk), at // chunk + c
                out_ref[block, :chunk] = jnp.concatenate([wide[rows], last[rows]], axis=1)
                small = [jnp.concatenate([row[:, rows], fill], axis=1) for row in (first, second)]
                small += [table_ref[...], jnp.zeros((EXTRA - 3, 4 * width), F32)]
                out_ref[block, chunk:] = jnp.concatenate(small, axis=0).astype(BF)

        tiles(model, tile, work)

    return near(
        body, [normed, inputs, rsq, branch, attn, *grads, attn_w, second_part, table],
        [((model // chunk, chunk + EXTRA, 4 * width), BF), ((half, model), F32), ((half, model), BF)],
    )


def finish_input(addends, inputs, gain, grad_middle):
    count, model = addends[0].shape

    def body(low_ref, got_ref, x_ref, gain_ref, mid_ref, out_ref):
        x = x_ref[:count].astype(F32)
        rsq = rsq_of(x)
        unit = x * rsq
        scaled = (low_ref[...].astype(F32) + got_ref[...].astype(F32)) * gain_ref[...]
        out_ref[...] = mid_ref[:count] + rsq * (scaled - unit * jnp.mean(scaled * unit, axis=1, keepdims=True))

    return near(body, [*addends, inputs, gain, grad_middle], [((count, model), F32)])[0]


def finish_output(addends, middle):
    count, model = addends[0].shape

    def body(low_ref, got_ref, mid_ref, out_ref):
        out_ref[...] = (mid_ref[:count] + low_ref[...].astype(F32) + got_ref[...].astype(F32)).astype(BF)

    return near(body, [*addends, middle], [((count, model), BF)])[0]


def rows_of(values, depth):
    if depth % 16:
        own, value = lax.axis_index("tp"), jnp.concatenate(values, axis=1)
        return [lax.dynamic_slice_in_dim(value, (own ^ k) * depth, depth, 0) for k in range(4)]

    def body(*refs):
        own = lax.axis_index("tp")
        for k in range(4):
            at = 0
            for ref in refs[: len(values)]:
                rows = ref[pl.ds(pl.multiple_of((own ^ k) * depth, depth), depth), :]
                refs[len(values) + k][:, at : at + ref.shape[1]] = rows
                at += ref.shape[1]

    return near(body, values, [((depth, sum(v.shape[1] for v in values)), BF)] * 4)


def unpack_mlp(pieces, count, ff):
    depth, width = pieces[0].shape

    def body(*refs):
        own, outs, held = lax.axis_index("tp"), refs[4:-1], refs[-1]
        for k in range(4):
            held[own ^ k] = refs[k][...]
        for i, out in enumerate(outs):
            for a in range(4):
                last = min(count, (a + 1) * ff)
                out[:, a * ff : last] = held[a, :, i * ff : i * ff + last - a * ff].astype(F32)

    return near(body, pieces, [((depth, count), F32)] * (width // ff), [pltpu.VMEM((4, depth, width), BF)])


def unpack_attn(pieces, depth, width, heads, buckets):
    rows = pieces[0].shape[0]

    def body(*refs):
        own, grads, first_ref, second_ref, table_ref, held = lax.axis_index("tp"), refs[4:8], *refs[8:]
        for k in range(4):
            held[own ^ k] = refs[k][...].astype(F32)
        for i, out in enumerate(grads):
            for a in range(4):
                out[:, a * width : (a + 1) * width] = held[a, :depth, i * width : (i + 1) * width]
        small = [held[a, depth : depth + EXTRA] for a in range(4)]
        first_ref[...] = sum(p[0:1, :depth] for p in small)
        second_ref[...] = small[0][1:2, :depth]
        for a in range(4):
            for h in range(heads):
                table_ref[a * heads + h : a * heads + h + 1] = small[a][2:3, h * buckets : (h + 1) * buckets]

    outs = [((depth, 4 * width), F32)] * 4 + [((1, depth), F32)] * 2 + [((4 * heads, buckets), F32)]
    return near(body, pieces, outs, [pltpu.VMEM((4, rows, 4 * width), F32)])


ORDER = (
    "Pa", "I0", "Pm", "a1", "a2", "C0", "M0", "g1", "a3", "u1", "g2", "I1s0", "d1", "a4", "d2", "a5", "C1s0",
    "I1s1", "I1e", "QK", "u2", "R0s0", "g3", "R0s1", "u3", "R0e", "d3", "g4", "u4", "R2s0", "d4", "R2s1", "R2e",
    "u5", "g5", "C1s1", "C1e", "d5", "ML", "rd1", "MB", "B0s0", "rd2", "O0s0", "rg1", "WU", "ru1", "B0e", "O0e",
    "rd3", "ru2", "rg2", "rd4", "B2s0", "rg3", "B2e", "AB", "ru3", "WA", "rd5", "N0s0", "ra1", "rg4", "O2", "ra2",
    "N0e", "rg5", "Xd0", "Xd1", "Xd2", "ra3", "Xd3", "ru4", "ra4", "ru5", "Xu0", "Xu1", "Xu2", "N2", "ra5", "Xa0",
    "Xa1", "Xa2", "Xu3", "Xa3",
)


def shards(
    block_input, cotangent, query_w, key_w, value_w, output_w, gate_w, up_w, down_w,
    first_gain, second_gain, bias_table, rel_bucket, doc_ids,
):
    rows, length, model = block_input.shape
    tokens = rows * length
    own = lax.axis_index("tp")
    parts = lax.axis_size("seq")
    count = lax.axis_size("rows") * parts
    bucket_count, head_count = bias_table.shape
    inner = query_w.shape[1]
    heads = head_count // 4
    dim = inner // head_count
    width = heads * dim
    depth = query_w.shape[0]
    chunk = 4 * depth
    hidden_count = gate_w.shape[1]
    ff = -(-hidden_count // (4 * 256)) * 256
    seq_len = doc_ids.shape[1]
    q_len = 4 * length
    shape = (heads, dim, rows, length)
    lanes = Lanes(count, 4)
    steps, tasks, have = {}, {}, {}

    def do(name):
        def keep(work):
            steps[name] = work
        return keep

    def task(key, names, make):
        def start():
            tasks[key] = Task(make())
            tasks[key].step()

        def end():
            have[key] = tasks[key].result()

        steps.update({name: lambda: tasks[key].step() for name in names})
        steps[names[0]], steps[names[-1]] = start, end

    def core(name, side=0):
        return [f"{name}s{n}" for n in range(CUTS[side])] + [f"{name}e"]

    def attn_blocks():
        weights = [query_w, key_w, value_w, output_w.T]
        gains = [first_gain.reshape(1, depth), second_gain.reshape(1, depth)]
        if depth % 16 == 0:
            return pack_attn(weights, gains, width)
        gains = jnp.pad(jnp.concatenate(gains, axis=0).astype(BF), ((0, EXTRA - 2), (0, 4 * width - depth)))
        return pack_plain(weights, width, gains)

    def mlp_blocks():
        weights = [down_w.T, gate_w, up_w]
        return pack_mlp(weights, ff) if depth % 16 == 0 else pack_plain(weights, ff, None)

    def attn_chunk():
        return gather_ring(lanes, stack_attn(tasks["Pa"].result(), chunk), chunk, 1)

    task("Pa", ["Pa", "Pa-"], lambda: exchange(lanes, attn_blocks()))
    task("Pm", ["Pm", "M0"], lambda: exchange(lanes, mlp_blocks()))
    task("a", ["a1", "a2", "a3", "a4", "a5"], attn_chunk)

    def mlp_chunk(i):
        if "chunks" not in have:
            have["chunks"] = stack_members(have["Pm"], [ff] * 3, PADS if ring_ok(count) else (0, 0, 0))
        return have["chunks"][i]

    task("d", ["d1", "d2", "d3", "d4", "d5"], lambda: gather_ring(lanes, mlp_chunk(0), chunk, -1))
    task("g", ["g1", "g2", "g3", "g4", "g5"], lambda: gather_ring(lanes, mlp_chunk(1), chunk, 1))
    task("u", ["u1", "u2", "u3", "u4", "u5"], lambda: gather_ring(lanes, mlp_chunk(2), chunk, -1))

    task("in", ["I0", *core("I1")], lambda: gather_tokens(lanes, block_input.reshape(tokens, model), CUTS[0]))
    task("cot", ["C0", *core("C1")], lambda: gather_tokens(lanes, cotangent.reshape(tokens, model), CUTS[0]))

    @do("QK")
    def _():
        one_hot = (rel_bucket[:, None] == jnp.arange(bucket_count, dtype=jnp.int32)).astype(F32)
        first = lax.axis_index("seq") * q_len
        one_hot = lax.dynamic_slice_in_dim(one_hot, seq_len - first - q_len, seq_len + q_len, 0)
        own_table = lax.dynamic_slice_in_dim(bias_table, own * heads, heads, 1)
        by_distance = lax.dot_general(own_table, one_hot, (((0,), (1,)), ((), ())), precision=HIGHEST)
        query_doc = lax.dynamic_slice_in_dim(doc_ids, first, q_len, 1)[:, :, None]
        attn_w, chunks = have["a"]
        gain_one, gain_two = spread_gains(chunks, chunk)
        normed, rsq_one, queries, keys, values = project(have["in"], gain_one, attn_w, width)
        queries = lanes.pin(queries)
        if parts > 1:
            keys = lax.all_gather(keys, "seq", axis=0)
            values = lax.all_gather(values, "seq", axis=0)
        else:
            keys, values = keys[None], values[None]
        have.update(
            one_hot=one_hot, attn_w=attn_w, gain_one=gain_one, gain_two=gain_two, normed=normed, rsq_one=rsq_one,
            scores=(queries, keys, values, by_distance, query_doc, doc_ids[:, None, :]),
        )

    def attention():
        have["attn"], keep, give = attn_forward(*have["scores"], have["attn_w"], *shape)
        return sum_tokens(lanes, keep, give, CUTS[0])

    task("branch", [*core("R0"), *core("R2")], attention)

    @do("ML")
    def _():
        middle, normed_mlp = norm_again(have["in"], *have["branch"], have["gain_two"])
        hidden, slopes = gated(normed_mlp, have["g"][0], have["u"][0])
        have.update(middle=middle, normed_mlp=normed_mlp, hidden=lanes.pin(hidden), slopes=slopes)

    @do("MB")
    def _():
        have["grad_pair"] = lanes.pin(gated_back(have["cot"], have["d"][0], have["slopes"]))

    task(
        "rd", ["rd1", "rd2", "rd3", "rd4", "rd5"],
        lambda: scatter_ring(lanes, weight_grad(have["cot"], have["hidden"], count), 1, chunk + RPADS[0]),
    )
    task(
        "back", [*core("B0", 1), *core("B2", 1)],
        lambda: sum_tokens(lanes, *back_through(have["grad_pair"], [have["g"][0], have["u"][0]]), CUTS[1]),
    )
    if "rm1" in ORDER:
        task(
            "rm", ["rm1", "rm2", "rm3", "rm4", "rm5"],
            lambda: scatter_ring(lanes, weight_grad(have["normed_mlp"], have["grad_pair"], count), -1, chunk + RPADS[1]),
        )
    else:
        @do("WU")
        def _():
            have["up_blocks"] = lanes.pin(weight_grad(have["normed_mlp"], have["grad_pair"], count, ff, 2 * ff))

        task(
            "rg", ["rg1", "rg2", "rg3", "rg4", "rg5"],
            lambda: scatter_ring(
                lanes, weight_grad(have["normed_mlp"], have["grad_pair"], count, 0, ff), -1, chunk + RPADS[1]
            ),
        )
        task("ru", ["ru1", "ru2", "ru3", "ru4", "ru5"], lambda: scatter_ring(lanes, have["up_blocks"], 1, chunk + RPADS[2]))
    task("out", [*core("O0", 1), "O2"], lambda: scatter_tokens(lanes, *back_through(have["hidden"], [have["d"][0]]), CUTS[1]))

    @do("AB")
    def _():
        grad_middle, grad_branch, second_part, grad_attn = norm_back(
            have["middle"], have["cot"], *have["back"], have["gain_two"], have["attn_w"], width
        )
        grad_q, grad_k, grad_v, table = attn_backward(
            *have["scores"], have["attn"], lanes.pin(grad_attn), have["one_hot"], *shape, 4 * width
        )
        if parts > 1:
            grad_k = lax.psum_scatter(grad_k, "seq", scatter_dimension=0, tiled=True)
            grad_v = lax.psum_scatter(grad_v, "seq", scatter_dimension=0, tiled=True)
        have.update(
            grad_middle=grad_middle, grad_branch=grad_branch, second_part=second_part, table=table,
            grads=(lanes.pin(grad_q), grad_k[0], grad_v[0]),
        )

    @do("WA")
    def _():
        four_grad, keep, give = attn_weight_grads(
            have["normed"], have["in"], have["rsq_one"], have["grad_branch"], have["attn"], have["grads"],
            have["attn_w"], have["second_part"], have["table"], chunk,
        )
        have.update(four_grad=lanes.pin(four_grad), in_parts=(keep, give))

    task("ra", ["ra1", "ra2", "ra3", "ra4", "ra5"], lambda: scatter_ring(lanes, have["four_grad"], 1, chunk + EXTRA))
    task("grad_in", [*core("N0", 1), "N2"], lambda: scatter_tokens(lanes, *have["in_parts"], CUTS[1]))

    if "rm1" in ORDER:
        one, two = ["rd"], ["rm"]
    else:
        one, two = ["rd", "rg"], ["ru"]
    task("Xd", ["Xd0", "Xd1", "Xd2", "Xd3"], lambda: exchange(lanes, rows_of([have[k] for k in one], depth), False))
    task("Xu", ["Xu0", "Xu1", "Xu2", "Xu3"], lambda: exchange(lanes, rows_of([have[k] for k in two], depth), False))
    task("Xa", ["Xa0", "Xa1", "Xa2", "Xa3"], lambda: exchange(lanes, split_attn(have["ra"], depth, width), False))

    for name in ORDER:
        steps[name]()
    block_output = finish_output(have["out"], have["middle"])
    input_grad = finish_input(have["grad_in"], have["in"], have["gain_one"], have["grad_middle"])

    mlp = unpack_mlp(have["Xd"], hidden_count, ff) + unpack_mlp(have["Xu"], hidden_count, ff)
    *grads, first_grad, second_grad, table_grad = unpack_attn(have["Xa"], depth, width, heads, bucket_count)
    return (
        block_output.reshape(rows, length, model), input_grad.reshape(rows, length, model),
        grads[0], grads[1], grads[2], grads[3].T,
        mlp[1], mlp[2], mlp[0].T, first_grad.reshape(depth), second_grad.reshape(depth), table_grad.T,
    )


def solution(mesh):
    row_count, blk_count = mesh.shape["rows"], mesh.shape["blk"]
    fine = Mesh(mesh.devices.reshape(row_count, blk_count // 4, 4), ("rows", "seq", "tp"))
    every = ("rows", "seq", "tp")
    tokens = P("rows", ("seq", "tp"), None)
    deep, wide, flat = P(every, None), P(None, every), P(every)
    return jax.shard_map(
        shards,
        mesh=fine,
        in_specs=(tokens, tokens, deep, deep, deep, wide, deep, deep, wide, flat, flat, P(), P(), P("rows", None)),
        out_specs=(tokens, tokens, deep, deep, deep, wide, deep, deep, wide, flat, flat, P()),
        check_vma=False,
    )
```

profile of v0, /device:TPU:0, one launch (start us, length us, event | category | flops | bytes accessed | tf_op | source)
XLA Modules:
  0.0 290.8 jit_solution(4872581698095784895)
XLA Ops:
  2.5 2.6 collective-permute-start.6
  8.2 2.3 collective-permute-done.5.refs_2_
  14.8 5.1 %collective-permute-done.8.refs_2_ = bf16[208,768]{1,0:T(8,128)(2,1)S(1)} collective-permute-done((bf16[208,768]{1,0:T(8,128)(2,1)S(1)}, bf16[208,768]{1,0:T(8,128)(2,1)S(1)}, u32[]{:S(2)}, u32[]{:S(2)}) %collective-permute-start.8) | collective-permute-done | bytes 319520 | tf_op jit(solution)/shard_map/ppermute | solution.py:67
  23.1 5.3 %collective-permute-done.2.refs_2_ = bf16[48,3072]{1,0:T(8,128)(2,1)S(1)} collective-permute-done((bf16[48,3072]{1,0:T(8,128)(2,1)S(1)}, bf16[48,3072]{1,0:T(8,128)(2,1)S(1)}, u32[]{:S(2)}, u32[]{:S(2)}) %collective-permute-start.2) | collective-permute-done | bytes 294944 | tf_op jit(solution)/shard_map/ppermute | solution.py:70
  34.9 7.0 %collective-permute-done.10.refs_2_ = bf16[198,1024]{1,0:T(8,128)(2,1)} collective-permute-done((bf16[198,1024]{1,0:T(8,128)(2,1)}, bf16[198,1024]{1,0:T(8,128)(2,1)}, u32[]{:S(2)}, u32[]{:S(2)}) %collective-permute-start.10) | collective-permute-done | bytes 405536 | tf_op jit(solution)/shard_map/ppermute | solution.py:67
  51.7 7.4 %collective-permute-done.19.refs_1_ = bf16[200,1024]{1,0:T(8,128)(2,1)} collective-permute-done((bf16[200,1024]{1,0:T(8,128)(2,1)S(1)}, bf16[200,1024]{1,0:T(8,128)(2,1)}, u32[]{:S(2)}, u32[]{:S(2)}) %collective-permute-start.19) | collective-permute-done | bytes 409632 | tf_op jit(solution)/shard_map/ppermute | solution.py:67
  59.1 2.0 collective-permute-start.21
  61.1 4.7 %collective-permute-done.17.refs_7_ = bf16[208,768]{1,0:T(8,128)(2,1)S(1)} collective-permute-done((bf16[208,768]{1,0:T(8,128)(2,1)S(1)}, bf16[208,768]{1,0:T(8,128)(2,1)S(1)}, u32[]{:S(2)}, u32[]{:S(2)}) %collective-permute-start.17) | collective-permute-done | bytes 319520 | tf_op jit(solution)/shard_map/ppermute | solution.py:67
  65.8 2.0 collective-permute-start.25
  71.9 3.6 %shard_map.236 = (f32[512,192]{1,0:T(8,128)S(1)}, f32[256,1536]{1,0:T(8,128)S(1)}, bf16[256,1536]{1,0:T(8,128)(2,1)S(1)}) custom-call(bf16[512,192]{1,0:T(8,128)(2,1)S(1)} %get-tuple-element.306.q_ref, bf16[1,512,192]{2,1,0:T(8,128)(2,1)S(1)} %bitcast.18, bf16[1,512,192]{2,1,0:T(8,128)(2,1)S(1)} %bitcast.20, f32[3,512]{1,0:T(4,128)S(1)} %fusion.1.w_ref, ...), custom_call_target="tpu_custom_call" | custom-call | tf_op jit(solution)/shard_map/pallas_call | solution.py:338
  76.2 2.0 collective-permute-start.27
  78.2 5.2 %collective-permute-done.24.refs_3_ = bf16[198,1024]{1,0:T(8,128)(2,1)S(1)} collective-permute-done((bf16[198,1024]{1,0:T(8,128)(2,1)}, bf16[198,1024]{1,0:T(8,128)(2,1)S(1)}, u32[]{:S(2)}, u32[]{:S(2)}) %collective-permute-start.24) | collective-permute-done | bytes 405536 | tf_op jit(solution)/shard_map/ppermute | solution.py:67
  83.4 2.0 collective-permute-start.34
  85.4 6.7 %collective-permute-done.28.refs_3_ = bf16[196,1024]{1,0:T(8,128)(2,1)S(1)} collective-permute-done((bf16[196,1024]{1,0:T(8,128)(2,1)S(1)}, bf16[196,1024]{1,0:T(8,128)(2,1)S(1)}, u32[]{:S(2)}, u32[]{:S(2)}) %collective-permute-start.28) | collective-permute-done | bytes 401440 | tf_op jit(solution)/shard_map/ppermute | solution.py:67
  95.9 5.0 %collective-permute-done.35.refs_3_ = bf16[200,1024]{1,0:T(8,128)(2,1)S(1)} collective-permute-done((bf16[200,1024]{1,0:T(8,128)(2,1)}, bf16[200,1024]{1,0:T(8,128)(2,1)S(1)}, u32[]{:S(2)}, u32[]{:S(2)}) %collective-permute-start.35) | collective-permute-done | bytes 409632 | tf_op jit(solution)/shard_map/ppermute | solution.py:67
  100.9 2.0 collective-permute-start.30
  103.0 3.3 %collective-permute-done.33.refs_6_ = bf16[198,1024]{1,0:T(8,128)(2,1)S(1)} collective-permute-done((bf16[198,1024]{1,0:T(8,128)(2,1)S(1)}, bf16[198,1024]{1,0:T(8,128)(2,1)S(1)}, u32[]{:S(2)}, u32[]{:S(2)}) %collective-permute-start.33) | collective-permute-done | bytes 405536 | tf_op jit(solution)/shard_map/ppermute | solution.py:67
  106.7 3.0 %collective-permute-done.32.refs_5_ = bf16[198,1024]{1,0:T(8,128)(2,1)S(1)} collective-permute-done((bf16[198,1024]{1,0:T(8,128)(2,1)S(1)}, bf16[198,1024]{1,0:T(8,128)(2,1)S(1)}, u32[]{:S(2)}, u32[]{:S(2)}) %collective-permute-start.32) | collective-permute-done | bytes 405536 | tf_op jit(solution)/shard_map/ppermute | solution.py:67
  111.3 7.2 %collective-permute-done.31.refs_5_ = bf16[196,1024]{1,0:T(8,128)(2,1)S(1)} collective-permute-done((bf16[196,1024]{1,0:T(8,128)(2,1)S(1)}, bf16[196,1024]{1,0:T(8,128)(2,1)S(1)}, u32[]{:S(2)}, u32[]{:S(2)}) %collective-permute-start.31) | collective-permute-done | bytes 401440 | tf_op jit(solution)/shard_map/ppermute | solution.py:67
  118.9 2.0 collective-permute-start.41
  120.9 6.4 %collective-permute-done.38.refs_5_ = bf16[200,1024]{1,0:T(8,128)(2,1)S(1)} collective-permute-done((bf16[200,1024]{1,0:T(8,128)(2,1)S(1)}, bf16[200,1024]{1,0:T(8,128)(2,1)S(1)}, u32[]{:S(2)}, u32[]{:S(2)}) %collective-permute-start.38) | collective-permute-done | bytes 409632 | tf_op jit(solution)/shard_map/ppermute | solution.py:67
  129.0 2.6 collective-permute-done.41.refs_7_
  131.5 2.8 collective-permute-done.40.refs_7_
  139.6 5.0 %shard_map.242 = (bf16[512,1024]{1,0:T(8,128)(2,1)S(1)}, f32[512,2048]{1,0:T(8,128)S(1)}) custom-call(bf16[512,1536]{1,0:T(8,128)(2,1)S(1)} %get-tuple-element.335.x_ref.left_ref, bf16[1536,1024]{1,0:T(8,128)(2,1)S(1)} %shard_map.240.gate_ref.refs_0_, bf16[1536,1024]{1,0:T(8,128)(2,1)S(1)} %shard_map.241.up_ref.refs_1_), custom_call_target="tpu_custom_call" | custom-call | tf_op jit(solution)/shard_map/pallas_call | solution.py:338
  144.7 2.6 collective-permute-done.42.refs_7_
  147.3 2.4 shard_map.245.blocks_ref
  151.9 2.5 shard_map.247.left_ref.right_ref
  154.4 5.1 %shard_map.248 = (f32[256,1536]{1,0:T(8,128)S(1)}, bf16[256,1536]{1,0:T(8,128)(2,1)S(1)}) custom-call(bf16[512,2048]{1,0:T(8,128)(2,1)S(1)} %shard_map.247.left_ref.right_ref, bf16[1536,1024]{1,0:T(8,128)(2,1)S(1)} %shard_map.240.gate_ref.refs_0_, bf16[1536,1024]{1,0:T(8,128)(2,1)S(1)} %shard_map.241.up_ref.refs_1_), custom_call_target="tpu_custom_call" | custom-call | tf_op jit(solution)/shard_map/pallas_call | solution.py:338
  159.6 2.9 %shard_map.244 = (f32[256,1536]{1,0:T(8,128)S(1)}, bf16[256,1536]{1,0:T(8,128)(2,1)S(1)}) custom-call(bf16[512,1024]{1,0:T(8,128)(2,1)S(1)} %get-tuple-element.345.left_ref.right_ref, bf16[1536,1024]{1,0:T(8,128)(2,1)S(1)} %shard_map.243.refs_0_.down_ref), custom_call_target="tpu_custom_call" | custom-call | tf_op jit(solution)/shard_map/pallas_call | solution.py:338
  165.2 2.4 shard_map.251.blocks_ref
  167.7 2.4 shard_map.250.blocks_ref
  174.6 2.5 collective-permute-done.51.refs_0_
  179.4 6.5 %collective-permute-done.50.refs_0_ = bf16[200,1024]{1,0:T(8,128)(2,1)S(1)} collective-permute-done((bf16[200,1024]{1,0:T(8,128)(2,1)S(1)}, bf16[200,1024]{1,0:T(8,128)(2,1)S(1)}, u32[]{:S(2)}, u32[]{:S(2)}) %collective-permute-start.50) | collective-permute-done | bytes 409632 | tf_op jit(solution)/shard_map/ppermute | solution.py:67
  188.3 6.5 %collective-permute-done.57.refs_1_ = bf16[200,1024]{1,0:T(8,128)(2,1)S(1)} collective-permute-done((bf16[200,1024]{1,0:T(8,128)(2,1)S(1)}, bf16[200,1024]{1,0:T(8,128)(2,1)S(1)}, u32[]{:S(2)}, u32[]{:S(2)}) %collective-permute-start.57) | collective-permute-done | bytes 409632 | tf_op jit(solution)/shard_map/ppermute | solution.py:67
  197.3 6.2 %collective-permute-done.54.refs_1_ = bf16[196,1024]{1,0:T(8,128)(2,1)S(1)} collective-permute-done((bf16[196,1024]{1,0:T(8,128)(2,1)S(1)}, bf16[196,1024]{1,0:T(8,128)(2,1)S(1)}, u32[]{:S(2)}, u32[]{:S(2)}) %collective-permute-start.54) | collective-permute-done | bytes 401440 | tf_op jit(solution)/shard_map/ppermute | solution.py:67
  207.6 2.1 shard_map.262
  209.6 5.8 %shard_map.263 = (bf16[512,192]{1,0:T(8,128)(2,1)S(1)}, bf16[1,512,192]{2,1,0:T(8,128)(2,1)S(1)}, bf16[1,512,192]{2,1,0:T(8,128)(2,1)S(1)}, f32[1,768]{1,0:T(1,128)S(1)}) custom-call(bf16[512,192]{1,0:T(8,128)(2,1)S(1)} %get-tuple-element.306.q_ref, bf16[1,512,192]{2,1,0:T(8,128)(2,1)S(1)} %bitcast.19, bf16[1,512,192]{2,1,0:T(8,128)(2,1)S(1)} %bitcast.21, ...), custom_call_target="tpu_custom_call" | custom-call | tf_op jit(solution)/shard_map/pallas_call | solution.py:338
  216.3 4.4 %shard_map.264 = (bf16[8,208,768]{2,1,0:T(8,128)(2,1)S(1)}, f32[256,1536]{1,0:T(8,128)S(1)}, bf16[256,1536]{1,0:T(8,128)(2,1)S(1)}) custom-call(bf16[512,1536]{1,0:T(8,128)(2,1)S(1)} %get-tuple-element.397.n_ref, bf16[512,1536]{1,0:T(8,128)(2,1)S(1)} %constant_dynamic-update-slice_fusion.x_ref, f32[512,128]{1,0:T(8,128)S(1)} %get-tuple-element.398.rsq_ref, ...), custom_call_target="tpu_custom_call" | custom-call | tf_op jit(solution)/shard_map/pallas_call | solution.py:338
  223.4 4.4 %collective-permute-done.59.refs_1_ = bf16[196,1024]{1,0:T(8,128)(2,1)S(1)} collective-permute-done((bf16[196,1024]{1,0:T(8,128)(2,1)S(1)}, bf16[196,1024]{1,0:T(8,128)(2,1)S(1)}, u32[]{:S(2)}, u32[]{:S(2)}) %collective-permute-start.59) | collective-permute-done | bytes 401440 | tf_op jit(solution)/shard_map/ppermute | solution.py:67
  232.8 3.9 %collective-permute-done.66.refs_0_ = bf16[208,768]{1,0:T(8,128)(2,1)S(1)} collective-permute-done((bf16[208,768]{1,0:T(8,128)(2,1)S(1)}, bf16[208,768]{1,0:T(8,128)(2,1)S(1)}, u32[]{:S(2)}, u32[]{:S(2)}) %collective-permute-start.66) | collective-permute-done | bytes 319520 | tf_op jit(solution)/shard_map/ppermute | solution.py:67
  238.8 2.3 collective-permute-done.71.refs_1_
  245.7 2.2 collective-permute-done.76.refs_1_
  248.0 4.3 %collective-permute-done.75.refs_0_ = bf16[208,768]{1,0:T(8,128)(2,1)S(1)} collective-permute-done((bf16[208,768]{1,0:T(8,128)(2,1)S(1)}, bf16[208,768]{1,0:T(8,128)(2,1)S(1)}, u32[]{:S(2)}, u32[]{:S(2)}) %collective-permute-start.75) | collective-permute-done | bytes 319520 | tf_op jit(solution)/shard_map/ppermute | solution.py:67
  256.0 3.3 %collective-permute-done.73.refs_2_ = bf16[48,2048]{1,0:T(8,128)(2,1)S(1)} collective-permute-done((bf16[48,2048]{1,0:T(8,128)(2,1)S(1)}, bf16[48,2048]{1,0:T(8,128)(2,1)S(1)}, u32[]{:S(2)}, u32[]{:S(2)}) %collective-permute-start.73) | collective-permute-done | bytes 196640 | tf_op jit(solution)/shard_map/ppermute | solution.py:70
  264.9 2.9 %collective-permute-done.79.refs_0_ = bf16[208,768]{1,0:T(8,128)(2,1)S(1)} collective-permute-done((bf16[208,768]{1,0:T(8,128)(2,1)S(1)}, bf16[208,768]{1,0:T(8,128)(2,1)S(1)}, u32[]{:S(2)}, u32[]{:S(2)}) %collective-permute-start.79) | collective-permute-done | bytes 319520 | tf_op jit(solution)/shard_map/ppermute | solution.py:67
  270.1 2.1 collective-permute-done.78.refs_1_
  272.3 4.4 %collective-permute-done.77.refs_0_ = bf16[200,1024]{1,0:T(8,128)(2,1)S(1)} collective-permute-done((bf16[200,1024]{1,0:T(8,128)(2,1)S(1)}, bf16[200,1024]{1,0:T(8,128)(2,1)S(1)}, u32[]{:S(2)}, u32[]{:S(2)}) %collective-permute-start.77) | collective-permute-done | bytes 409632 | tf_op jit(solution)/shard_map/ppermute | solution.py:67
  279.1 3.2 %collective-permute-done.81.refs_0_ = bf16[208,768]{1,0:T(8,128)(2,1)S(1)} collective-permute-done((bf16[208,768]{1,0:T(8,128)(2,1)S(1)}, bf16[208,768]{1,0:T(8,128)(2,1)S(1)}, u32[]{:S(2)}, u32[]{:S(2)}) %collective-permute-start.81) | collective-permute-done | bytes 319520 | tf_op jit(solution)/shard_map/ppermute | solution.py:67
  (216 shorter events, 104.9 us)
Async XLA Ops:
  14.5 13.9 %collective-permute-start.2 = (bf16[48,3072]{1,0:T(8,128)(2,1)S(1)}, bf16[48,3072]{1,0:T(8,128)(2,1)S(1)}, u32[]{:S(2)}, u32[]{:S(2)}) collective-permute-start(bf16[48,3072]{1,0:T(8,128)(2,1)S(1)} %get-tuple-element.269), channel_id=1, source_target_pairs={{0,2},{1,3},{2,0},{3,1},{4,6},{5,7},{6,4},{7,5},{8,10},{9,11},{10,... | collective-permute-start | bytes 884744 | tf_op jit(solution)/shard_map/ppermute | solution.py:70
  29.2 12.7 %collective-permute-start.10 = (bf16[198,1024]{1,0:T(8,128)(2,1)}, bf16[198,1024]{1,0:T(8,128)(2,1)}, u32[]{:S(2)}, u32[]{:S(2)}) collective-permute-start(bf16[198,1024]{1,0:T(8,128)(2,1)} %get-tuple-element.283.refs_0_), channel_id=1, source_target_pairs={{0,4},{8,0},{16,8},{24,16},{28,24},{20,28},{12,20},{4,12},{1,5},{9... | collective-permute-start | bytes 1216520 | tf_op jit(solution)/shard_map/ppermute | solution.py:67
  30.9 12.7 %collective-permute-start.9 = (bf16[198,1024]{1,0:T(8,128)(2,1)}, bf16[198,1024]{1,0:T(8,128)(2,1)}, u32[]{:S(2)}, u32[]{:S(2)}) collective-permute-start(bf16[198,1024]{1,0:T(8,128)(2,1)} %get-tuple-element.283.refs_0_), channel_id=1, source_target_pairs={{0,8},{8,16},{16,24},{24,28},{28,20},{20,12},{12,4},{4,0},{1,9},{9... | collective-permute-start | bytes 1216520 | tf_op jit(solution)/shard_map/ppermute | solution.py:67
  32.9 14.3 %collective-permute-start.16 = (bf16[208,768]{1,0:T(8,128)(2,1)S(1)}, bf16[208,768]{1,0:T(8,128)(2,1)S(1)}, u32[]{:S(2)}, u32[]{:S(2)}) collective-permute-start(bf16[208,768]{1,0:T(8,128)(2,1)S(1)} %collective-permute-done.12.refs_4_), channel_id=1, source_target_pairs={{0,4},{8,0},{16,8},{24,16},{28,24},{20,28},{12,20},{4,12},{1,5},{9... | collective-permute-start | bytes 958472 | tf_op jit(solution)/shard_map/ppermute | solution.py:67
  34.4 15.8 %collective-permute-start.15 = (bf16[208,768]{1,0:T(8,128)(2,1)S(1)}, bf16[208,768]{1,0:T(8,128)(2,1)S(1)}, u32[]{:S(2)}, u32[]{:S(2)}) collective-permute-start(bf16[208,768]{1,0:T(8,128)(2,1)S(1)} %collective-permute-done.11.refs_3_), channel_id=1, source_target_pairs={{0,8},{8,16},{16,24},{24,28},{28,20},{20,12},{12,4},{4,0},{1,9},{9... | collective-permute-start | bytes 958472 | tf_op jit(solution)/shard_map/ppermute | solution.py:67
  41.9 23.9 %collective-permute-start.14 = (bf16[128,1536]{1,0:T(8,128)(2,1)}, bf16[128,1536]{1,0:T(8,128)(2,1)}, u32[]{:S(2)}, u32[]{:S(2)}) collective-permute-start(bf16[128,1536]{1,0:T(8,128)(2,1)} %bitcast.27), channel_id=1, source_target_pairs={{0,2},{1,3},{2,0},{3,1},{4,6},{5,7},{6,4},{7,5},{8,10},{9,11},{10,... | collective-permute-start | bytes 1179656 | tf_op jit(solution)/shard_map/ppermute | solution.py:70
  43.6 24.3 %collective-permute-start.13 = (bf16[128,1536]{1,0:T(8,128)(2,1)}, bf16[128,1536]{1,0:T(8,128)(2,1)}, u32[]{:S(2)}, u32[]{:S(2)}) collective-permute-start(bf16[128,1536]{1,0:T(8,128)(2,1)} %bitcast), channel_id=1, source_target_pairs={{0,1},{1,0},{2,3},{3,2},{4,5},{5,4},{6,7},{7,6},{8,9},{9,8},{10,11... | collective-permute-start | bytes 1179656 | tf_op jit(solution)/shard_map/ppermute | solution.py:70
  43.6 15.5 %collective-permute-start.19 = (bf16[200,1024]{1,0:T(8,128)(2,1)S(1)}, bf16[200,1024]{1,0:T(8,128)(2,1)}, u32[]{:S(2)}, u32[]{:S(2)}) collective-permute-start(bf16[200,1024]{1,0:T(8,128)(2,1)S(1)} %get-tuple-element.293.refs_0_), channel_id=1, source_target_pairs={{0,8},{8,16},{16,24},{24,28},{28,20},{20,12},{12,4},{4,0},{1,9},{9... | collective-permute-start | bytes 1228808 | tf_op jit(solution)/shard_map/ppermute | solution.py:67
  50.2 15.6 %collective-permute-start.17 = (bf16[208,768]{1,0:T(8,128)(2,1)S(1)}, bf16[208,768]{1,0:T(8,128)(2,1)S(1)}, u32[]{:S(2)}, u32[]{:S(2)}) collective-permute-start(bf16[208,768]{1,0:T(8,128)(2,1)S(1)} %collective-permute-done.15.refs_5_), channel_id=1, source_target_pairs={{0,8},{8,16},{16,24},{24,28},{28,20},{20,12},{12,4},{4,0},{1,9},{9... | collective-permute-start | bytes 958472 | tf_op jit(solution)/shard_map/ppermute | solution.py:67
  59.1 16.5 %collective-permute-start.22 = (bf16[196,1024]{1,0:T(8,128)(2,1)}, bf16[196,1024]{1,0:T(8,128)(2,1)S(1)}, u32[]{:S(2)}, u32[]{:S(2)}) collective-permute-start(bf16[196,1024]{1,0:T(8,128)(2,1)} %copy-done.2), channel_id=1, source_target_pairs={{0,8},{8,16},{16,24},{24,28},{28,20},{20,12},{12,4},{4,0},{1,9},{9... | collective-permute-start | bytes 1204232 | tf_op jit(solution)/shard_map/ppermute | solution.py:67
  59.1 16.5 %collective-permute-start.21 = (bf16[196,1024]{1,0:T(8,128)(2,1)}, bf16[196,1024]{1,0:T(8,128)(2,1)S(1)}, u32[]{:S(2)}, u32[]{:S(2)}) collective-permute-start(bf16[196,1024]{1,0:T(8,128)(2,1)} %copy-done.2), channel_id=1, source_target_pairs={{0,4},{8,0},{16,8},{24,16},{28,24},{20,28},{12,20},{4,12},{1,5},{9... | collective-permute-start | bytes 1204232 | tf_op jit(solution)/shard_map/ppermute | solution.py:67
  65.8 17.6 %collective-permute-start.24 = (bf16[198,1024]{1,0:T(8,128)(2,1)}, bf16[198,1024]{1,0:T(8,128)(2,1)S(1)}, u32[]{:S(2)}, u32[]{:S(2)}) collective-permute-start(bf16[198,1024]{1,0:T(8,128)(2,1)} %collective-permute-done.9.refs_1_), channel_id=1, source_target_pairs={{0,8},{8,16},{16,24},{24,28},{28,20},{20,12},{12,4},{4,0},{1,9},{9... | collective-permute-start | bytes 1216520 | tf_op jit(solution)/shard_map/ppermute | solution.py:67
  76.2 16.0 %collective-permute-start.28 = (bf16[196,1024]{1,0:T(8,128)(2,1)S(1)}, bf16[196,1024]{1,0:T(8,128)(2,1)S(1)}, u32[]{:S(2)}, u32[]{:S(2)}) collective-permute-start(bf16[196,1024]{1,0:T(8,128)(2,1)S(1)} %collective-permute-done.22.refs_1_), channel_id=1, source_target_pairs={{0,8},{8,16},{16,24},{24,28},{28,20},{20,12},{12,4},{4,0},{1,9},{9... | collective-permute-start | bytes 1204232 | tf_op jit(solution)/shard_map/ppermute | solution.py:67
  76.2 16.0 %collective-permute-start.27 = (bf16[196,1024]{1,0:T(8,128)(2,1)S(1)}, bf16[196,1024]{1,0:T(8,128)(2,1)S(1)}, u32[]{:S(2)}, u32[]{:S(2)}) collective-permute-start(bf16[196,1024]{1,0:T(8,128)(2,1)S(1)} %collective-permute-done.21.refs_2_), channel_id=1, source_target_pairs={{0,4},{8,0},{16,8},{24,16},{28,24},{20,28},{12,20},{4,12},{1,5},{9... | collective-permute-start | bytes 1204232 | tf_op jit(solution)/shard_map/ppermute | solution.py:67
  83.4 17.5 %collective-permute-start.35 = (bf16[200,1024]{1,0:T(8,128)(2,1)}, bf16[200,1024]{1,0:T(8,128)(2,1)S(1)}, u32[]{:S(2)}, u32[]{:S(2)}) collective-permute-start(bf16[200,1024]{1,0:T(8,128)(2,1)} %collective-permute-done.19.refs_1_), channel_id=1, source_target_pairs={{0,8},{8,16},{16,24},{24,28},{28,20},{20,12},{12,4},{4,0},{1,9},{9... | collective-permute-start | bytes 1228808 | tf_op jit(solution)/shard_map/ppermute | solution.py:67
  83.4 17.5 %collective-permute-start.34 = (bf16[200,1024]{1,0:T(8,128)(2,1)}, bf16[200,1024]{1,0:T(8,128)(2,1)S(1)}, u32[]{:S(2)}, u32[]{:S(2)}) collective-permute-start(bf16[200,1024]{1,0:T(8,128)(2,1)} %collective-permute-done.18.refs_2_), channel_id=1, source_target_pairs={{0,4},{8,0},{16,8},{24,16},{28,24},{20,28},{12,20},{4,12},{1,5},{9... | collective-permute-start | bytes 1228808 | tf_op jit(solution)/shard_map/ppermute | solution.py:67
  92.3 26.2 %collective-permute-start.29 = (bf16[256,1536]{1,0:T(8,128)(2,1)S(1)}, bf16[256,1536]{1,0:T(8,128)(2,1)S(1)}, u32[]{:S(2)}, u32[]{:S(2)}) collective-permute-start(bf16[256,1536]{1,0:T(8,128)(2,1)S(1)} %shard_map.237.left_ref), channel_id=1, source_target_pairs={{0,2},{1,3},{2,0},{3,1},{4,6},{5,7},{6,4},{7,5},{8,10},{9,11},{10,... | collective-permute-start | bytes 2359304 | tf_op jit(solution)/shard_map/ppermute | solution.py:70
  93.9 12.4 %collective-permute-start.33 = (bf16[198,1024]{1,0:T(8,128)(2,1)S(1)}, bf16[198,1024]{1,0:T(8,128)(2,1)S(1)}, u32[]{:S(2)}, u32[]{:S(2)}) collective-permute-start(bf16[198,1024]{1,0:T(8,128)(2,1)S(1)} %collective-permute-done.25.refs_4_), channel_id=1, source_target_pairs={{0,4},{8,0},{16,8},{24,16},{28,24},{20,28},{12,20},{4,12},{1,5},{9... | collective-permute-start | bytes 1216520 | tf_op jit(solution)/shard_map/ppermute | solution.py:67
  95.4 14.3 %collective-permute-start.32 = (bf16[198,1024]{1,0:T(8,128)(2,1)S(1)}, bf16[198,1024]{1,0:T(8,128)(2,1)S(1)}, u32[]{:S(2)}, u32[]{:S(2)}) collective-permute-start(bf16[198,1024]{1,0:T(8,128)(2,1)S(1)} %collective-permute-done.24.refs_3_), channel_id=1, source_target_pairs={{0,8},{8,16},{16,24},{24,28},{28,20},{20,12},{12,4},{4,0},{1,9},{9... | collective-permute-start | bytes 1216520 | tf_op jit(solution)/shard_map/ppermute | solution.py:67
  100.9 17.6 %collective-permute-start.31 = (bf16[196,1024]{1,0:T(8,128)(2,1)S(1)}, bf16[196,1024]{1,0:T(8,128)(2,1)S(1)}, u32[]{:S(2)}, u32[]{:S(2)}) collective-permute-start(bf16[196,1024]{1,0:T(8,128)(2,1)S(1)} %collective-permute-done.28.refs_3_), channel_id=1, source_target_pairs={{0,8},{8,16},{16,24},{24,28},{28,20},{20,12},{12,4},{4,0},{1,9},{9... | collective-permute-start | bytes 1204232 | tf_op jit(solution)/shard_map/ppermute | solution.py:67
  100.9 17.6 %collective-permute-start.30 = (bf16[196,1024]{1,0:T(8,128)(2,1)S(1)}, bf16[196,1024]{1,0:T(8,128)(2,1)S(1)}, u32[]{:S(2)}, u32[]{:S(2)}) collective-permute-start(bf16[196,1024]{1,0:T(8,128)(2,1)S(1)} %collective-permute-done.27.refs_4_), channel_id=1, source_target_pairs={{0,4},{8,0},{16,8},{24,16},{28,24},{20,28},{12,20},{4,12},{1,5},{9... | collective-permute-start | bytes 1204232 | tf_op jit(solution)/shard_map/ppermute | solution.py:67
  106.3 21.0 %collective-permute-start.38 = (bf16[200,1024]{1,0:T(8,128)(2,1)S(1)}, bf16[200,1024]{1,0:T(8,128)(2,1)S(1)}, u32[]{:S(2)}, u32[]{:S(2)}) collective-permute-start(bf16[200,1024]{1,0:T(8,128)(2,1)S(1)} %collective-permute-done.35.refs_3_), channel_id=1, source_target_pairs={{0,8},{8,16},{16,24},{24,28},{28,20},{20,12},{12,4},{4,0},{1,9},{9... | collective-permute-start | bytes 1228808 | tf_op jit(solution)/shard_map/ppermute | solution.py:67
  109.7 17.6 %collective-permute-start.37 = (bf16[200,1024]{1,0:T(8,128)(2,1)S(1)}, bf16[200,1024]{1,0:T(8,128)(2,1)S(1)}, u32[]{:S(2)}, u32[]{:S(2)}) collective-permute-start(bf16[200,1024]{1,0:T(8,128)(2,1)S(1)} %collective-permute-done.34.refs_4_), channel_id=1, source_target_pairs={{0,4},{8,0},{16,8},{24,16},{28,24},{20,28},{12,20},{4,12},{1,5},{9... | collective-permute-start | bytes 1228808 | tf_op jit(solution)/shard_map/ppermute | solution.py:67
  118.8 15.5 %collective-permute-start.40 = (bf16[198,1024]{1,0:T(8,128)(2,1)S(1)}, bf16[198,1024]{1,0:T(8,128)(2,1)S(1)}, u32[]{:S(2)}, u32[]{:S(2)}) collective-permute-start(bf16[198,1024]{1,0:T(8,128)(2,1)S(1)} %collective-permute-done.32.refs_5_), channel_id=1, source_target_pairs={{0,8},{8,16},{16,24},{24,28},{28,20},{20,12},{12,4},{4,0},{1,9},{9... | collective-permute-start | bytes 1216520 | tf_op jit(solution)/shard_map/ppermute | solution.py:67
  118.9 12.7 %collective-permute-start.41 = (bf16[196,1024]{1,0:T(8,128)(2,1)S(1)}, bf16[196,1024]{1,0:T(8,128)(2,1)S(1)}, u32[]{:S(2)}, u32[]{:S(2)}) collective-permute-start(bf16[196,1024]{1,0:T(8,128)(2,1)S(1)} %collective-permute-done.30.refs_6_), channel_id=1, source_target_pairs={{0,4},{8,0},{16,8},{24,16},{28,24},{20,28},{12,20},{4,12},{1,5},{9... | collective-permute-start | bytes 1204232 | tf_op jit(solution)/shard_map/ppermute | solution.py:67
  149.8 12.7 %collective-permute-start.45 = (bf16[200,1024]{1,0:T(8,128)(2,1)S(1)}, bf16[200,1024]{1,0:T(8,128)(2,1)S(1)}, u32[]{:S(2)}, u32[]{:S(2)}) collective-permute-start(bf16[200,1024]{1,0:T(8,128)(2,1)S(1)} %shard_map.246), channel_id=1, source_target_pairs={{0,8},{8,16},{16,24},{24,28},{28,20},{20,12},{12,4},{4,0},{1,9},{9... | collective-permute-start | bytes 1228808 | tf_op jit(solution)/shard_map/ppermute | solution.py:67
  170.4 24.6 %collective-permute-start.55 = (bf16[256,1536]{1,0:T(8,128)(2,1)S(1)}, bf16[256,1536]{1,0:T(8,128)(2,1)S(1)}, u32[]{:S(2)}, u32[]{:S(2)}) collective-permute-start(bf16[256,1536]{1,0:T(8,128)(2,1)S(1)} %shard_map.254.left_ref), channel_id=1, source_target_pairs={{0,2},{1,3},{2,0},{3,1},{4,6},{5,7},{6,4},{7,5},{8,10},{9,11},{10,... | collective-permute-start | bytes 2359304 | tf_op jit(solution)/shard_map/ppermute | solution.py:70
  172.0 13.9 %collective-permute-start.50 = (bf16[200,1024]{1,0:T(8,128)(2,1)S(1)}, bf16[200,1024]{1,0:T(8,128)(2,1)S(1)}, u32[]{:S(2)}, u32[]{:S(2)}) collective-permute-start(bf16[200,1024]{1,0:T(8,128)(2,1)S(1)} %shard_map.253), channel_id=1, source_target_pairs={{0,8},{8,16},{16,24},{24,28},{28,20},{20,12},{12,4},{4,0},{1,9},{9... | collective-permute-start | bytes 1228808 | tf_op jit(solution)/shard_map/ppermute | solution.py:67
  173.6 12.5 %collective-permute-start.49 = (bf16[196,1024]{1,0:T(8,128)(2,1)S(1)}, bf16[196,1024]{1,0:T(8,128)(2,1)S(1)}, u32[]{:S(2)}, u32[]{:S(2)}) collective-permute-start(bf16[196,1024]{1,0:T(8,128)(2,1)S(1)} %shard_map.252), channel_id=1, source_target_pairs={{0,4},{8,0},{16,8},{24,16},{28,24},{20,28},{12,20},{4,12},{1,5},{9... | collective-permute-start | bytes 1204232 | tf_op jit(solution)/shard_map/ppermute | solution.py:67
  177.3 17.4 %collective-permute-start.57 = (bf16[200,1024]{1,0:T(8,128)(2,1)S(1)}, bf16[200,1024]{1,0:T(8,128)(2,1)S(1)}, u32[]{:S(2)}, u32[]{:S(2)}) collective-permute-start(bf16[200,1024]{1,0:T(8,128)(2,1)S(1)} %get-tuple-element.382), channel_id=1, source_target_pairs={{0,4},{8,0},{16,8},{24,16},{28,24},{20,28},{12,20},{4,12},{1,5},{9... | collective-permute-start | bytes 1228808 | tf_op jit(solution)/shard_map/ppermute | solution.py:67
  179.0 15.8 %collective-permute-start.56 = (bf16[200,1024]{1,0:T(8,128)(2,1)S(1)}, bf16[200,1024]{1,0:T(8,128)(2,1)S(1)}, u32[]{:S(2)}, u32[]{:S(2)}) collective-permute-start(bf16[200,1024]{1,0:T(8,128)(2,1)S(1)} %get-tuple-element.372), channel_id=1, source_target_pairs={{0,8},{8,16},{16,24},{24,28},{28,20},{20,12},{12,4},{4,0},{1,9},{9... | collective-permute-start | bytes 1228808 | tf_op jit(solution)/shard_map/ppermute | solution.py:67
  186.2 17.3 %collective-permute-start.54 = (bf16[196,1024]{1,0:T(8,128)(2,1)S(1)}, bf16[196,1024]{1,0:T(8,128)(2,1)S(1)}, u32[]{:S(2)}, u32[]{:S(2)}) collective-permute-start(bf16[196,1024]{1,0:T(8,128)(2,1)S(1)} %get-tuple-element.381), channel_id=1, source_target_pairs={{0,4},{8,0},{16,8},{24,16},{28,24},{20,28},{12,20},{4,12},{1,5},{9... | collective-permute-start | bytes 1204232 | tf_op jit(solution)/shard_map/ppermute | solution.py:67
  187.8 16.2 %collective-permute-start.53 = (bf16[196,1024]{1,0:T(8,128)(2,1)S(1)}, bf16[196,1024]{1,0:T(8,128)(2,1)S(1)}, u32[]{:S(2)}, u32[]{:S(2)}) collective-permute-start(bf16[196,1024]{1,0:T(8,128)(2,1)S(1)} %get-tuple-element.380), channel_id=1, source_target_pairs={{0,8},{8,16},{16,24},{24,28},{28,20},{20,12},{12,4},{4,0},{1,9},{9... | collective-permute-start | bytes 1204232 | tf_op jit(solution)/shard_map/ppermute | solution.py:67
  195.3 20.2 %collective-permute-start.62 = (bf16[200,1024]{1,0:T(8,128)(2,1)S(1)}, bf16[200,1024]{1,0:T(8,128)(2,1)S(1)}, u32[]{:S(2)}, u32[]{:S(2)}) collective-permute-start(bf16[200,1024]{1,0:T(8,128)(2,1)S(1)} %get-tuple-element.412), channel_id=1, source_target_pairs={{0,4},{8,0},{16,8},{24,16},{28,24},{20,28},{12,20},{4,12},{1,5},{9... | collective-permute-start | bytes 1228808 | tf_op jit(solution)/shard_map/ppermute | solution.py:67
  196.8 19.3 %collective-permute-start.61 = (bf16[200,1024]{1,0:T(8,128)(2,1)S(1)}, bf16[200,1024]{1,0:T(8,128)(2,1)S(1)}, u32[]{:S(2)}, u32[]{:S(2)}) collective-permute-start(bf16[200,1024]{1,0:T(8,128)(2,1)S(1)} %get-tuple-element.376), channel_id=1, source_target_pairs={{0,8},{8,16},{16,24},{24,28},{28,20},{20,12},{12,4},{4,0},{1,9},{9... | collective-permute-start | bytes 1228808 | tf_op jit(solution)/shard_map/ppermute | solution.py:67
  203.5 17.6 %collective-permute-start.64 = (bf16[200,1024]{1,0:T(8,128)(2,1)S(1)}, bf16[200,1024]{1,0:T(8,128)(2,1)S(1)}, u32[]{:S(2)}, u32[]{:S(2)}) collective-permute-start(bf16[200,1024]{1,0:T(8,128)(2,1)S(1)} %get-tuple-element.420), channel_id=1, source_target_pairs={{0,4},{8,0},{16,8},{24,16},{28,24},{20,28},{12,20},{4,12},{1,5},{9... | collective-permute-start | bytes 1228808 | tf_op jit(solution)/shard_map/ppermute | solution.py:67
  204.0 17.1 %collective-permute-start.63 = (bf16[200,1024]{1,0:T(8,128)(2,1)S(1)}, bf16[200,1024]{1,0:T(8,128)(2,1)S(1)}, u32[]{:S(2)}, u32[]{:S(2)}) collective-permute-start(bf16[200,1024]{1,0:T(8,128)(2,1)S(1)} %get-tuple-element.387), channel_id=1, source_target_pairs={{0,8},{8,16},{16,24},{24,28},{28,20},{20,12},{12,4},{4,0},{1,9},{9... | collective-permute-start | bytes 1228808 | tf_op jit(solution)/shard_map/ppermute | solution.py:67
  205.9 23.9 %collective-permute-start.58 = (bf16[196,1024]{1,0:T(8,128)(2,1)S(1)}, bf16[196,1024]{1,0:T(8,128)(2,1)S(1)}, u32[]{:S(2)}, u32[]{:S(2)}) collective-permute-start(bf16[196,1024]{1,0:T(8,128)(2,1)S(1)} %get-tuple-element.395), channel_id=1, source_target_pairs={{0,8},{8,16},{16,24},{24,28},{28,20},{20,12},{12,4},{4,0},{1,9},{9... | collective-permute-start | bytes 1204232 | tf_op jit(solution)/shard_map/ppermute | solution.py:67
  215.4 12.4 %collective-permute-start.59 = (bf16[196,1024]{1,0:T(8,128)(2,1)S(1)}, bf16[196,1024]{1,0:T(8,128)(2,1)S(1)}, u32[]{:S(2)}, u32[]{:S(2)}) collective-permute-start(bf16[196,1024]{1,0:T(8,128)(2,1)S(1)} %get-tuple-element.396), channel_id=1, source_target_pairs={{0,4},{8,0},{16,8},{24,16},{28,24},{20,28},{12,20},{4,12},{1,5},{9... | collective-permute-start | bytes 1204232 | tf_op jit(solution)/shard_map/ppermute | solution.py:67
  221.1 21.6 %collective-permute-start.65 = (bf16[256,1536]{1,0:T(8,128)(2,1)S(1)}, bf16[256,1536]{1,0:T(8,128)(2,1)S(1)}, u32[]{:S(2)}, u32[]{:S(2)}) collective-permute-start(bf16[256,1536]{1,0:T(8,128)(2,1)S(1)} %get-tuple-element.422), channel_id=1, source_target_pairs={{0,1},{1,0},{2,3},{3,2},{4,5},{5,4},{6,7},{7,6},{8,9},{9,8},{10,11... | collective-permute-start | bytes 2359304 | tf_op jit(solution)/shard_map/ppermute | solution.py:70
  222.7 14.0 %collective-permute-start.66 = (bf16[208,768]{1,0:T(8,128)(2,1)S(1)}, bf16[208,768]{1,0:T(8,128)(2,1)S(1)}, u32[]{:S(2)}, u32[]{:S(2)}) collective-permute-start(bf16[208,768]{1,0:T(8,128)(2,1)S(1)} %shard_map.266), channel_id=1, source_target_pairs={{0,8},{8,16},{16,24},{24,28},{28,20},{20,12},{12,4},{4,0},{1,9},{9... | collective-permute-start | bytes 958472 | tf_op jit(solution)/shard_map/ppermute | solution.py:67
  231.6 13.8 %collective-permute-start.70 = (bf16[196,1024]{1,0:T(8,128)(2,1)S(1)}, bf16[196,1024]{1,0:T(8,128)(2,1)S(1)}, u32[]{:S(2)}, u32[]{:S(2)}) collective-permute-start(bf16[196,1024]{1,0:T(8,128)(2,1)S(1)} %get-tuple-element.428), channel_id=1, source_target_pairs={{0,8},{8,16},{16,24},{24,28},{28,20},{20,12},{12,4},{4,0},{1,9},{9... | collective-permute-start | bytes 1204232 | tf_op jit(solution)/shard_map/ppermute | solution.py:67
  238.4 13.9 %collective-permute-start.75 = (bf16[208,768]{1,0:T(8,128)(2,1)S(1)}, bf16[208,768]{1,0:T(8,128)(2,1)S(1)}, u32[]{:S(2)}, u32[]{:S(2)}) collective-permute-start(bf16[208,768]{1,0:T(8,128)(2,1)S(1)} %get-tuple-element.434), channel_id=1, source_target_pairs={{0,8},{8,16},{16,24},{24,28},{28,20},{20,12},{12,4},{4,0},{1,9},{9... | collective-permute-start | bytes 958472 | tf_op jit(solution)/shard_map/ppermute | solution.py:67
  241.1 18.3 %collective-permute-start.69 = (bf16[200,1024]{1,0:T(8,128)(2,1)S(1)}, bf16[200,1024]{1,0:T(8,128)(2,1)S(1)}, u32[]{:S(2)}, u32[]{:S(2)}) collective-permute-start(bf16[200,1024]{1,0:T(8,128)(2,1)S(1)} %get-tuple-element.437), channel_id=1, source_target_pairs={{0,4},{8,0},{16,8},{24,16},{28,24},{20,28},{12,20},{4,12},{1,5},{9... | collective-permute-start | bytes 1228808 | tf_op jit(solution)/shard_map/ppermute | solution.py:67
  242.7 18.4 %collective-permute-start.68 = (bf16[200,1024]{1,0:T(8,128)(2,1)S(1)}, bf16[200,1024]{1,0:T(8,128)(2,1)S(1)}, u32[]{:S(2)}, u32[]{:S(2)}) collective-permute-start(bf16[200,1024]{1,0:T(8,128)(2,1)S(1)} %get-tuple-element.417), channel_id=1, source_target_pairs={{0,8},{8,16},{16,24},{24,28},{28,20},{20,12},{12,4},{4,0},{1,9},{9... | collective-permute-start | bytes 1228808 | tf_op jit(solution)/shard_map/ppermute | solution.py:67
  262.9 13.8 %collective-permute-start.77 = (bf16[200,1024]{1,0:T(8,128)(2,1)S(1)}, bf16[200,1024]{1,0:T(8,128)(2,1)S(1)}, u32[]{:S(2)}, u32[]{:S(2)}) collective-permute-start(bf16[200,1024]{1,0:T(8,128)(2,1)S(1)} %get-tuple-element.459), channel_id=1, source_target_pairs={{0,8},{8,16},{16,24},{24,28},{28,20},{20,12},{12,4},{4,0},{1,9},{9... | collective-permute-start | bytes 1228808 | tf_op jit(solution)/shard_map/ppermute | solution.py:67
  263.4 15.2 %collective-permute-start.67 = (bf16[128,1536]{1,0:T(8,128)(2,1)S(1)}, bf16[128,1536]{1,0:T(8,128)(2,1)S(1)}, u32[]{:S(2)}, u32[]{:S(2)}) collective-permute-start(bf16[128,1536]{1,0:T(8,128)(2,1)S(1)} %get-tuple-element.506), channel_id=1, source_target_pairs={{0,2},{1,3},{2,0},{3,1},{4,6},{5,7},{6,4},{7,5},{8,10},{9,11},{10,... | collective-permute-start | bytes 1179656 | tf_op jit(solution)/shard_map/ppermute | solution.py:70
  269.7 12.6 %collective-permute-start.81 = (bf16[208,768]{1,0:T(8,128)(2,1)S(1)}, bf16[208,768]{1,0:T(8,128)(2,1)S(1)}, u32[]{:S(2)}, u32[]{:S(2)}) collective-permute-start(bf16[208,768]{1,0:T(8,128)(2,1)S(1)} %get-tuple-element.466), channel_id=1, source_target_pairs={{0,8},{8,16},{16,24},{24,28},{28,20},{20,12},{12,4},{4,0},{1,9},{9... | collective-permute-start | bytes 958472 | tf_op jit(solution)/shard_map/ppermute | solution.py:67
  (48 other events, 563.4 us)
where the time goes:
time: 291 us
  waiting for transfers between devices  146 us (50%)
  starting transfers between devices  80.4 us (28%)
  Pallas kernels  57.9 us (20%)
  local copies, waits for them, and re-layouts  4.61 us (2%)
    ppermute x56, waiting for transfers between devices, shift(): return lax.ppermute(value, RING, self.pairs[step])  131 us
    ppermute x56, starting transfers between devices, shift(): return lax.ppermute(value, RING, self.pairs[step])  57.8 us
    pallas_call x54, Pallas kernels, near(): pl.pallas_call(body, in_specs=[spec] * len(arrays), out_specs=[spec] * le...  54.8 us
    ppermute x33, starting transfers between devices, partner(): return lax.ppermute(value, 'tp', [(i, i ^ bit) for i in range(self.ways)])  22.6 us
    ppermute x33, waiting for transfers between devices, partner(): return lax.ppermute(value, 'tp', [(i, i ^ bit) for i in range(self.ways)])  14.8 us
  transfers between devices with their start and end apart: 89, of which 42 were waited for; matrix products, arithmetic and copies ran while one was open for 2% of the time, Pallas kernels for 18%

commit v1 on v0

--- a/solution.py
+++ b/solution.py
@@ -13,7 +13,7 @@
 HIGHEST = lax.Precision.HIGHEST
 RING = ("rows", "seq")
 MAX_RING = 8
-EXTRA = 16
+EXTRA = 8
 PADS = (8, 6, 4)
 RPADS = (8, 4, 8)
 CUTS = (2, 1)
@@ -417,7 +417,7 @@
 
 
 def tiles(total, tile, work):
-    lax.fori_loop(0, total // tile, lambda i, _: work(pl.multiple_of(i * tile, tile)), None)
+    lax.fori_loop(0, total // tile, lambda i, _: work(pl.multiple_of(i * tile, tile)), None, unroll=2)
 
 
 def rsq_of(value):
@@ -918,11 +918,23 @@
 
     task("branch", [*core("R0"), *core("R2")], attention)
 
+    branch_end, cot_end = steps[core("R2")[-1]], steps[core("C1")[-1]]
+
+    @do(core("R2")[-1])
+    def _():
+        branch_end()
+        middle, normed_mlp = norm_again(have["in"], *have["branch"], have["gain_two"])
+        have.update(middle=middle, normed_mlp=lanes.pin(normed_mlp))
+
+    @do(core("C1")[-1])
+    def _():
+        cot_end()
+        have["cot"] = lanes.pin(have["cot"])
+
     @do("ML")
     def _():
-        middle, normed_mlp = norm_again(have["in"], *have["branch"], have["gain_two"])
-        hidden, slopes = gated(normed_mlp, have["g"][0], have["u"][0])
-        have.update(middle=middle, normed_mlp=normed_mlp, hidden=lanes.pin(hidden), slopes=slopes)
+        hidden, slopes = gated(have["normed_mlp"], have["g"][0], have["u"][0])
+        have.update(hidden=lanes.pin(hidden), slopes=slopes)
 
     @do("MB")
     def _():
@@ -979,7 +991,7 @@
         )
         have.update(four_grad=lanes.pin(four_grad), in_parts=(keep, give))
 
-    task("ra", ["ra1", "ra2", "ra3", "ra4", "ra5"], lambda: scatter_ring(lanes, have["four_grad"], 1, chunk + EXTRA))
+    task("ra", ["ra1", "ra2", "ra3", "ra4", "ra5"], lambda: scatter_ring(lanes, have["four_grad"], -1, chunk + EXTRA))
     task("grad_in", [*core("N0", 1), "N2"], lambda: scatter_tokens(lanes, *have["in_parts"], CUTS[1]))
 
     if "rm1" in ORDER:

time: 291 us -> 287 us (0.986)
  waiting for transfers between devices: 146 us -> 143 us
    ppermute x56, waiting for transfers between devices: 131 us -> 125 us  [shift(): return lax.ppermute(value, RING, self.pairs[step])]
    ppermute x33, waiting for transfers between devices: 14.8 us -> 18 us  [partner(): return lax.ppermute(value, 'tp', [(i, i ^ bit) for i in range(self.ways)])]
  transfers between devices with their start and end apart: 89 -> 89, of which waited for: 42 -> 42; matrix products, arithmetic and copies ran while one was open for 2% -> 2% of each run, Pallas kernels for 18% -> 17%
where the time goes in v1:
time: 287 us
  waiting for transfers between devices  143 us (50%)
  starting transfers between devices  81.8 us (29%)
  Pallas kernels  55 us (19%)
  local copies, waits for them, and re-layouts  4.18 us (1%)
    ppermute x56, waiting for transfers between devices, shift(): return lax.ppermute(value, RING, self.pairs[step])  125 us
    ppermute x56, starting transfers between devices, shift(): return lax.ppermute(value, RING, self.pairs[step])  59.7 us
    pallas_call x54, Pallas kernels, near(): pl.pallas_call(body, in_specs=[spec] * len(arrays), out_specs=[spec] * le...  52 us
    ppermute x33, starting transfers between devices, partner(): return lax.ppermute(value, 'tp', [(i, i ^ bit) for i in range(self.ways)])  22.2 us
    ppermute x33, waiting for transfers between devices, partner(): return lax.ppermute(value, 'tp', [(i, i ^ bit) for i in range(self.ways)])  18 us
  transfers between devices with their start and end apart: 89, of which 42 were waited for; matrix products, arithmetic and copies ran while one was open for 2% of the time, Pallas kernels for 17%

profile of v1, /device:TPU:0, one launch (start us, length us, event | category | flops | bytes accessed | tf_op | source)
XLA Modules:
  0.0 286.9 jit_solution(16959705469392142480)
XLA Ops:
  2.5 2.6 collective-permute-start.6
  7.9 2.1 collective-permute-done.5.refs_2_
  14.3 4.6 %collective-permute-done.8.refs_2_ = bf16[200,768]{1,0:T(8,128)(2,1)S(1)} collective-permute-done((bf16[200,768]{1,0:T(8,128)(2,1)S(1)}, bf16[200,768]{1,0:T(8,128)(2,1)S(1)}, u32[]{:S(2)}, u32[]{:S(2)}) %collective-permute-start.8) | collective-permute-done | bytes 307232 | tf_op jit(solution)/shard_map/ppermute | solution.py:67
  22.3 5.5 %collective-permute-done.2.refs_2_ = bf16[48,3072]{1,0:T(8,128)(2,1)S(1)} collective-permute-done((bf16[48,3072]{1,0:T(8,128)(2,1)S(1)}, bf16[48,3072]{1,0:T(8,128)(2,1)S(1)}, u32[]{:S(2)}, u32[]{:S(2)}) %collective-permute-start.2) | collective-permute-done | bytes 294944 | tf_op jit(solution)/shard_map/ppermute | solution.py:70
  34.4 7.0 %collective-permute-done.10.refs_2_ = bf16[198,1024]{1,0:T(8,128)(2,1)} collective-permute-done((bf16[198,1024]{1,0:T(8,128)(2,1)}, bf16[198,1024]{1,0:T(8,128)(2,1)}, u32[]{:S(2)}, u32[]{:S(2)}) %collective-permute-start.10) | collective-permute-done | bytes 405536 | tf_op jit(solution)/shard_map/ppermute | solution.py:67
  51.3 6.7 %collective-permute-done.19.refs_1_ = bf16[200,1024]{1,0:T(8,128)(2,1)} collective-permute-done((bf16[200,1024]{1,0:T(8,128)(2,1)S(1)}, bf16[200,1024]{1,0:T(8,128)(2,1)}, u32[]{:S(2)}, u32[]{:S(2)}) %collective-permute-start.19) | collective-permute-done | bytes 409632 | tf_op jit(solution)/shard_map/ppermute | solution.py:67
  58.0 2.0 collective-permute-start.21
  60.0 4.4 %collective-permute-done.17.refs_7_ = bf16[200,768]{1,0:T(8,128)(2,1)S(1)} collective-permute-done((bf16[200,768]{1,0:T(8,128)(2,1)S(1)}, bf16[200,768]{1,0:T(8,128)(2,1)S(1)}, u32[]{:S(2)}, u32[]{:S(2)}) %collective-permute-start.17) | collective-permute-done | bytes 307232 | tf_op jit(solution)/shard_map/ppermute | solution.py:67
  64.5 2.0 collective-permute-start.25
  70.6 3.6 %shard_map.236 = (f32[512,192]{1,0:T(8,128)S(1)}, f32[256,1536]{1,0:T(8,128)S(1)}, bf16[256,1536]{1,0:T(8,128)(2,1)S(1)}) custom-call(bf16[512,192]{1,0:T(8,128)(2,1)S(1)} %get-tuple-element.308.q_ref, bf16[1,512,192]{2,1,0:T(8,128)(2,1)S(1)} %bitcast.18, bf16[1,512,192]{2,1,0:T(8,128)(2,1)S(1)} %bitcast.20, f32[3,512]{1,0:T(4,128)S(1)} %fusion.1.w_ref, ...), custom_call_target="tpu_custom_call" | custom-call | tf_op jit(solution)/shard_map/pallas_call | solution.py:338
  74.8 2.0 collective-permute-start.27
  76.9 5.2 %collective-permute-done.24.refs_3_ = bf16[198,1024]{1,0:T(8,128)(2,1)S(1)} collective-permute-done((bf16[198,1024]{1,0:T(8,128)(2,1)}, bf16[198,1024]{1,0:T(8,128)(2,1)S(1)}, u32[]{:S(2)}, u32[]{:S(2)}) %collective-permute-start.24) | collective-permute-done | bytes 405536 | tf_op jit(solution)/shard_map/ppermute | solution.py:67
  82.1 2.0 collective-permute-start.34
  84.1 6.7 %collective-permute-done.28.refs_3_ = bf16[196,1024]{1,0:T(8,128)(2,1)S(1)} collective-permute-done((bf16[196,1024]{1,0:T(8,128)(2,1)S(1)}, bf16[196,1024]{1,0:T(8,128)(2,1)S(1)}, u32[]{:S(2)}, u32[]{:S(2)}) %collective-permute-start.28) | collective-permute-done | bytes 401440 | tf_op jit(solution)/shard_map/ppermute | solution.py:67
  94.6 5.0 %collective-permute-done.35.refs_3_ = bf16[200,1024]{1,0:T(8,128)(2,1)S(1)} collective-permute-done((bf16[200,1024]{1,0:T(8,128)(2,1)}, bf16[200,1024]{1,0:T(8,128)(2,1)S(1)}, u32[]{:S(2)}, u32[]{:S(2)}) %collective-permute-start.35) | collective-permute-done | bytes 409632 | tf_op jit(solution)/shard_map/ppermute | solution.py:67
  99.6 2.0 collective-permute-start.30
  101.6 3.3 %collective-permute-done.33.refs_6_ = bf16[198,1024]{1,0:T(8,128)(2,1)S(1)} collective-permute-done((bf16[198,1024]{1,0:T(8,128)(2,1)S(1)}, bf16[198,1024]{1,0:T(8,128)(2,1)S(1)}, u32[]{:S(2)}, u32[]{:S(2)}) %collective-permute-start.33) | collective-permute-done | bytes 405536 | tf_op jit(solution)/shard_map/ppermute | solution.py:67
  105.4 3.0 %collective-permute-done.32.refs_5_ = bf16[198,1024]{1,0:T(8,128)(2,1)S(1)} collective-permute-done((bf16[198,1024]{1,0:T(8,128)(2,1)S(1)}, bf16[198,1024]{1,0:T(8,128)(2,1)S(1)}, u32[]{:S(2)}, u32[]{:S(2)}) %collective-permute-start.32) | collective-permute-done | bytes 405536 | tf_op jit(solution)/shard_map/ppermute | solution.py:67
  110.0 7.2 %collective-permute-done.31.refs_5_ = bf16[196,1024]{1,0:T(8,128)(2,1)S(1)} collective-permute-done((bf16[196,1024]{1,0:T(8,128)(2,1)S(1)}, bf16[196,1024]{1,0:T(8,128)(2,1)S(1)}, u32[]{:S(2)}, u32[]{:S(2)}) %collective-permute-start.31) | collective-permute-done | bytes 401440 | tf_op jit(solution)/shard_map/ppermute | solution.py:67
  117.6 2.0 collective-permute-start.41
  119.6 6.4 %collective-permute-done.38.refs_5_ = bf16[200,1024]{1,0:T(8,128)(2,1)S(1)} collective-permute-done((bf16[200,1024]{1,0:T(8,128)(2,1)S(1)}, bf16[200,1024]{1,0:T(8,128)(2,1)S(1)}, u32[]{:S(2)}, u32[]{:S(2)}) %collective-permute-start.38) | collective-permute-done | bytes 409632 | tf_op jit(solution)/shard_map/ppermute | solution.py:67
  130.2 3.0 %collective-permute-done.40.refs_7_ = bf16[198,1024]{1,0:T(8,128)(2,1)S(1)} collective-permute-done((bf16[198,1024]{1,0:T(8,128)(2,1)S(1)}, bf16[198,1024]{1,0:T(8,128)(2,1)S(1)}, u32[]{:S(2)}, u32[]{:S(2)}) %collective-permute-start.40) | collective-permute-done | bytes 405536 | tf_op jit(solution)/shard_map/ppermute | solution.py:67
  136.6 4.7 %shard_map.242 = (bf16[512,1024]{1,0:T(8,128)(2,1)S(1)}, f32[512,2048]{1,0:T(8,128)S(1)}) custom-call(bf16[512,1536]{1,0:T(8,128)(2,1)S(1)} %get-tuple-element.338.x_ref.left_ref, bf16[1536,1024]{1,0:T(8,128)(2,1)S(1)} %shard_map.240.gate_ref.refs_0_, bf16[1536,1024]{1,0:T(8,128)(2,1)S(1)} %shard_map.241.up_ref.refs_1_), custom_call_target="tpu_custom_call" | custom-call | tf_op jit(solution)/shard_map/pallas_call | solution.py:338
  142.5 2.7 collective-permute-done.42.refs_7_
  145.1 2.1 shard_map.245.blocks_ref
  149.2 2.2 shard_map.247.left_ref.right_ref
  151.4 4.7 %shard_map.248 = (f32[256,1536]{1,0:T(8,128)S(1)}, bf16[256,1536]{1,0:T(8,128)(2,1)S(1)}) custom-call(bf16[512,2048]{1,0:T(8,128)(2,1)S(1)} %shard_map.247.left_ref.right_ref, bf16[1536,1024]{1,0:T(8,128)(2,1)S(1)} %shard_map.240.gate_ref.refs_0_, bf16[1536,1024]{1,0:T(8,128)(2,1)S(1)} %shard_map.241.up_ref.refs_1_), custom_call_target="tpu_custom_call" | custom-call | tf_op jit(solution)/shard_map/pallas_call | solution.py:338
  156.2 2.5 shard_map.244
  161.4 2.0 shard_map.251.blocks_ref
  163.5 2.0 shard_map.250.blocks_ref
  171.0 2.3 collective-permute-done.51.refs_0_
  175.6 6.5 %collective-permute-done.50.refs_0_ = bf16[200,1024]{1,0:T(8,128)(2,1)S(1)} collective-permute-done((bf16[200,1024]{1,0:T(8,128)(2,1)S(1)}, bf16[200,1024]{1,0:T(8,128)(2,1)S(1)}, u32[]{:S(2)}, u32[]{:S(2)}) %collective-permute-start.50) | collective-permute-done | bytes 409632 | tf_op jit(solution)/shard_map/ppermute | solution.py:67
  184.5 5.8 %collective-permute-done.57.refs_1_ = bf16[200,1024]{1,0:T(8,128)(2,1)S(1)} collective-permute-done((bf16[200,1024]{1,0:T(8,128)(2,1)S(1)}, bf16[200,1024]{1,0:T(8,128)(2,1)S(1)}, u32[]{:S(2)}, u32[]{:S(2)}) %collective-permute-start.57) | collective-permute-done | bytes 409632 | tf_op jit(solution)/shard_map/ppermute | solution.py:67
  193.5 5.5 %collective-permute-done.54.refs_1_ = bf16[196,1024]{1,0:T(8,128)(2,1)S(1)} collective-permute-done((bf16[196,1024]{1,0:T(8,128)(2,1)S(1)}, bf16[196,1024]{1,0:T(8,128)(2,1)S(1)}, u32[]{:S(2)}, u32[]{:S(2)}) %collective-permute-start.54) | collective-permute-done | bytes 401440 | tf_op jit(solution)/shard_map/ppermute | solution.py:67
  203.3 2.1 shard_map.262
  205.4 5.8 %shard_map.263 = (bf16[512,192]{1,0:T(8,128)(2,1)S(1)}, bf16[1,512,192]{2,1,0:T(8,128)(2,1)S(1)}, bf16[1,512,192]{2,1,0:T(8,128)(2,1)S(1)}, f32[1,768]{1,0:T(1,128)S(1)}) custom-call(bf16[512,192]{1,0:T(8,128)(2,1)S(1)} %get-tuple-element.308.q_ref, bf16[1,512,192]{2,1,0:T(8,128)(2,1)S(1)} %bitcast.19, bf16[1,512,192]{2,1,0:T(8,128)(2,1)S(1)} %bitcast.21, ...), custom_call_target="tpu_custom_call" | custom-call | tf_op jit(solution)/shard_map/pallas_call | solution.py:338
  211.9 3.9 %shard_map.264 = (bf16[8,200,768]{2,1,0:T(8,128)(2,1)S(1)}, f32[256,1536]{1,0:T(8,128)S(1)}, bf16[256,1536]{1,0:T(8,128)(2,1)S(1)}) custom-call(bf16[512,1536]{1,0:T(8,128)(2,1)S(1)} %get-tuple-element.401.n_ref, bf16[512,1536]{1,0:T(8,128)(2,1)S(1)} %constant_dynamic-update-slice_fusion.x_ref, f32[512,128]{1,0:T(8,128)S(1)} %get-tuple-element.402.rsq_ref, ...), custom_call_target="tpu_custom_call" | custom-call | tf_op jit(solution)/shard_map/pallas_call | solution.py:338
  220.5 4.7 %collective-permute-done.59.refs_1_ = bf16[196,1024]{1,0:T(8,128)(2,1)S(1)} collective-permute-done((bf16[196,1024]{1,0:T(8,128)(2,1)S(1)}, bf16[196,1024]{1,0:T(8,128)(2,1)S(1)}, u32[]{:S(2)}, u32[]{:S(2)}) %collective-permute-start.59) | collective-permute-done | bytes 401440 | tf_op jit(solution)/shard_map/ppermute | solution.py:67
  228.9 2.9 %collective-permute-done.66.refs_0_ = bf16[200,768]{1,0:T(8,128)(2,1)S(1)} collective-permute-done((bf16[200,768]{1,0:T(8,128)(2,1)S(1)}, bf16[200,768]{1,0:T(8,128)(2,1)S(1)}, u32[]{:S(2)}, u32[]{:S(2)}) %collective-permute-start.66) | collective-permute-done | bytes 307232 | tf_op jit(solution)/shard_map/ppermute | solution.py:67
  234.0 6.6 %collective-permute-done.71.refs_1_ = bf16[196,1024]{1,0:T(8,128)(2,1)S(1)} collective-permute-done((bf16[196,1024]{1,0:T(8,128)(2,1)S(1)}, bf16[196,1024]{1,0:T(8,128)(2,1)S(1)}, u32[]{:S(2)}, u32[]{:S(2)}) %collective-permute-start.71) | collective-permute-done | bytes 401440 | tf_op jit(solution)/shard_map/ppermute | solution.py:67
  243.2 3.9 %collective-permute-done.76.refs_1_ = bf16[200,768]{1,0:T(8,128)(2,1)S(1)} collective-permute-done((bf16[200,768]{1,0:T(8,128)(2,1)S(1)}, bf16[200,768]{1,0:T(8,128)(2,1)S(1)}, u32[]{:S(2)}, u32[]{:S(2)}) %collective-permute-start.76) | collective-permute-done | bytes 307232 | tf_op jit(solution)/shard_map/ppermute | solution.py:67
  249.7 4.6 %collective-permute-done.74.refs_3_ = bf16[48,2048]{1,0:T(8,128)(2,1)S(1)} collective-permute-done((bf16[48,2048]{1,0:T(8,128)(2,1)S(1)}, bf16[48,2048]{1,0:T(8,128)(2,1)S(1)}, u32[]{:S(2)}, u32[]{:S(2)}) %collective-permute-start.74) | collective-permute-done | bytes 196640 | tf_op jit(solution)/shard_map/ppermute | solution.py:70
  257.4 2.2 collective-permute-start.78
  261.4 2.0 collective-permute-done.79.refs_0_
  265.6 4.2 %collective-permute-done.78.refs_1_ = bf16[200,1024]{1,0:T(8,128)(2,1)S(1)} collective-permute-done((bf16[200,1024]{1,0:T(8,128)(2,1)S(1)}, bf16[200,1024]{1,0:T(8,128)(2,1)S(1)}, u32[]{:S(2)}, u32[]{:S(2)}) %collective-permute-start.78) | collective-permute-done | bytes 409632 | tf_op jit(solution)/shard_map/ppermute | solution.py:67
  269.8 2.4 collective-permute-done.77.refs_0_
  272.5 2.0 collective-permute-start.88
  276.2 1.9 collective-permute-done.81.refs_0_
  (211 shorter events, 104.9 us)
Async XLA Ops:
  13.9 13.9 %collective-permute-start.2 = (bf16[48,3072]{1,0:T(8,128)(2,1)S(1)}, bf16[48,3072]{1,0:T(8,128)(2,1)S(1)}, u32[]{:S(2)}, u32[]{:S(2)}) collective-permute-start(bf16[48,3072]{1,0:T(8,128)(2,1)S(1)} %get-tuple-element.271), channel_id=1, source_target_pairs={{0,2},{1,3},{2,0},{3,1},{4,6},{5,7},{6,4},{7,5},{8,10},{9,11},{10,... | collective-permute-start | bytes 884744 | tf_op jit(solution)/shard_map/ppermute | solution.py:70
  28.7 12.7 %collective-permute-start.10 = (bf16[198,1024]{1,0:T(8,128)(2,1)}, bf16[198,1024]{1,0:T(8,128)(2,1)}, u32[]{:S(2)}, u32[]{:S(2)}) collective-permute-start(bf16[198,1024]{1,0:T(8,128)(2,1)} %get-tuple-element.285.refs_0_), channel_id=1, source_target_pairs={{0,4},{8,0},{16,8},{24,16},{28,24},{20,28},{12,20},{4,12},{1,5},{9... | collective-permute-start | bytes 1216520 | tf_op jit(solution)/shard_map/ppermute | solution.py:67
  30.3 12.7 %collective-permute-start.9 = (bf16[198,1024]{1,0:T(8,128)(2,1)}, bf16[198,1024]{1,0:T(8,128)(2,1)}, u32[]{:S(2)}, u32[]{:S(2)}) collective-permute-start(bf16[198,1024]{1,0:T(8,128)(2,1)} %get-tuple-element.285.refs_0_), channel_id=1, source_target_pairs={{0,8},{8,16},{16,24},{24,28},{28,20},{20,12},{12,4},{4,0},{1,9},{9... | collective-permute-start | bytes 1216520 | tf_op jit(solution)/shard_map/ppermute | solution.py:67
  32.3 14.1 %collective-permute-start.16 = (bf16[200,768]{1,0:T(8,128)(2,1)S(1)}, bf16[200,768]{1,0:T(8,128)(2,1)S(1)}, u32[]{:S(2)}, u32[]{:S(2)}) collective-permute-start(bf16[200,768]{1,0:T(8,128)(2,1)S(1)} %collective-permute-done.12.refs_4_), channel_id=1, source_target_pairs={{0,4},{8,0},{16,8},{24,16},{28,24},{20,28},{12,20},{4,12},{1,5},{9... | collective-permute-start | bytes 921608 | tf_op jit(solution)/shard_map/ppermute | solution.py:67
  33.9 15.3 %collective-permute-start.15 = (bf16[200,768]{1,0:T(8,128)(2,1)S(1)}, bf16[200,768]{1,0:T(8,128)(2,1)S(1)}, u32[]{:S(2)}, u32[]{:S(2)}) collective-permute-start(bf16[200,768]{1,0:T(8,128)(2,1)S(1)} %collective-permute-done.11.refs_3_), channel_id=1, source_target_pairs={{0,8},{8,16},{16,24},{24,28},{28,20},{20,12},{12,4},{4,0},{1,9},{9... | collective-permute-start | bytes 921608 | tf_op jit(solution)/shard_map/ppermute | solution.py:67
  41.4 23.1 %collective-permute-start.14 = (bf16[128,1536]{1,0:T(8,128)(2,1)}, bf16[128,1536]{1,0:T(8,128)(2,1)}, u32[]{:S(2)}, u32[]{:S(2)}) collective-permute-start(bf16[128,1536]{1,0:T(8,128)(2,1)} %bitcast.26), channel_id=1, source_target_pairs={{0,2},{1,3},{2,0},{3,1},{4,6},{5,7},{6,4},{7,5},{8,10},{9,11},{10,... | collective-permute-start | bytes 1179656 | tf_op jit(solution)/shard_map/ppermute | solution.py:70
  43.0 23.5 %collective-permute-start.13 = (bf16[128,1536]{1,0:T(8,128)(2,1)}, bf16[128,1536]{1,0:T(8,128)(2,1)}, u32[]{:S(2)}, u32[]{:S(2)}) collective-permute-start(bf16[128,1536]{1,0:T(8,128)(2,1)} %bitcast), channel_id=1, source_target_pairs={{0,1},{1,0},{2,3},{3,2},{4,5},{5,4},{6,7},{7,6},{8,9},{9,8},{10,11... | collective-permute-start | bytes 1179656 | tf_op jit(solution)/shard_map/ppermute | solution.py:70
  43.0 15.0 %collective-permute-start.19 = (bf16[200,1024]{1,0:T(8,128)(2,1)S(1)}, bf16[200,1024]{1,0:T(8,128)(2,1)}, u32[]{:S(2)}, u32[]{:S(2)}) collective-permute-start(bf16[200,1024]{1,0:T(8,128)(2,1)S(1)} %get-tuple-element.295.refs_0_), channel_id=1, source_target_pairs={{0,8},{8,16},{16,24},{24,28},{28,20},{20,12},{12,4},{4,0},{1,9},{9... | collective-permute-start | bytes 1228808 | tf_op jit(solution)/shard_map/ppermute | solution.py:67
  49.1 15.4 %collective-permute-start.17 = (bf16[200,768]{1,0:T(8,128)(2,1)S(1)}, bf16[200,768]{1,0:T(8,128)(2,1)S(1)}, u32[]{:S(2)}, u32[]{:S(2)}) collective-permute-start(bf16[200,768]{1,0:T(8,128)(2,1)S(1)} %collective-permute-done.15.refs_5_), channel_id=1, source_target_pairs={{0,8},{8,16},{16,24},{24,28},{28,20},{20,12},{12,4},{4,0},{1,9},{9... | collective-permute-start | bytes 921608 | tf_op jit(solution)/shard_map/ppermute | solution.py:67
  58.0 16.2 %collective-permute-start.22 = (bf16[196,1024]{1,0:T(8,128)(2,1)S(1)}, bf16[196,1024]{1,0:T(8,128)(2,1)S(1)}, u32[]{:S(2)}, u32[]{:S(2)}) collective-permute-start(bf16[196,1024]{1,0:T(8,128)(2,1)S(1)} %get-tuple-element.289.refs_0_), channel_id=1, source_target_pairs={{0,8},{8,16},{16,24},{24,28},{28,20},{20,12},{12,4},{4,0},{1,9},{9... | collective-permute-start | bytes 1204232 | tf_op jit(solution)/shard_map/ppermute | solution.py:67
  58.0 16.2 %collective-permute-start.21 = (bf16[196,1024]{1,0:T(8,128)(2,1)S(1)}, bf16[196,1024]{1,0:T(8,128)(2,1)S(1)}, u32[]{:S(2)}, u32[]{:S(2)}) collective-permute-start(bf16[196,1024]{1,0:T(8,128)(2,1)S(1)} %get-tuple-element.289.refs_0_), channel_id=1, source_target_pairs={{0,4},{8,0},{16,8},{24,16},{28,24},{20,28},{12,20},{4,12},{1,5},{9... | collective-permute-start | bytes 1204232 | tf_op jit(solution)/shard_map/ppermute | solution.py:67
  64.5 17.6 %collective-permute-start.24 = (bf16[198,1024]{1,0:T(8,128)(2,1)}, bf16[198,1024]{1,0:T(8,128)(2,1)S(1)}, u32[]{:S(2)}, u32[]{:S(2)}) collective-permute-start(bf16[198,1024]{1,0:T(8,128)(2,1)} %collective-permute-done.9.refs_1_), channel_id=1, source_target_pairs={{0,8},{8,16},{16,24},{24,28},{28,20},{20,12},{12,4},{4,0},{1,9},{9... | collective-permute-start | bytes 1216520 | tf_op jit(solution)/shard_map/ppermute | solution.py:67
  74.8 16.0 %collective-permute-start.28 = (bf16[196,1024]{1,0:T(8,128)(2,1)S(1)}, bf16[196,1024]{1,0:T(8,128)(2,1)S(1)}, u32[]{:S(2)}, u32[]{:S(2)}) collective-permute-start(bf16[196,1024]{1,0:T(8,128)(2,1)S(1)} %collective-permute-done.22.refs_1_), channel_id=1, source_target_pairs={{0,8},{8,16},{16,24},{24,28},{28,20},{20,12},{12,4},{4,0},{1,9},{9... | collective-permute-start | bytes 1204232 | tf_op jit(solution)/shard_map/ppermute | solution.py:67
  74.8 16.0 %collective-permute-start.27 = (bf16[196,1024]{1,0:T(8,128)(2,1)S(1)}, bf16[196,1024]{1,0:T(8,128)(2,1)S(1)}, u32[]{:S(2)}, u32[]{:S(2)}) collective-permute-start(bf16[196,1024]{1,0:T(8,128)(2,1)S(1)} %collective-permute-done.21.refs_2_), channel_id=1, source_target_pairs={{0,4},{8,0},{16,8},{24,16},{28,24},{20,28},{12,20},{4,12},{1,5},{9... | collective-permute-start | bytes 1204232 | tf_op jit(solution)/shard_map/ppermute | solution.py:67
  82.1 17.5 %collective-permute-start.35 = (bf16[200,1024]{1,0:T(8,128)(2,1)}, bf16[200,1024]{1,0:T(8,128)(2,1)S(1)}, u32[]{:S(2)}, u32[]{:S(2)}) collective-permute-start(bf16[200,1024]{1,0:T(8,128)(2,1)} %collective-permute-done.19.refs_1_), channel_id=1, source_target_pairs={{0,8},{8,16},{16,24},{24,28},{28,20},{20,12},{12,4},{4,0},{1,9},{9... | collective-permute-start | bytes 1228808 | tf_op jit(solution)/shard_map/ppermute | solution.py:67
  82.1 17.5 %collective-permute-start.34 = (bf16[200,1024]{1,0:T(8,128)(2,1)}, bf16[200,1024]{1,0:T(8,128)(2,1)S(1)}, u32[]{:S(2)}, u32[]{:S(2)}) collective-permute-start(bf16[200,1024]{1,0:T(8,128)(2,1)} %collective-permute-done.18.refs_2_), channel_id=1, source_target_pairs={{0,4},{8,0},{16,8},{24,16},{28,24},{20,28},{12,20},{4,12},{1,5},{9... | collective-permute-start | bytes 1228808 | tf_op jit(solution)/shard_map/ppermute | solution.py:67
  91.0 26.1 %collective-permute-start.29 = (bf16[256,1536]{1,0:T(8,128)(2,1)S(1)}, bf16[256,1536]{1,0:T(8,128)(2,1)S(1)}, u32[]{:S(2)}, u32[]{:S(2)}) collective-permute-start(bf16[256,1536]{1,0:T(8,128)(2,1)S(1)} %shard_map.237.left_ref), channel_id=1, source_target_pairs={{0,2},{1,3},{2,0},{3,1},{4,6},{5,7},{6,4},{7,5},{8,10},{9,11},{10,... | collective-permute-start | bytes 2359304 | tf_op jit(solution)/shard_map/ppermute | solution.py:70
  94.2 14.2 %collective-permute-start.32 = (bf16[198,1024]{1,0:T(8,128)(2,1)S(1)}, bf16[198,1024]{1,0:T(8,128)(2,1)S(1)}, u32[]{:S(2)}, u32[]{:S(2)}) collective-permute-start(bf16[198,1024]{1,0:T(8,128)(2,1)S(1)} %collective-permute-done.24.refs_3_), channel_id=1, source_target_pairs={{0,8},{8,16},{16,24},{24,28},{28,20},{20,12},{12,4},{4,0},{1,9},{9... | collective-permute-start | bytes 1216520 | tf_op jit(solution)/shard_map/ppermute | solution.py:67
  99.6 17.6 %collective-permute-start.31 = (bf16[196,1024]{1,0:T(8,128)(2,1)S(1)}, bf16[196,1024]{1,0:T(8,128)(2,1)S(1)}, u32[]{:S(2)}, u32[]{:S(2)}) collective-permute-start(bf16[196,1024]{1,0:T(8,128)(2,1)S(1)} %collective-permute-done.28.refs_3_), channel_id=1, source_target_pairs={{0,8},{8,16},{16,24},{24,28},{28,20},{20,12},{12,4},{4,0},{1,9},{9... | collective-permute-start | bytes 1204232 | tf_op jit(solution)/shard_map/ppermute | solution.py:67
  99.6 17.6 %collective-permute-start.30 = (bf16[196,1024]{1,0:T(8,128)(2,1)S(1)}, bf16[196,1024]{1,0:T(8,128)(2,1)S(1)}, u32[]{:S(2)}, u32[]{:S(2)}) collective-permute-start(bf16[196,1024]{1,0:T(8,128)(2,1)S(1)} %collective-permute-done.27.refs_4_), channel_id=1, source_target_pairs={{0,4},{8,0},{16,8},{24,16},{28,24},{20,28},{12,20},{4,12},{1,5},{9... | collective-permute-start | bytes 1204232 | tf_op jit(solution)/shard_map/ppermute | solution.py:67
  105.0 21.0 %collective-permute-start.38 = (bf16[200,1024]{1,0:T(8,128)(2,1)S(1)}, bf16[200,1024]{1,0:T(8,128)(2,1)S(1)}, u32[]{:S(2)}, u32[]{:S(2)}) collective-permute-start(bf16[200,1024]{1,0:T(8,128)(2,1)S(1)} %collective-permute-done.35.refs_3_), channel_id=1, source_target_pairs={{0,8},{8,16},{16,24},{24,28},{28,20},{20,12},{12,4},{4,0},{1,9},{9... | collective-permute-start | bytes 1228808 | tf_op jit(solution)/shard_map/ppermute | solution.py:67
  108.4 17.6 %collective-permute-start.37 = (bf16[200,1024]{1,0:T(8,128)(2,1)S(1)}, bf16[200,1024]{1,0:T(8,128)(2,1)S(1)}, u32[]{:S(2)}, u32[]{:S(2)}) collective-permute-start(bf16[200,1024]{1,0:T(8,128)(2,1)S(1)} %collective-permute-done.34.refs_4_), channel_id=1, source_target_pairs={{0,4},{8,0},{16,8},{24,16},{28,24},{20,28},{12,20},{4,12},{1,5},{9... | collective-permute-start | bytes 1228808 | tf_op jit(solution)/shard_map/ppermute | solution.py:67
  117.5 15.8 %collective-permute-start.40 = (bf16[198,1024]{1,0:T(8,128)(2,1)S(1)}, bf16[198,1024]{1,0:T(8,128)(2,1)S(1)}, u32[]{:S(2)}, u32[]{:S(2)}) collective-permute-start(bf16[198,1024]{1,0:T(8,128)(2,1)S(1)} %collective-permute-done.32.refs_5_), channel_id=1, source_target_pairs={{0,8},{8,16},{16,24},{24,28},{28,20},{20,12},{12,4},{4,0},{1,9},{9... | collective-permute-start | bytes 1216520 | tf_op jit(solution)/shard_map/ppermute | solution.py:67
  117.6 12.7 %collective-permute-start.41 = (bf16[196,1024]{1,0:T(8,128)(2,1)S(1)}, bf16[196,1024]{1,0:T(8,128)(2,1)S(1)}, u32[]{:S(2)}, u32[]{:S(2)}) collective-permute-start(bf16[196,1024]{1,0:T(8,128)(2,1)S(1)} %collective-permute-done.30.refs_6_), channel_id=1, source_target_pairs={{0,4},{8,0},{16,8},{24,16},{28,24},{20,28},{12,20},{4,12},{1,5},{9... | collective-permute-start | bytes 1204232 | tf_op jit(solution)/shard_map/ppermute | solution.py:67
  165.9 25.3 %collective-permute-start.55 = (bf16[256,1536]{1,0:T(8,128)(2,1)S(1)}, bf16[256,1536]{1,0:T(8,128)(2,1)S(1)}, u32[]{:S(2)}, u32[]{:S(2)}) collective-permute-start(bf16[256,1536]{1,0:T(8,128)(2,1)S(1)} %shard_map.254.left_ref), channel_id=1, source_target_pairs={{0,2},{1,3},{2,0},{3,1},{4,6},{5,7},{6,4},{7,5},{8,10},{9,11},{10,... | collective-permute-start | bytes 2359304 | tf_op jit(solution)/shard_map/ppermute | solution.py:70
  167.5 14.6 %collective-permute-start.50 = (bf16[200,1024]{1,0:T(8,128)(2,1)S(1)}, bf16[200,1024]{1,0:T(8,128)(2,1)S(1)}, u32[]{:S(2)}, u32[]{:S(2)}) collective-permute-start(bf16[200,1024]{1,0:T(8,128)(2,1)S(1)} %shard_map.253), channel_id=1, source_target_pairs={{0,8},{8,16},{16,24},{24,28},{28,20},{20,12},{12,4},{4,0},{1,9},{9... | collective-permute-start | bytes 1228808 | tf_op jit(solution)/shard_map/ppermute | solution.py:67
  169.1 13.2 %collective-permute-start.49 = (bf16[196,1024]{1,0:T(8,128)(2,1)S(1)}, bf16[196,1024]{1,0:T(8,128)(2,1)S(1)}, u32[]{:S(2)}, u32[]{:S(2)}) collective-permute-start(bf16[196,1024]{1,0:T(8,128)(2,1)S(1)} %shard_map.252), channel_id=1, source_target_pairs={{0,4},{8,0},{16,8},{24,16},{28,24},{20,28},{12,20},{4,12},{1,5},{9... | collective-permute-start | bytes 1204232 | tf_op jit(solution)/shard_map/ppermute | solution.py:67
  173.5 16.7 %collective-permute-start.57 = (bf16[200,1024]{1,0:T(8,128)(2,1)S(1)}, bf16[200,1024]{1,0:T(8,128)(2,1)S(1)}, u32[]{:S(2)}, u32[]{:S(2)}) collective-permute-start(bf16[200,1024]{1,0:T(8,128)(2,1)S(1)} %get-tuple-element.386), channel_id=1, source_target_pairs={{0,4},{8,0},{16,8},{24,16},{28,24},{20,28},{12,20},{4,12},{1,5},{9... | collective-permute-start | bytes 1228808 | tf_op jit(solution)/shard_map/ppermute | solution.py:67
  175.2 15.7 %collective-permute-start.56 = (bf16[200,1024]{1,0:T(8,128)(2,1)S(1)}, bf16[200,1024]{1,0:T(8,128)(2,1)S(1)}, u32[]{:S(2)}, u32[]{:S(2)}) collective-permute-start(bf16[200,1024]{1,0:T(8,128)(2,1)S(1)} %get-tuple-element.376), channel_id=1, source_target_pairs={{0,8},{8,16},{16,24},{24,28},{28,20},{20,12},{12,4},{4,0},{1,9},{9... | collective-permute-start | bytes 1228808 | tf_op jit(solution)/shard_map/ppermute | solution.py:67
  182.4 16.6 %collective-permute-start.54 = (bf16[196,1024]{1,0:T(8,128)(2,1)S(1)}, bf16[196,1024]{1,0:T(8,128)(2,1)S(1)}, u32[]{:S(2)}, u32[]{:S(2)}) collective-permute-start(bf16[196,1024]{1,0:T(8,128)(2,1)S(1)} %get-tuple-element.385), channel_id=1, source_target_pairs={{0,4},{8,0},{16,8},{24,16},{28,24},{20,28},{12,20},{4,12},{1,5},{9... | collective-permute-start | bytes 1204232 | tf_op jit(solution)/shard_map/ppermute | solution.py:67
  184.0 15.6 %collective-permute-start.53 = (bf16[196,1024]{1,0:T(8,128)(2,1)S(1)}, bf16[196,1024]{1,0:T(8,128)(2,1)S(1)}, u32[]{:S(2)}, u32[]{:S(2)}) collective-permute-start(bf16[196,1024]{1,0:T(8,128)(2,1)S(1)} %get-tuple-element.384), channel_id=1, source_target_pairs={{0,8},{8,16},{16,24},{24,28},{28,20},{20,12},{12,4},{4,0},{1,9},{9... | collective-permute-start | bytes 1204232 | tf_op jit(solution)/shard_map/ppermute | solution.py:67
  191.4 19.7 %collective-permute-start.62 = (bf16[200,1024]{1,0:T(8,128)(2,1)S(1)}, bf16[200,1024]{1,0:T(8,128)(2,1)S(1)}, u32[]{:S(2)}, u32[]{:S(2)}) collective-permute-start(bf16[200,1024]{1,0:T(8,128)(2,1)S(1)} %get-tuple-element.416), channel_id=1, source_target_pairs={{0,4},{8,0},{16,8},{24,16},{28,24},{20,28},{12,20},{4,12},{1,5},{9... | collective-permute-start | bytes 1228808 | tf_op jit(solution)/shard_map/ppermute | solution.py:67
  193.0 18.6 %collective-permute-start.61 = (bf16[200,1024]{1,0:T(8,128)(2,1)S(1)}, bf16[200,1024]{1,0:T(8,128)(2,1)S(1)}, u32[]{:S(2)}, u32[]{:S(2)}) collective-permute-start(bf16[200,1024]{1,0:T(8,128)(2,1)S(1)} %get-tuple-element.380), channel_id=1, source_target_pairs={{0,8},{8,16},{16,24},{24,28},{28,20},{20,12},{12,4},{4,0},{1,9},{9... | collective-permute-start | bytes 1228808 | tf_op jit(solution)/shard_map/ppermute | solution.py:67
  199.0 17.6 %collective-permute-start.64 = (bf16[200,1024]{1,0:T(8,128)(2,1)S(1)}, bf16[200,1024]{1,0:T(8,128)(2,1)S(1)}, u32[]{:S(2)}, u32[]{:S(2)}) collective-permute-start(bf16[200,1024]{1,0:T(8,128)(2,1)S(1)} %get-tuple-element.424), channel_id=1, source_target_pairs={{0,4},{8,0},{16,8},{24,16},{28,24},{20,28},{12,20},{4,12},{1,5},{9... | collective-permute-start | bytes 1228808 | tf_op jit(solution)/shard_map/ppermute | solution.py:67
  199.7 17.6 %collective-permute-start.63 = (bf16[200,1024]{1,0:T(8,128)(2,1)S(1)}, bf16[200,1024]{1,0:T(8,128)(2,1)S(1)}, u32[]{:S(2)}, u32[]{:S(2)}) collective-permute-start(bf16[200,1024]{1,0:T(8,128)(2,1)S(1)} %get-tuple-element.391), channel_id=1, source_target_pairs={{0,8},{8,16},{16,24},{24,28},{28,20},{20,12},{12,4},{4,0},{1,9},{9... | collective-permute-start | bytes 1228808 | tf_op jit(solution)/shard_map/ppermute | solution.py:67
  201.4 23.8 %collective-permute-start.58 = (bf16[196,1024]{1,0:T(8,128)(2,1)S(1)}, bf16[196,1024]{1,0:T(8,128)(2,1)S(1)}, u32[]{:S(2)}, u32[]{:S(2)}) collective-permute-start(bf16[196,1024]{1,0:T(8,128)(2,1)S(1)} %get-tuple-element.399), channel_id=1, source_target_pairs={{0,8},{8,16},{16,24},{24,28},{28,20},{20,12},{12,4},{4,0},{1,9},{9... | collective-permute-start | bytes 1204232 | tf_op jit(solution)/shard_map/ppermute | solution.py:67
  211.1 14.0 %collective-permute-start.59 = (bf16[196,1024]{1,0:T(8,128)(2,1)S(1)}, bf16[196,1024]{1,0:T(8,128)(2,1)S(1)}, u32[]{:S(2)}, u32[]{:S(2)}) collective-permute-start(bf16[196,1024]{1,0:T(8,128)(2,1)S(1)} %get-tuple-element.400), channel_id=1, source_target_pairs={{0,4},{8,0},{16,8},{24,16},{28,24},{20,28},{12,20},{4,12},{1,5},{9... | collective-permute-start | bytes 1204232 | tf_op jit(solution)/shard_map/ppermute | solution.py:67
  217.2 24.1 %collective-permute-start.65 = (bf16[256,1536]{1,0:T(8,128)(2,1)S(1)}, bf16[256,1536]{1,0:T(8,128)(2,1)S(1)}, u32[]{:S(2)}, u32[]{:S(2)}) collective-permute-start(bf16[256,1536]{1,0:T(8,128)(2,1)S(1)} %get-tuple-element.426), channel_id=1, source_target_pairs={{0,1},{1,0},{2,3},{3,2},{4,5},{5,4},{6,7},{7,6},{8,9},{9,8},{10,11... | collective-permute-start | bytes 2359304 | tf_op jit(solution)/shard_map/ppermute | solution.py:70
  218.9 12.9 %collective-permute-start.66 = (bf16[200,768]{1,0:T(8,128)(2,1)S(1)}, bf16[200,768]{1,0:T(8,128)(2,1)S(1)}, u32[]{:S(2)}, u32[]{:S(2)}) collective-permute-start(bf16[200,768]{1,0:T(8,128)(2,1)S(1)} %shard_map.266), channel_id=1, source_target_pairs={{0,4},{8,0},{16,8},{24,16},{28,24},{20,28},{12,20},{4,12},{1,5},{9... | collective-permute-start | bytes 921608 | tf_op jit(solution)/shard_map/ppermute | solution.py:67
  225.4 15.1 %collective-permute-start.71 = (bf16[196,1024]{1,0:T(8,128)(2,1)S(1)}, bf16[196,1024]{1,0:T(8,128)(2,1)S(1)}, u32[]{:S(2)}, u32[]{:S(2)}) collective-permute-start(bf16[196,1024]{1,0:T(8,128)(2,1)S(1)} %get-tuple-element.443), channel_id=1, source_target_pairs={{0,4},{8,0},{16,8},{24,16},{28,24},{20,28},{12,20},{4,12},{1,5},{9... | collective-permute-start | bytes 1204232 | tf_op jit(solution)/shard_map/ppermute | solution.py:67
  226.6 16.3 %collective-permute-start.70 = (bf16[196,1024]{1,0:T(8,128)(2,1)S(1)}, bf16[196,1024]{1,0:T(8,128)(2,1)S(1)}, u32[]{:S(2)}, u32[]{:S(2)}) collective-permute-start(bf16[196,1024]{1,0:T(8,128)(2,1)S(1)} %get-tuple-element.432), channel_id=1, source_target_pairs={{0,8},{8,16},{16,24},{24,28},{28,20},{20,12},{12,4},{4,0},{1,9},{9... | collective-permute-start | bytes 1204232 | tf_op jit(solution)/shard_map/ppermute | solution.py:67
  231.9 15.2 %collective-permute-start.76 = (bf16[200,768]{1,0:T(8,128)(2,1)S(1)}, bf16[200,768]{1,0:T(8,128)(2,1)S(1)}, u32[]{:S(2)}, u32[]{:S(2)}) collective-permute-start(bf16[200,768]{1,0:T(8,128)(2,1)S(1)} %get-tuple-element.452), channel_id=1, source_target_pairs={{0,4},{8,0},{16,8},{24,16},{28,24},{20,28},{12,20},{4,12},{1,5},{9... | collective-permute-start | bytes 921608 | tf_op jit(solution)/shard_map/ppermute | solution.py:67
  232.7 14.4 %collective-permute-start.75 = (bf16[200,768]{1,0:T(8,128)(2,1)S(1)}, bf16[200,768]{1,0:T(8,128)(2,1)S(1)}, u32[]{:S(2)}, u32[]{:S(2)}) collective-permute-start(bf16[200,768]{1,0:T(8,128)(2,1)S(1)} %get-tuple-element.438), channel_id=1, source_target_pairs={{0,8},{8,16},{16,24},{24,28},{28,20},{20,12},{12,4},{4,0},{1,9},{9... | collective-permute-start | bytes 921608 | tf_op jit(solution)/shard_map/ppermute | solution.py:67
  240.5 16.6 %collective-permute-start.69 = (bf16[200,1024]{1,0:T(8,128)(2,1)S(1)}, bf16[200,1024]{1,0:T(8,128)(2,1)S(1)}, u32[]{:S(2)}, u32[]{:S(2)}) collective-permute-start(bf16[200,1024]{1,0:T(8,128)(2,1)S(1)} %get-tuple-element.441), channel_id=1, source_target_pairs={{0,4},{8,0},{16,8},{24,16},{28,24},{20,28},{12,20},{4,12},{1,5},{9... | collective-permute-start | bytes 1228808 | tf_op jit(solution)/shard_map/ppermute | solution.py:67
  241.3 15.9 %collective-permute-start.68 = (bf16[200,1024]{1,0:T(8,128)(2,1)S(1)}, bf16[200,1024]{1,0:T(8,128)(2,1)S(1)}, u32[]{:S(2)}, u32[]{:S(2)}) collective-permute-start(bf16[200,1024]{1,0:T(8,128)(2,1)S(1)} %get-tuple-element.421), channel_id=1, source_target_pairs={{0,8},{8,16},{16,24},{24,28},{28,20},{20,12},{12,4},{4,0},{1,9},{9... | collective-permute-start | bytes 1228808 | tf_op jit(solution)/shard_map/ppermute | solution.py:67
  248.1 13.3 %collective-permute-start.80 = (bf16[200,768]{1,0:T(8,128)(2,1)S(1)}, bf16[200,768]{1,0:T(8,128)(2,1)S(1)}, u32[]{:S(2)}, u32[]{:S(2)}) collective-permute-start(bf16[200,768]{1,0:T(8,128)(2,1)S(1)} %get-tuple-element.465), channel_id=1, source_target_pairs={{0,4},{8,0},{16,8},{24,16},{28,24},{20,28},{12,20},{4,12},{1,5},{9... | collective-permute-start | bytes 921608 | tf_op jit(solution)/shard_map/ppermute | solution.py:67
  259.6 14.8 %collective-permute-start.67 = (bf16[128,1536]{1,0:T(8,128)(2,1)S(1)}, bf16[128,1536]{1,0:T(8,128)(2,1)S(1)}, u32[]{:S(2)}, u32[]{:S(2)}) collective-permute-start(bf16[128,1536]{1,0:T(8,128)(2,1)S(1)} %get-tuple-element.510), channel_id=1, source_target_pairs={{0,2},{1,3},{2,0},{3,1},{4,6},{5,7},{6,4},{7,5},{8,10},{9,11},{10,... | collective-permute-start | bytes 1179656 | tf_op jit(solution)/shard_map/ppermute | solution.py:70
  265.4 12.7 %collective-permute-start.81 = (bf16[200,768]{1,0:T(8,128)(2,1)S(1)}, bf16[200,768]{1,0:T(8,128)(2,1)S(1)}, u32[]{:S(2)}, u32[]{:S(2)}) collective-permute-start(bf16[200,768]{1,0:T(8,128)(2,1)S(1)} %get-tuple-element.470), channel_id=1, source_target_pairs={{0,8},{8,16},{16,24},{24,28},{28,20},{20,12},{12,4},{4,0},{1,9},{9... | collective-permute-start | bytes 921608 | tf_op jit(solution)/shard_map/ppermute | solution.py:67
  (47 other events, 557.1 us)

commit v2 on v1

--- a/solution.py
+++ b/solution.py
@@ -15,7 +15,7 @@
 MAX_RING = 8
 EXTRA = 8
 PADS = (8, 6, 4)
-RPADS = (8, 4, 8)
+RPADS = (6, 4, 6)
 CUTS = (2, 1)
 FREE = pl.CostEstimate(flops=0, transcendentals=0, bytes_accessed=0)
 
@@ -809,10 +809,10 @@
 ORDER = (
     "Pa", "I0", "Pm", "a1", "a2", "C0", "M0", "g1", "a3", "u1", "g2", "I1s0", "d1", "a4", "d2", "a5", "C1s0",
     "I1s1", "I1e", "QK", "u2", "R0s0", "g3", "R0s1", "u3", "R0e", "d3", "g4", "u4", "R2s0", "d4", "R2s1", "R2e",
-    "u5", "g5", "C1s1", "C1e", "d5", "ML", "rd1", "MB", "B0s0", "rd2", "O0s0", "rg1", "WU", "ru1", "B0e", "O0e",
-    "rd3", "ru2", "rg2", "rd4", "B2s0", "rg3", "B2e", "AB", "ru3", "WA", "rd5", "N0s0", "ra1", "rg4", "O2", "ra2",
-    "N0e", "rg5", "Xd0", "Xd1", "Xd2", "ra3", "Xd3", "ru4", "ra4", "ru5", "Xu0", "Xu1", "Xu2", "N2", "ra5", "Xa0",
-    "Xa1", "Xa2", "Xu3", "Xa3",
+    "u5", "g5", "C1s1", "C1e", "ML", "rd1", "d5", "MB", "B0s0", "rd2", "O0s0", "rg1", "WU", "O0e", "ru1", "B0e",
+    "rd3", "ru2", "rg2", "rd4", "B2s0", "rg3", "B2e", "AB", "WA", "ru3", "rd5", "N0s0", "ra1", "rg4", "O2", "ra2",
+    "N0e", "rg5", "Xd0", "Xd1", "Xd2", "ra3", "Xd3", "ru4", "ra4", "ru5", "Xu0", "Xu1", "N2", "ra5", "Xa0", "Xu2",
+    "Xa1", "Xu3", "Xa2", "Xa3",
 )
 
 
@@ -956,16 +956,16 @@
     else:
         @do("WU")
         def _():
-            have["up_blocks"] = lanes.pin(weight_grad(have["normed_mlp"], have["grad_pair"], count, ff, 2 * ff))
+            have["up_blocks"] = lanes.pin(weight_grad(have["normed_mlp"], lanes.pin(have["grad_pair"]), count, ff, 2 * ff))
 
         task(
             "rg", ["rg1", "rg2", "rg3", "rg4", "rg5"],
             lambda: scatter_ring(
-                lanes, weight_grad(have["normed_mlp"], have["grad_pair"], count, 0, ff), -1, chunk + RPADS[1]
+                lanes, weight_grad(have["normed_mlp"], lanes.pin(have["grad_pair"]), count, 0, ff), -1, chunk + RPADS[1]
             ),
         )
         task("ru", ["ru1", "ru2", "ru3", "ru4", "ru5"], lambda: scatter_ring(lanes, have["up_blocks"], 1, chunk + RPADS[2]))
-    task("out", [*core("O0", 1), "O2"], lambda: scatter_tokens(lanes, *back_through(have["hidden"], [have["d"][0]]), CUTS[1]))
+    task("out", [*core("O0", 1), "O2"], lambda: scatter_tokens(lanes, *back_through(lanes.pin(have["hidden"]), [have["d"][0]]), CUTS[1]))
 
     @do("AB")
     def _():

time: 287 us -> 284 us (0.990)
  waiting for transfers between devices: 143 us -> 140 us
    ppermute x33, waiting for transfers between devices: 18 us -> 13.9 us  [partner(): return lax.ppermute(value, 'tp', [(i, i ^ bit) for i in range(self.ways)])]
  transfers between devices with their start and end apart: 89 -> 89, of which waited for: 42 -> 48; matrix products, arithmetic and copies ran while one was open for 2% -> 2% of each run, Pallas kernels for 17% -> 17%
where the time goes in v2:
time: 284 us; the launch traced here: 283 us
  waiting for transfers between devices  140 us (49%)
  starting transfers between devices  82.1 us (29%)
  Pallas kernels  54.1 us (19%)
  local copies, waits for them, and re-layouts  4.19 us (1%)
    ppermute x56, waiting for transfers between devices, shift(): return lax.ppermute(value, RING, self.pairs[step])  126 us
    ppermute x56, starting transfers between devices, shift(): return lax.ppermute(value, RING, self.pairs[step])  57.7 us
    pallas_call x54, Pallas kernels, near(): pl.pallas_call(body, in_specs=[spec] * len(arrays), out_specs=[spec] * le...  51 us
    ppermute x33, starting transfers between devices, partner(): return lax.ppermute(value, 'tp', [(i, i ^ bit) for i in range(self.ways)])  24.3 us
    ppermute x33, waiting for transfers between devices, partner(): return lax.ppermute(value, 'tp', [(i, i ^ bit) for i in range(self.ways)])  13.9 us
  transfers between devices with their start and end apart: 89, of which 48 were waited for; matrix products, arithmetic and copies ran while one was open for 2% of the time, Pallas kernels for 17%

profile of v2, /device:TPU:0, one launch (start us, length us, event | category | flops | bytes accessed | tf_op | source)
XLA Modules:
  0.0 283.4 jit_solution(16737911257568780560)
XLA Ops:
  2.5 2.6 collective-permute-start.6
  7.9 2.1 collective-permute-done.5.refs_2_
  12.1 1.8 collective-permute-start.3
  14.3 4.6 %collective-permute-done.7.refs_1_ = bf16[200,768]{1,0:T(8,128)(2,1)S(1)} collective-permute-done((bf16[200,768]{1,0:T(8,128)(2,1)S(1)}, bf16[200,768]{1,0:T(8,128)(2,1)S(1)}, u32[]{:S(2)}, u32[]{:S(2)}) %collective-permute-start.7) | collective-permute-done | bytes 307232 | tf_op jit(solution)/shard_map/ppermute | solution.py:67
  22.4 5.5 %collective-permute-done.2.refs_2_ = bf16[48,3072]{1,0:T(8,128)(2,1)S(1)} collective-permute-done((bf16[48,3072]{1,0:T(8,128)(2,1)S(1)}, bf16[48,3072]{1,0:T(8,128)(2,1)S(1)}, u32[]{:S(2)}, u32[]{:S(2)}) %collective-permute-start.2) | collective-permute-done | bytes 294944 | tf_op jit(solution)/shard_map/ppermute | solution.py:70
  33.7 6.7 %collective-permute-done.10.refs_2_ = bf16[198,1024]{1,0:T(8,128)(2,1)} collective-permute-done((bf16[198,1024]{1,0:T(8,128)(2,1)S(1)}, bf16[198,1024]{1,0:T(8,128)(2,1)}, u32[]{:S(2)}, u32[]{:S(2)}) %collective-permute-start.10) | collective-permute-done | bytes 405536 | tf_op jit(solution)/shard_map/ppermute | solution.py:67
  44.2 4.4 %collective-permute-done.15.refs_5_ = bf16[200,768]{1,0:T(8,128)(2,1)S(1)} collective-permute-done((bf16[200,768]{1,0:T(8,128)(2,1)S(1)}, bf16[200,768]{1,0:T(8,128)(2,1)S(1)}, u32[]{:S(2)}, u32[]{:S(2)}) %collective-permute-start.15) | collective-permute-done | bytes 307232 | tf_op jit(solution)/shard_map/ppermute | solution.py:67
  51.2 3.2 %collective-permute-done.18.refs_2_ = bf16[200,1024]{1,0:T(8,128)(2,1)} collective-permute-done((bf16[200,1024]{1,0:T(8,128)(2,1)S(1)}, bf16[200,1024]{1,0:T(8,128)(2,1)}, u32[]{:S(2)}, u32[]{:S(2)}) %collective-permute-start.18) | collective-permute-done | bytes 409632 | tf_op jit(solution)/shard_map/ppermute | solution.py:67
  57.9 6.1 %collective-permute-done.17.refs_7_ = bf16[200,768]{1,0:T(8,128)(2,1)S(1)} collective-permute-done((bf16[200,768]{1,0:T(8,128)(2,1)S(1)}, bf16[200,768]{1,0:T(8,128)(2,1)S(1)}, u32[]{:S(2)}, u32[]{:S(2)}) %collective-permute-start.17) | collective-permute-done | bytes 307232 | tf_op jit(solution)/shard_map/ppermute | solution.py:67
  70.1 3.6 %shard_map.236 = (f32[512,192]{1,0:T(8,128)S(1)}, f32[256,1536]{1,0:T(8,128)S(1)}, bf16[256,1536]{1,0:T(8,128)(2,1)S(1)}) custom-call(bf16[512,192]{1,0:T(8,128)(2,1)S(1)} %get-tuple-element.311.q_ref, bf16[1,512,192]{2,1,0:T(8,128)(2,1)S(1)} %bitcast.18, bf16[1,512,192]{2,1,0:T(8,128)(2,1)S(1)} %bitcast.20, f32[3,512]{1,0:T(4,128)S(1)} %fusion.1.w_ref, ...), custom_call_target="tpu_custom_call" | custom-call | tf_op jit(solution)/shard_map/pallas_call | solution.py:338
  76.4 4.7 %collective-permute-done.24.refs_3_ = bf16[198,1024]{1,0:T(8,128)(2,1)S(1)} collective-permute-done((bf16[198,1024]{1,0:T(8,128)(2,1)}, bf16[198,1024]{1,0:T(8,128)(2,1)S(1)}, u32[]{:S(2)}, u32[]{:S(2)}) %collective-permute-start.24) | collective-permute-done | bytes 405536 | tf_op jit(solution)/shard_map/ppermute | solution.py:67
  83.2 3.5 %collective-permute-done.27.refs_4_ = bf16[196,1024]{1,0:T(8,128)(2,1)S(1)} collective-permute-done((bf16[196,1024]{1,0:T(8,128)(2,1)S(1)}, bf16[196,1024]{1,0:T(8,128)(2,1)S(1)}, u32[]{:S(2)}, u32[]{:S(2)}) %collective-permute-start.27) | collective-permute-done | bytes 401440 | tf_op jit(solution)/shard_map/ppermute | solution.py:67
  86.6 3.2 %collective-permute-done.28.refs_3_ = bf16[196,1024]{1,0:T(8,128)(2,1)S(1)} collective-permute-done((bf16[196,1024]{1,0:T(8,128)(2,1)S(1)}, bf16[196,1024]{1,0:T(8,128)(2,1)S(1)}, u32[]{:S(2)}, u32[]{:S(2)}) %collective-permute-start.28) | collective-permute-done | bytes 401440 | tf_op jit(solution)/shard_map/ppermute | solution.py:67
  93.6 1.8 collective-permute-done.34.refs_4_
  99.1 8.3 %collective-permute-done.32.refs_5_ = bf16[198,1024]{1,0:T(8,128)(2,1)S(1)} collective-permute-done((bf16[198,1024]{1,0:T(8,128)(2,1)S(1)}, bf16[198,1024]{1,0:T(8,128)(2,1)S(1)}, u32[]{:S(2)}, u32[]{:S(2)}) %collective-permute-start.32) | collective-permute-done | bytes 405536 | tf_op jit(solution)/shard_map/ppermute | solution.py:67
  109.4 3.9 %collective-permute-done.30.refs_6_ = bf16[196,1024]{1,0:T(8,128)(2,1)S(1)} collective-permute-done((bf16[196,1024]{1,0:T(8,128)(2,1)S(1)}, bf16[196,1024]{1,0:T(8,128)(2,1)S(1)}, u32[]{:S(2)}, u32[]{:S(2)}) %collective-permute-start.30) | collective-permute-done | bytes 401440 | tf_op jit(solution)/shard_map/ppermute | solution.py:67
  113.3 2.8 %collective-permute-done.31.refs_5_ = bf16[196,1024]{1,0:T(8,128)(2,1)S(1)} collective-permute-done((bf16[196,1024]{1,0:T(8,128)(2,1)S(1)}, bf16[196,1024]{1,0:T(8,128)(2,1)S(1)}, u32[]{:S(2)}, u32[]{:S(2)}) %collective-permute-start.31) | collective-permute-done | bytes 401440 | tf_op jit(solution)/shard_map/ppermute | solution.py:67
  118.6 3.0 %collective-permute-done.37.refs_6_ = bf16[200,1024]{1,0:T(8,128)(2,1)S(1)} collective-permute-done((bf16[200,1024]{1,0:T(8,128)(2,1)S(1)}, bf16[200,1024]{1,0:T(8,128)(2,1)S(1)}, u32[]{:S(2)}, u32[]{:S(2)}) %collective-permute-start.37) | collective-permute-done | bytes 409632 | tf_op jit(solution)/shard_map/ppermute | solution.py:67
  121.5 3.4 %collective-permute-done.38.refs_5_ = bf16[200,1024]{1,0:T(8,128)(2,1)S(1)} collective-permute-done((bf16[200,1024]{1,0:T(8,128)(2,1)S(1)}, bf16[200,1024]{1,0:T(8,128)(2,1)S(1)}, u32[]{:S(2)}, u32[]{:S(2)}) %collective-permute-start.38) | collective-permute-done | bytes 409632 | tf_op jit(solution)/shard_map/ppermute | solution.py:67
  127.5 2.2 collective-permute-done.41.refs_7_
  129.6 2.7 collective-permute-done.40.refs_7_
  135.6 4.7 %shard_map.242 = (bf16[512,1024]{1,0:T(8,128)(2,1)S(1)}, f32[512,2048]{1,0:T(8,128)S(1)}) custom-call(bf16[512,1536]{1,0:T(8,128)(2,1)S(1)} %get-tuple-element.341.x_ref.left_ref, bf16[1536,1024]{1,0:T(8,128)(2,1)S(1)} %shard_map.240.gate_ref.refs_0_, bf16[1536,1024]{1,0:T(8,128)(2,1)S(1)} %shard_map.241.up_ref.refs_1_), custom_call_target="tpu_custom_call" | custom-call | tf_op jit(solution)/shard_map/pallas_call | solution.py:338
  141.5 2.1 shard_map.243.blocks_ref
  145.6 2.2 shard_map.246.left_ref.right_ref
  147.9 4.7 %shard_map.247 = (f32[256,1536]{1,0:T(8,128)S(1)}, bf16[256,1536]{1,0:T(8,128)(2,1)S(1)}) custom-call(bf16[512,2048]{1,0:T(8,128)(2,1)S(1)} %shard_map.246.left_ref.right_ref, bf16[1536,1024]{1,0:T(8,128)(2,1)S(1)} %shard_map.240.gate_ref.refs_0_, bf16[1536,1024]{1,0:T(8,128)(2,1)S(1)} %shard_map.241.up_ref.refs_1_), custom_call_target="tpu_custom_call" | custom-call | tf_op jit(solution)/shard_map/pallas_call | solution.py:338
  152.6 2.7 collective-permute-done.44.refs_0_
  155.3 2.5 shard_map.249
  160.5 2.0 shard_map.250.blocks_ref
  162.6 2.0 shard_map.252.blocks_ref
  168.6 2.1 collective-permute-done.50.refs_0_
  173.6 6.0 %collective-permute-done.49.refs_0_ = bf16[198,1024]{1,0:T(8,128)(2,1)S(1)} collective-permute-done((bf16[198,1024]{1,0:T(8,128)(2,1)S(1)}, bf16[198,1024]{1,0:T(8,128)(2,1)S(1)}, u32[]{:S(2)}, u32[]{:S(2)}) %collective-permute-start.49) | collective-permute-done | bytes 405536 | tf_op jit(solution)/shard_map/ppermute | solution.py:67
  182.3 6.1 %collective-permute-done.56.refs_0_ = bf16[198,1024]{1,0:T(8,128)(2,1)S(1)} collective-permute-done((bf16[198,1024]{1,0:T(8,128)(2,1)S(1)}, bf16[198,1024]{1,0:T(8,128)(2,1)S(1)}, u32[]{:S(2)}, u32[]{:S(2)}) %collective-permute-start.56) | collective-permute-done | bytes 405536 | tf_op jit(solution)/shard_map/ppermute | solution.py:67
  191.4 5.7 %collective-permute-done.53.refs_0_ = bf16[196,1024]{1,0:T(8,128)(2,1)S(1)} collective-permute-done((bf16[196,1024]{1,0:T(8,128)(2,1)S(1)}, bf16[196,1024]{1,0:T(8,128)(2,1)S(1)}, u32[]{:S(2)}, u32[]{:S(2)}) %collective-permute-start.53) | collective-permute-done | bytes 401440 | tf_op jit(solution)/shard_map/ppermute | solution.py:67
  200.3 2.1 shard_map.262
  202.4 5.8 %shard_map.263 = (bf16[512,192]{1,0:T(8,128)(2,1)S(1)}, bf16[1,512,192]{2,1,0:T(8,128)(2,1)S(1)}, bf16[1,512,192]{2,1,0:T(8,128)(2,1)S(1)}, f32[1,768]{1,0:T(1,128)S(1)}) custom-call(bf16[512,192]{1,0:T(8,128)(2,1)S(1)} %get-tuple-element.311.q_ref, bf16[1,512,192]{2,1,0:T(8,128)(2,1)S(1)} %bitcast.19, bf16[1,512,192]{2,1,0:T(8,128)(2,1)S(1)} %bitcast.21, ...), custom_call_target="tpu_custom_call" | custom-call | tf_op jit(solution)/shard_map/pallas_call | solution.py:338
  208.1 3.9 %shard_map.264 = (bf16[8,200,768]{2,1,0:T(8,128)(2,1)S(1)}, f32[256,1536]{1,0:T(8,128)S(1)}, bf16[256,1536]{1,0:T(8,128)(2,1)S(1)}) custom-call(bf16[512,1536]{1,0:T(8,128)(2,1)S(1)} %get-tuple-element.407.n_ref, bf16[512,1536]{1,0:T(8,128)(2,1)S(1)} %constant_dynamic-update-slice_fusion.x_ref, f32[512,128]{1,0:T(8,128)S(1)} %get-tuple-element.408.rsq_ref, ...), custom_call_target="tpu_custom_call" | custom-call | tf_op jit(solution)/shard_map/pallas_call | solution.py:338
  218.4 4.1 %collective-permute-done.58.refs_0_ = bf16[196,1024]{1,0:T(8,128)(2,1)S(1)} collective-permute-done((bf16[196,1024]{1,0:T(8,128)(2,1)S(1)}, bf16[196,1024]{1,0:T(8,128)(2,1)S(1)}, u32[]{:S(2)}, u32[]{:S(2)}) %collective-permute-start.58) | collective-permute-done | bytes 401440 | tf_op jit(solution)/shard_map/ppermute | solution.py:67
  222.6 2.0 collective-permute-done.59.refs_1_
  226.8 4.3 %collective-permute-done.66.refs_0_ = bf16[200,768]{1,0:T(8,128)(2,1)S(1)} collective-permute-done((bf16[200,768]{1,0:T(8,128)(2,1)S(1)}, bf16[200,768]{1,0:T(8,128)(2,1)S(1)}, u32[]{:S(2)}, u32[]{:S(2)}) %collective-permute-start.66) | collective-permute-done | bytes 307232 | tf_op jit(solution)/shard_map/ppermute | solution.py:67
  233.3 3.1 %collective-permute-done.70.refs_0_ = bf16[196,1024]{1,0:T(8,128)(2,1)S(1)} collective-permute-done((bf16[196,1024]{1,0:T(8,128)(2,1)S(1)}, bf16[196,1024]{1,0:T(8,128)(2,1)S(1)}, u32[]{:S(2)}, u32[]{:S(2)}) %collective-permute-start.70) | collective-permute-done | bytes 401440 | tf_op jit(solution)/shard_map/ppermute | solution.py:67
  240.2 2.8 collective-permute-done.75.refs_0_
  243.0 3.5 %collective-permute-done.76.refs_1_ = bf16[200,768]{1,0:T(8,128)(2,1)S(1)} collective-permute-done((bf16[200,768]{1,0:T(8,128)(2,1)S(1)}, bf16[200,768]{1,0:T(8,128)(2,1)S(1)}, u32[]{:S(2)}, u32[]{:S(2)}) %collective-permute-start.76) | collective-permute-done | bytes 307232 | tf_op jit(solution)/shard_map/ppermute | solution.py:67
  251.7 2.7 collective-permute-done.73.refs_2_
  256.8 2.4 collective-permute-start.67
  262.7 4.3 %collective-permute-done.77.refs_0_ = bf16[198,1024]{1,0:T(8,128)(2,1)S(1)} collective-permute-done((bf16[198,1024]{1,0:T(8,128)(2,1)S(1)}, bf16[198,1024]{1,0:T(8,128)(2,1)S(1)}, u32[]{:S(2)}, u32[]{:S(2)}) %collective-permute-start.77) | collective-permute-done | bytes 405536 | tf_op jit(solution)/shard_map/ppermute | solution.py:67
  267.0 2.2 collective-permute-done.78.refs_1_
  269.4 3.0 %collective-permute-start.84 = (bf16[48,1024]{1,0:T(8,128)(2,1)S(1)}, bf16[48,1024]{1,0:T(8,128)(2,1)S(1)}, u32[]{:S(2)}, u32[]{:S(2)}) collective-permute-start(bf16[48,1024]{1,0:T(8,128)(2,1)S(1)} %get-tuple-element.481), channel_id=1, source_target_pairs={{0,2},{1,3},{2,0},{3,1},{4,6},{5,7},{6,4},{7,5},{8,10},{9,11},{10,... | collective-permute-start | bytes 294920 | tf_op jit(solution)/shard_map/ppermute | solution.py:70
  272.7 2.7 collective-permute-done.82.refs_1_
  (215 shorter events, 110.3 us)
Async XLA Ops:
  13.9 13.9 %collective-permute-start.2 = (bf16[48,3072]{1,0:T(8,128)(2,1)S(1)}, bf16[48,3072]{1,0:T(8,128)(2,1)S(1)}, u32[]{:S(2)}, u32[]{:S(2)}) collective-permute-start(bf16[48,3072]{1,0:T(8,128)(2,1)S(1)} %get-tuple-element.274), channel_id=1, source_target_pairs={{0,2},{1,3},{2,0},{3,1},{4,6},{5,7},{6,4},{7,5},{8,10},{9,11},{10,... | collective-permute-start | bytes 884744 | tf_op jit(solution)/shard_map/ppermute | solution.py:70
  27.9 12.5 %collective-permute-start.10 = (bf16[198,1024]{1,0:T(8,128)(2,1)S(1)}, bf16[198,1024]{1,0:T(8,128)(2,1)}, u32[]{:S(2)}, u32[]{:S(2)}) collective-permute-start(bf16[198,1024]{1,0:T(8,128)(2,1)S(1)} %get-tuple-element.288.refs_0_), channel_id=1, source_target_pairs={{0,4},{8,0},{16,8},{24,16},{28,24},{20,28},{12,20},{4,12},{1,5},{9... | collective-permute-start | bytes 1216520 | tf_op jit(solution)/shard_map/ppermute | solution.py:67
  29.6 12.5 %collective-permute-start.9 = (bf16[198,1024]{1,0:T(8,128)(2,1)S(1)}, bf16[198,1024]{1,0:T(8,128)(2,1)}, u32[]{:S(2)}, u32[]{:S(2)}) collective-permute-start(bf16[198,1024]{1,0:T(8,128)(2,1)S(1)} %get-tuple-element.288.refs_0_), channel_id=1, source_target_pairs={{0,8},{8,16},{16,24},{24,28},{28,20},{20,12},{12,4},{4,0},{1,9},{9... | collective-permute-start | bytes 1216520 | tf_op jit(solution)/shard_map/ppermute | solution.py:67
  31.7 17.0 %collective-permute-start.15 = (bf16[200,768]{1,0:T(8,128)(2,1)S(1)}, bf16[200,768]{1,0:T(8,128)(2,1)S(1)}, u32[]{:S(2)}, u32[]{:S(2)}) collective-permute-start(bf16[200,768]{1,0:T(8,128)(2,1)S(1)} %collective-permute-done.11.refs_3_), channel_id=1, source_target_pairs={{0,8},{8,16},{16,24},{24,28},{28,20},{20,12},{12,4},{4,0},{1,9},{9... | collective-permute-start | bytes 921608 | tf_op jit(solution)/shard_map/ppermute | solution.py:67
  33.3 15.4 %collective-permute-start.16 = (bf16[200,768]{1,0:T(8,128)(2,1)S(1)}, bf16[200,768]{1,0:T(8,128)(2,1)S(1)}, u32[]{:S(2)}, u32[]{:S(2)}) collective-permute-start(bf16[200,768]{1,0:T(8,128)(2,1)S(1)} %collective-permute-done.12.refs_4_), channel_id=1, source_target_pairs={{0,4},{8,0},{16,8},{24,16},{28,24},{20,28},{12,20},{4,12},{1,5},{9... | collective-permute-start | bytes 921608 | tf_op jit(solution)/shard_map/ppermute | solution.py:67
  40.5 23.9 %collective-permute-start.14 = (bf16[128,1536]{1,0:T(8,128)(2,1)}, bf16[128,1536]{1,0:T(8,128)(2,1)}, u32[]{:S(2)}, u32[]{:S(2)}) collective-permute-start(bf16[128,1536]{1,0:T(8,128)(2,1)} %bitcast.26), channel_id=1, source_target_pairs={{0,2},{1,3},{2,0},{3,1},{4,6},{5,7},{6,4},{7,5},{8,10},{9,11},{10,... | collective-permute-start | bytes 1179656 | tf_op jit(solution)/shard_map/ppermute | solution.py:70
  43.7 13.8 %collective-permute-start.19 = (bf16[200,1024]{1,0:T(8,128)(2,1)S(1)}, bf16[200,1024]{1,0:T(8,128)(2,1)}, u32[]{:S(2)}, u32[]{:S(2)}) collective-permute-start(bf16[200,1024]{1,0:T(8,128)(2,1)S(1)} %get-tuple-element.298.refs_0_), channel_id=1, source_target_pairs={{0,8},{8,16},{16,24},{24,28},{28,20},{20,12},{12,4},{4,0},{1,9},{9... | collective-permute-start | bytes 1228808 | tf_op jit(solution)/shard_map/ppermute | solution.py:67
  48.6 17.4 %collective-permute-start.13 = (bf16[128,1536]{1,0:T(8,128)(2,1)}, bf16[128,1536]{1,0:T(8,128)(2,1)}, u32[]{:S(2)}, u32[]{:S(2)}) collective-permute-start(bf16[128,1536]{1,0:T(8,128)(2,1)} %bitcast), channel_id=1, source_target_pairs={{0,1},{1,0},{2,3},{3,2},{4,5},{5,4},{6,7},{7,6},{8,9},{9,8},{10,11... | collective-permute-start | bytes 1179656 | tf_op jit(solution)/shard_map/ppermute | solution.py:70
  48.6 15.4 %collective-permute-start.17 = (bf16[200,768]{1,0:T(8,128)(2,1)S(1)}, bf16[200,768]{1,0:T(8,128)(2,1)S(1)}, u32[]{:S(2)}, u32[]{:S(2)}) collective-permute-start(bf16[200,768]{1,0:T(8,128)(2,1)S(1)} %collective-permute-done.15.refs_5_), channel_id=1, source_target_pairs={{0,8},{8,16},{16,24},{24,28},{28,20},{20,12},{12,4},{4,0},{1,9},{9... | collective-permute-start | bytes 921608 | tf_op jit(solution)/shard_map/ppermute | solution.py:67
  54.4 19.4 %collective-permute-start.21 = (bf16[196,1024]{1,0:T(8,128)(2,1)}, bf16[196,1024]{1,0:T(8,128)(2,1)S(1)}, u32[]{:S(2)}, u32[]{:S(2)}) collective-permute-start(bf16[196,1024]{1,0:T(8,128)(2,1)} %copy-done.2), channel_id=1, source_target_pairs={{0,4},{8,0},{16,8},{24,16},{28,24},{20,28},{12,20},{4,12},{1,5},{9... | collective-permute-start | bytes 1204232 | tf_op jit(solution)/shard_map/ppermute | solution.py:67
  57.5 16.2 %collective-permute-start.22 = (bf16[196,1024]{1,0:T(8,128)(2,1)}, bf16[196,1024]{1,0:T(8,128)(2,1)S(1)}, u32[]{:S(2)}, u32[]{:S(2)}) collective-permute-start(bf16[196,1024]{1,0:T(8,128)(2,1)} %copy-done.2), channel_id=1, source_target_pairs={{0,8},{8,16},{16,24},{24,28},{28,20},{20,12},{12,4},{4,0},{1,9},{9... | collective-permute-start | bytes 1204232 | tf_op jit(solution)/shard_map/ppermute | solution.py:67
  64.0 17.1 %collective-permute-start.24 = (bf16[198,1024]{1,0:T(8,128)(2,1)}, bf16[198,1024]{1,0:T(8,128)(2,1)S(1)}, u32[]{:S(2)}, u32[]{:S(2)}) collective-permute-start(bf16[198,1024]{1,0:T(8,128)(2,1)} %collective-permute-done.9.refs_1_), channel_id=1, source_target_pairs={{0,8},{8,16},{16,24},{24,28},{28,20},{20,12},{12,4},{4,0},{1,9},{9... | collective-permute-start | bytes 1216520 | tf_op jit(solution)/shard_map/ppermute | solution.py:67
  64.4 16.7 %collective-permute-start.25 = (bf16[198,1024]{1,0:T(8,128)(2,1)}, bf16[198,1024]{1,0:T(8,128)(2,1)S(1)}, u32[]{:S(2)}, u32[]{:S(2)}) collective-permute-start(bf16[198,1024]{1,0:T(8,128)(2,1)} %collective-permute-done.10.refs_2_), channel_id=1, source_target_pairs={{0,4},{8,0},{16,8},{24,16},{28,24},{20,28},{12,20},{4,12},{1,5},{9... | collective-permute-start | bytes 1216520 | tf_op jit(solution)/shard_map/ppermute | solution.py:67
  75.9 13.9 %collective-permute-start.28 = (bf16[196,1024]{1,0:T(8,128)(2,1)S(1)}, bf16[196,1024]{1,0:T(8,128)(2,1)S(1)}, u32[]{:S(2)}, u32[]{:S(2)}) collective-permute-start(bf16[196,1024]{1,0:T(8,128)(2,1)S(1)} %collective-permute-done.22.refs_1_), channel_id=1, source_target_pairs={{0,8},{8,16},{16,24},{24,28},{28,20},{20,12},{12,4},{4,0},{1,9},{9... | collective-permute-start | bytes 1204232 | tf_op jit(solution)/shard_map/ppermute | solution.py:67
  81.1 14.3 %collective-permute-start.34 = (bf16[200,1024]{1,0:T(8,128)(2,1)}, bf16[200,1024]{1,0:T(8,128)(2,1)S(1)}, u32[]{:S(2)}, u32[]{:S(2)}) collective-permute-start(bf16[200,1024]{1,0:T(8,128)(2,1)} %collective-permute-done.18.refs_2_), channel_id=1, source_target_pairs={{0,4},{8,0},{16,8},{24,16},{28,24},{20,28},{12,20},{4,12},{1,5},{9... | collective-permute-start | bytes 1228808 | tf_op jit(solution)/shard_map/ppermute | solution.py:67
  82.7 15.9 %collective-permute-start.35 = (bf16[200,1024]{1,0:T(8,128)(2,1)}, bf16[200,1024]{1,0:T(8,128)(2,1)S(1)}, u32[]{:S(2)}, u32[]{:S(2)}) collective-permute-start(bf16[200,1024]{1,0:T(8,128)(2,1)} %collective-permute-done.19.refs_1_), channel_id=1, source_target_pairs={{0,8},{8,16},{16,24},{24,28},{28,20},{20,12},{12,4},{4,0},{1,9},{9... | collective-permute-start | bytes 1228808 | tf_op jit(solution)/shard_map/ppermute | solution.py:67
  90.0 26.1 %collective-permute-start.29 = (bf16[256,1536]{1,0:T(8,128)(2,1)S(1)}, bf16[256,1536]{1,0:T(8,128)(2,1)S(1)}, u32[]{:S(2)}, u32[]{:S(2)}) collective-permute-start(bf16[256,1536]{1,0:T(8,128)(2,1)S(1)} %shard_map.237.left_ref), channel_id=1, source_target_pairs={{0,2},{1,3},{2,0},{3,1},{4,6},{5,7},{6,4},{7,5},{8,10},{9,11},{10,... | collective-permute-start | bytes 2359304 | tf_op jit(solution)/shard_map/ppermute | solution.py:70
  91.6 15.8 %collective-permute-start.32 = (bf16[198,1024]{1,0:T(8,128)(2,1)S(1)}, bf16[198,1024]{1,0:T(8,128)(2,1)S(1)}, u32[]{:S(2)}, u32[]{:S(2)}) collective-permute-start(bf16[198,1024]{1,0:T(8,128)(2,1)S(1)} %collective-permute-done.24.refs_3_), channel_id=1, source_target_pairs={{0,8},{8,16},{16,24},{24,28},{28,20},{20,12},{12,4},{4,0},{1,9},{9... | collective-permute-start | bytes 1216520 | tf_op jit(solution)/shard_map/ppermute | solution.py:67
  92.1 16.8 %collective-permute-start.33 = (bf16[198,1024]{1,0:T(8,128)(2,1)S(1)}, bf16[198,1024]{1,0:T(8,128)(2,1)S(1)}, u32[]{:S(2)}, u32[]{:S(2)}) collective-permute-start(bf16[198,1024]{1,0:T(8,128)(2,1)S(1)} %collective-permute-done.25.refs_4_), channel_id=1, source_target_pairs={{0,4},{8,0},{16,8},{24,16},{28,24},{20,28},{12,20},{4,12},{1,5},{9... | collective-permute-start | bytes 1216520 | tf_op jit(solution)/shard_map/ppermute | solution.py:67
  95.4 17.9 %collective-permute-start.30 = (bf16[196,1024]{1,0:T(8,128)(2,1)S(1)}, bf16[196,1024]{1,0:T(8,128)(2,1)S(1)}, u32[]{:S(2)}, u32[]{:S(2)}) collective-permute-start(bf16[196,1024]{1,0:T(8,128)(2,1)S(1)} %collective-permute-done.27.refs_4_), channel_id=1, source_target_pairs={{0,4},{8,0},{16,8},{24,16},{28,24},{20,28},{12,20},{4,12},{1,5},{9... | collective-permute-start | bytes 1204232 | tf_op jit(solution)/shard_map/ppermute | solution.py:67
  98.6 17.6 %collective-permute-start.31 = (bf16[196,1024]{1,0:T(8,128)(2,1)S(1)}, bf16[196,1024]{1,0:T(8,128)(2,1)S(1)}, u32[]{:S(2)}, u32[]{:S(2)}) collective-permute-start(bf16[196,1024]{1,0:T(8,128)(2,1)S(1)} %collective-permute-done.28.refs_3_), channel_id=1, source_target_pairs={{0,8},{8,16},{16,24},{24,28},{28,20},{20,12},{12,4},{4,0},{1,9},{9... | collective-permute-start | bytes 1204232 | tf_op jit(solution)/shard_map/ppermute | solution.py:67
  107.4 14.2 %collective-permute-start.37 = (bf16[200,1024]{1,0:T(8,128)(2,1)S(1)}, bf16[200,1024]{1,0:T(8,128)(2,1)S(1)}, u32[]{:S(2)}, u32[]{:S(2)}) collective-permute-start(bf16[200,1024]{1,0:T(8,128)(2,1)S(1)} %collective-permute-done.34.refs_4_), channel_id=1, source_target_pairs={{0,4},{8,0},{16,8},{24,16},{28,24},{20,28},{12,20},{4,12},{1,5},{9... | collective-permute-start | bytes 1228808 | tf_op jit(solution)/shard_map/ppermute | solution.py:67
  109.0 16.0 %collective-permute-start.38 = (bf16[200,1024]{1,0:T(8,128)(2,1)S(1)}, bf16[200,1024]{1,0:T(8,128)(2,1)S(1)}, u32[]{:S(2)}, u32[]{:S(2)}) collective-permute-start(bf16[200,1024]{1,0:T(8,128)(2,1)S(1)} %collective-permute-done.35.refs_3_), channel_id=1, source_target_pairs={{0,8},{8,16},{16,24},{24,28},{28,20},{20,12},{12,4},{4,0},{1,9},{9... | collective-permute-start | bytes 1228808 | tf_op jit(solution)/shard_map/ppermute | solution.py:67
  116.5 15.9 %collective-permute-start.40 = (bf16[198,1024]{1,0:T(8,128)(2,1)S(1)}, bf16[198,1024]{1,0:T(8,128)(2,1)S(1)}, u32[]{:S(2)}, u32[]{:S(2)}) collective-permute-start(bf16[198,1024]{1,0:T(8,128)(2,1)S(1)} %collective-permute-done.32.refs_5_), channel_id=1, source_target_pairs={{0,8},{8,16},{16,24},{24,28},{28,20},{20,12},{12,4},{4,0},{1,9},{9... | collective-permute-start | bytes 1216520 | tf_op jit(solution)/shard_map/ppermute | solution.py:67
  117.0 12.6 %collective-permute-start.41 = (bf16[196,1024]{1,0:T(8,128)(2,1)S(1)}, bf16[196,1024]{1,0:T(8,128)(2,1)S(1)}, u32[]{:S(2)}, u32[]{:S(2)}) collective-permute-start(bf16[196,1024]{1,0:T(8,128)(2,1)S(1)} %collective-permute-done.30.refs_6_), channel_id=1, source_target_pairs={{0,4},{8,0},{16,8},{24,16},{28,24},{20,28},{12,20},{4,12},{1,5},{9... | collective-permute-start | bytes 1204232 | tf_op jit(solution)/shard_map/ppermute | solution.py:67
  165.0 24.0 %collective-permute-start.55 = (bf16[256,1536]{1,0:T(8,128)(2,1)S(1)}, bf16[256,1536]{1,0:T(8,128)(2,1)S(1)}, u32[]{:S(2)}, u32[]{:S(2)}) collective-permute-start(bf16[256,1536]{1,0:T(8,128)(2,1)S(1)} %shard_map.255.left_ref), channel_id=1, source_target_pairs={{0,2},{1,3},{2,0},{3,1},{4,6},{5,7},{6,4},{7,5},{8,10},{9,11},{10,... | collective-permute-start | bytes 2359304 | tf_op jit(solution)/shard_map/ppermute | solution.py:70
  166.6 13.0 %collective-permute-start.49 = (bf16[198,1024]{1,0:T(8,128)(2,1)S(1)}, bf16[198,1024]{1,0:T(8,128)(2,1)S(1)}, u32[]{:S(2)}, u32[]{:S(2)}) collective-permute-start(bf16[198,1024]{1,0:T(8,128)(2,1)S(1)} %shard_map.254), channel_id=1, source_target_pairs={{0,8},{8,16},{16,24},{24,28},{28,20},{20,12},{12,4},{4,0},{1,9},{9... | collective-permute-start | bytes 1216520 | tf_op jit(solution)/shard_map/ppermute | solution.py:67
  167.0 13.0 %collective-permute-start.48 = (bf16[196,1024]{1,0:T(8,128)(2,1)S(1)}, bf16[196,1024]{1,0:T(8,128)(2,1)S(1)}, u32[]{:S(2)}, u32[]{:S(2)}) collective-permute-start(bf16[196,1024]{1,0:T(8,128)(2,1)S(1)} %shard_map.251), channel_id=1, source_target_pairs={{0,4},{8,0},{16,8},{24,16},{28,24},{20,28},{12,20},{4,12},{1,5},{9... | collective-permute-start | bytes 1204232 | tf_op jit(solution)/shard_map/ppermute | solution.py:67
  171.5 16.9 %collective-permute-start.56 = (bf16[198,1024]{1,0:T(8,128)(2,1)S(1)}, bf16[198,1024]{1,0:T(8,128)(2,1)S(1)}, u32[]{:S(2)}, u32[]{:S(2)}) collective-permute-start(bf16[198,1024]{1,0:T(8,128)(2,1)S(1)} %get-tuple-element.382), channel_id=1, source_target_pairs={{0,8},{8,16},{16,24},{24,28},{28,20},{20,12},{12,4},{4,0},{1,9},{9... | collective-permute-start | bytes 1216520 | tf_op jit(solution)/shard_map/ppermute | solution.py:67
  172.0 16.8 %collective-permute-start.57 = (bf16[198,1024]{1,0:T(8,128)(2,1)S(1)}, bf16[198,1024]{1,0:T(8,128)(2,1)S(1)}, u32[]{:S(2)}, u32[]{:S(2)}) collective-permute-start(bf16[198,1024]{1,0:T(8,128)(2,1)S(1)} %get-tuple-element.392), channel_id=1, source_target_pairs={{0,4},{8,0},{16,8},{24,16},{28,24},{20,28},{12,20},{4,12},{1,5},{9... | collective-permute-start | bytes 1216520 | tf_op jit(solution)/shard_map/ppermute | solution.py:67
  180.2 16.9 %collective-permute-start.53 = (bf16[196,1024]{1,0:T(8,128)(2,1)S(1)}, bf16[196,1024]{1,0:T(8,128)(2,1)S(1)}, u32[]{:S(2)}, u32[]{:S(2)}) collective-permute-start(bf16[196,1024]{1,0:T(8,128)(2,1)S(1)} %get-tuple-element.390), channel_id=1, source_target_pairs={{0,8},{8,16},{16,24},{24,28},{28,20},{20,12},{12,4},{4,0},{1,9},{9... | collective-permute-start | bytes 1204232 | tf_op jit(solution)/shard_map/ppermute | solution.py:67
  180.7 16.9 %collective-permute-start.54 = (bf16[196,1024]{1,0:T(8,128)(2,1)S(1)}, bf16[196,1024]{1,0:T(8,128)(2,1)S(1)}, u32[]{:S(2)}, u32[]{:S(2)}) collective-permute-start(bf16[196,1024]{1,0:T(8,128)(2,1)S(1)} %get-tuple-element.391), channel_id=1, source_target_pairs={{0,4},{8,0},{16,8},{24,16},{28,24},{20,28},{12,20},{4,12},{1,5},{9... | collective-permute-start | bytes 1204232 | tf_op jit(solution)/shard_map/ppermute | solution.py:67
  189.3 22.8 %collective-permute-start.63 = (bf16[198,1024]{1,0:T(8,128)(2,1)S(1)}, bf16[198,1024]{1,0:T(8,128)(2,1)S(1)}, u32[]{:S(2)}, u32[]{:S(2)}) collective-permute-start(bf16[198,1024]{1,0:T(8,128)(2,1)S(1)} %get-tuple-element.386), channel_id=1, source_target_pairs={{0,8},{8,16},{16,24},{24,28},{28,20},{20,12},{12,4},{4,0},{1,9},{9... | collective-permute-start | bytes 1216520 | tf_op jit(solution)/shard_map/ppermute | solution.py:67
  189.8 23.9 %collective-permute-start.64 = (bf16[198,1024]{1,0:T(8,128)(2,1)S(1)}, bf16[198,1024]{1,0:T(8,128)(2,1)S(1)}, u32[]{:S(2)}, u32[]{:S(2)}) collective-permute-start(bf16[198,1024]{1,0:T(8,128)(2,1)S(1)} %get-tuple-element.425), channel_id=1, source_target_pairs={{0,4},{8,0},{16,8},{24,16},{28,24},{20,28},{12,20},{4,12},{1,5},{9... | collective-permute-start | bytes 1216520 | tf_op jit(solution)/shard_map/ppermute | solution.py:67
  197.1 17.6 %collective-permute-start.61 = (bf16[198,1024]{1,0:T(8,128)(2,1)S(1)}, bf16[198,1024]{1,0:T(8,128)(2,1)S(1)}, u32[]{:S(2)}, u32[]{:S(2)}) collective-permute-start(bf16[198,1024]{1,0:T(8,128)(2,1)S(1)} %get-tuple-element.397), channel_id=1, source_target_pairs={{0,8},{8,16},{16,24},{24,28},{28,20},{20,12},{12,4},{4,0},{1,9},{9... | collective-permute-start | bytes 1216520 | tf_op jit(solution)/shard_map/ppermute | solution.py:67
  197.6 17.6 %collective-permute-start.62 = (bf16[198,1024]{1,0:T(8,128)(2,1)S(1)}, bf16[198,1024]{1,0:T(8,128)(2,1)S(1)}, u32[]{:S(2)}, u32[]{:S(2)}) collective-permute-start(bf16[198,1024]{1,0:T(8,128)(2,1)S(1)} %get-tuple-element.424), channel_id=1, source_target_pairs={{0,4},{8,0},{16,8},{24,16},{28,24},{20,28},{12,20},{4,12},{1,5},{9... | collective-permute-start | bytes 1216520 | tf_op jit(solution)/shard_map/ppermute | solution.py:67
  199.5 23.0 %collective-permute-start.58 = (bf16[196,1024]{1,0:T(8,128)(2,1)S(1)}, bf16[196,1024]{1,0:T(8,128)(2,1)S(1)}, u32[]{:S(2)}, u32[]{:S(2)}) collective-permute-start(bf16[196,1024]{1,0:T(8,128)(2,1)S(1)} %get-tuple-element.405), channel_id=1, source_target_pairs={{0,8},{8,16},{16,24},{24,28},{28,20},{20,12},{12,4},{4,0},{1,9},{9... | collective-permute-start | bytes 1204232 | tf_op jit(solution)/shard_map/ppermute | solution.py:67
  212.1 12.5 %collective-permute-start.59 = (bf16[196,1024]{1,0:T(8,128)(2,1)S(1)}, bf16[196,1024]{1,0:T(8,128)(2,1)S(1)}, u32[]{:S(2)}, u32[]{:S(2)}) collective-permute-start(bf16[196,1024]{1,0:T(8,128)(2,1)S(1)} %get-tuple-element.406), channel_id=1, source_target_pairs={{0,4},{8,0},{16,8},{24,16},{28,24},{20,28},{12,20},{4,12},{1,5},{9... | collective-permute-start | bytes 1204232 | tf_op jit(solution)/shard_map/ppermute | solution.py:67
  215.2 21.7 %collective-permute-start.65 = (bf16[256,1536]{1,0:T(8,128)(2,1)S(1)}, bf16[256,1536]{1,0:T(8,128)(2,1)S(1)}, u32[]{:S(2)}, u32[]{:S(2)}) collective-permute-start(bf16[256,1536]{1,0:T(8,128)(2,1)S(1)} %get-tuple-element.432), channel_id=1, source_target_pairs={{0,1},{1,0},{2,3},{3,2},{4,5},{5,4},{6,7},{7,6},{8,9},{9,8},{10,11... | collective-permute-start | bytes 2359304 | tf_op jit(solution)/shard_map/ppermute | solution.py:70
  216.8 14.3 %collective-permute-start.66 = (bf16[200,768]{1,0:T(8,128)(2,1)S(1)}, bf16[200,768]{1,0:T(8,128)(2,1)S(1)}, u32[]{:S(2)}, u32[]{:S(2)}) collective-permute-start(bf16[200,768]{1,0:T(8,128)(2,1)S(1)} %shard_map.265), channel_id=1, source_target_pairs={{0,4},{8,0},{16,8},{24,16},{28,24},{20,28},{12,20},{4,12},{1,5},{9... | collective-permute-start | bytes 921608 | tf_op jit(solution)/shard_map/ppermute | solution.py:67
  225.3 14.6 %collective-permute-start.71 = (bf16[196,1024]{1,0:T(8,128)(2,1)S(1)}, bf16[196,1024]{1,0:T(8,128)(2,1)S(1)}, u32[]{:S(2)}, u32[]{:S(2)}) collective-permute-start(bf16[196,1024]{1,0:T(8,128)(2,1)S(1)} %get-tuple-element.449), channel_id=1, source_target_pairs={{0,4},{8,0},{16,8},{24,16},{28,24},{20,28},{12,20},{4,12},{1,5},{9... | collective-permute-start | bytes 1204232 | tf_op jit(solution)/shard_map/ppermute | solution.py:67
  231.8 14.7 %collective-permute-start.76 = (bf16[200,768]{1,0:T(8,128)(2,1)S(1)}, bf16[200,768]{1,0:T(8,128)(2,1)S(1)}, u32[]{:S(2)}, u32[]{:S(2)}) collective-permute-start(bf16[200,768]{1,0:T(8,128)(2,1)S(1)} %get-tuple-element.458), channel_id=1, source_target_pairs={{0,4},{8,0},{16,8},{24,16},{28,24},{20,28},{12,20},{4,12},{1,5},{9... | collective-permute-start | bytes 921608 | tf_op jit(solution)/shard_map/ppermute | solution.py:67
  236.4 18.0 %collective-permute-start.68 = (bf16[198,1024]{1,0:T(8,128)(2,1)S(1)}, bf16[198,1024]{1,0:T(8,128)(2,1)S(1)}, u32[]{:S(2)}, u32[]{:S(2)}) collective-permute-start(bf16[198,1024]{1,0:T(8,128)(2,1)S(1)} %get-tuple-element.430), channel_id=1, source_target_pairs={{0,8},{8,16},{16,24},{24,28},{28,20},{20,12},{12,4},{4,0},{1,9},{9... | collective-permute-start | bytes 1216520 | tf_op jit(solution)/shard_map/ppermute | solution.py:67
  236.9 17.6 %collective-permute-start.69 = (bf16[198,1024]{1,0:T(8,128)(2,1)S(1)}, bf16[198,1024]{1,0:T(8,128)(2,1)S(1)}, u32[]{:S(2)}, u32[]{:S(2)}) collective-permute-start(bf16[198,1024]{1,0:T(8,128)(2,1)S(1)} %get-tuple-element.447), channel_id=1, source_target_pairs={{0,4},{8,0},{16,8},{24,16},{28,24},{20,28},{12,20},{4,12},{1,5},{9... | collective-permute-start | bytes 1216520 | tf_op jit(solution)/shard_map/ppermute | solution.py:67
  254.6 12.4 %collective-permute-start.77 = (bf16[198,1024]{1,0:T(8,128)(2,1)S(1)}, bf16[198,1024]{1,0:T(8,128)(2,1)S(1)}, u32[]{:S(2)}, u32[]{:S(2)}) collective-permute-start(bf16[198,1024]{1,0:T(8,128)(2,1)S(1)} %get-tuple-element.469), channel_id=1, source_target_pairs={{0,8},{8,16},{16,24},{24,28},{28,20},{20,12},{12,4},{4,0},{1,9},{9... | collective-permute-start | bytes 1216520 | tf_op jit(solution)/shard_map/ppermute | solution.py:67
  255.1 14.1 %collective-permute-start.78 = (bf16[198,1024]{1,0:T(8,128)(2,1)S(1)}, bf16[198,1024]{1,0:T(8,128)(2,1)S(1)}, u32[]{:S(2)}, u32[]{:S(2)}) collective-permute-start(bf16[198,1024]{1,0:T(8,128)(2,1)S(1)} %get-tuple-element.470), channel_id=1, source_target_pairs={{0,4},{8,0},{16,8},{24,16},{28,24},{20,28},{12,20},{4,12},{1,5},{9... | collective-permute-start | bytes 1216520 | tf_op jit(solution)/shard_map/ppermute | solution.py:67
  256.8 15.6 %collective-permute-start.67 = (bf16[128,1536]{1,0:T(8,128)(2,1)S(1)}, bf16[128,1536]{1,0:T(8,128)(2,1)S(1)}, u32[]{:S(2)}, u32[]{:S(2)}) collective-permute-start(bf16[128,1536]{1,0:T(8,128)(2,1)S(1)} %get-tuple-element.516), channel_id=1, source_target_pairs={{0,2},{1,3},{2,0},{3,1},{4,6},{5,7},{6,4},{7,5},{8,10},{9,11},{10,... | collective-permute-start | bytes 1179656 | tf_op jit(solution)/shard_map/ppermute | solution.py:70
  261.3 14.1 %collective-permute-start.82 = (bf16[200,768]{1,0:T(8,128)(2,1)S(1)}, bf16[200,768]{1,0:T(8,128)(2,1)S(1)}, u32[]{:S(2)}, u32[]{:S(2)}) collective-permute-start(bf16[200,768]{1,0:T(8,128)(2,1)S(1)} %get-tuple-element.485), channel_id=1, source_target_pairs={{0,4},{8,0},{16,8},{24,16},{28,24},{20,28},{12,20},{4,12},{1,5},{9... | collective-permute-start | bytes 921608 | tf_op jit(solution)/shard_map/ppermute | solution.py:67
  (49 other events, 546.2 us)

commit v3 on v2

--- a/solution.py
+++ b/solution.py
@@ -14,7 +14,7 @@
 RING = ("rows", "seq")
 MAX_RING = 8
 EXTRA = 8
-PADS = (8, 6, 4)
+PADS = (8, 7, 5)
 RPADS = (6, 4, 6)
 CUTS = (2, 1)
 FREE = pl.CostEstimate(flops=0, transcendentals=0, bytes_accessed=0)

time: 284 us -> 284 us (level)
  no operation moved by 1% of the time
where the time goes in v3:
time: 284 us; the launch traced here: 283 us
  waiting for transfers between devices  140 us (49%)
  starting transfers between devices  81.9 us (29%)
  Pallas kernels  54.1 us (19%)
  local copies, waits for them, and re-layouts  4.19 us (1%)
    ppermute x56, waiting for transfers between devices, shift(): return lax.ppermute(value, RING, self.pairs[step])  127 us
    ppermute x56, starting transfers between devices, shift(): return lax.ppermute(value, RING, self.pairs[step])  57.7 us
    pallas_call x54, Pallas kernels, near(): pl.pallas_call(body, in_specs=[spec] * len(arrays), out_specs=[spec] * le...  51 us
    ppermute x33, starting transfers between devices, partner(): return lax.ppermute(value, 'tp', [(i, i ^ bit) for i in range(self.ways)])  24.2 us
    ppermute x33, waiting for transfers between devices, partner(): return lax.ppermute(value, 'tp', [(i, i ^ bit) for i in range(self.ways)])  13.9 us
  transfers between devices with their start and end apart: 89, of which 48 were waited for; matrix products, arithmetic and copies ran while one was open for 2% of the time, Pallas kernels for 17%

profile of v3, /device:TPU:0, one launch (start us, length us, event | category | flops | bytes accessed | tf_op | source)
XLA Modules:
  0.0 283.4 jit_solution(2986903227864388702)
XLA Ops:
  2.5 2.6 collective-permute-start.6
  7.9 2.1 collective-permute-done.5.refs_2_
  12.1 1.8 collective-permute-start.3
  14.3 4.6 %collective-permute-done.7.refs_1_ = bf16[200,768]{1,0:T(8,128)(2,1)S(1)} collective-permute-done((bf16[200,768]{1,0:T(8,128)(2,1)S(1)}, bf16[200,768]{1,0:T(8,128)(2,1)S(1)}, u32[]{:S(2)}, u32[]{:S(2)}) %collective-permute-start.7) | collective-permute-done | bytes 307232 | tf_op jit(solution)/shard_map/ppermute | solution.py:67
  22.4 5.5 %collective-permute-done.2.refs_2_ = bf16[48,3072]{1,0:T(8,128)(2,1)S(1)} collective-permute-done((bf16[48,3072]{1,0:T(8,128)(2,1)S(1)}, bf16[48,3072]{1,0:T(8,128)(2,1)S(1)}, u32[]{:S(2)}, u32[]{:S(2)}) %collective-permute-start.2) | collective-permute-done | bytes 294944 | tf_op jit(solution)/shard_map/ppermute | solution.py:70
  33.7 6.7 %collective-permute-done.10.refs_2_ = bf16[199,1024]{1,0:T(8,128)(2,1)} collective-permute-done((bf16[199,1024]{1,0:T(8,128)(2,1)S(1)}, bf16[199,1024]{1,0:T(8,128)(2,1)}, u32[]{:S(2)}, u32[]{:S(2)}) %collective-permute-start.10) | collective-permute-done | bytes 407584 | tf_op jit(solution)/shard_map/ppermute | solution.py:67
  44.2 4.4 %collective-permute-done.15.refs_5_ = bf16[200,768]{1,0:T(8,128)(2,1)S(1)} collective-permute-done((bf16[200,768]{1,0:T(8,128)(2,1)S(1)}, bf16[200,768]{1,0:T(8,128)(2,1)S(1)}, u32[]{:S(2)}, u32[]{:S(2)}) %collective-permute-start.15) | collective-permute-done | bytes 307232 | tf_op jit(solution)/shard_map/ppermute | solution.py:67
  51.2 3.2 %collective-permute-done.18.refs_2_ = bf16[200,1024]{1,0:T(8,128)(2,1)} collective-permute-done((bf16[200,1024]{1,0:T(8,128)(2,1)S(1)}, bf16[200,1024]{1,0:T(8,128)(2,1)}, u32[]{:S(2)}, u32[]{:S(2)}) %collective-permute-start.18) | collective-permute-done | bytes 409632 | tf_op jit(solution)/shard_map/ppermute | solution.py:67
  57.9 6.1 %collective-permute-done.17.refs_7_ = bf16[200,768]{1,0:T(8,128)(2,1)S(1)} collective-permute-done((bf16[200,768]{1,0:T(8,128)(2,1)S(1)}, bf16[200,768]{1,0:T(8,128)(2,1)S(1)}, u32[]{:S(2)}, u32[]{:S(2)}) %collective-permute-start.17) | collective-permute-done | bytes 307232 | tf_op jit(solution)/shard_map/ppermute | solution.py:67
  70.1 3.6 %shard_map.236 = (f32[512,192]{1,0:T(8,128)S(1)}, f32[256,1536]{1,0:T(8,128)S(1)}, bf16[256,1536]{1,0:T(8,128)(2,1)S(1)}) custom-call(bf16[512,192]{1,0:T(8,128)(2,1)S(1)} %get-tuple-element.311.q_ref, bf16[1,512,192]{2,1,0:T(8,128)(2,1)S(1)} %bitcast.18, bf16[1,512,192]{2,1,0:T(8,128)(2,1)S(1)} %bitcast.20, f32[3,512]{1,0:T(4,128)S(1)} %fusion.1.w_ref, ...), custom_call_target="tpu_custom_call" | custom-call | tf_op jit(solution)/shard_map/pallas_call | solution.py:338
  76.4 4.7 %collective-permute-done.24.refs_3_ = bf16[199,1024]{1,0:T(8,128)(2,1)S(1)} collective-permute-done((bf16[199,1024]{1,0:T(8,128)(2,1)}, bf16[199,1024]{1,0:T(8,128)(2,1)S(1)}, u32[]{:S(2)}, u32[]{:S(2)}) %collective-permute-start.24) | collective-permute-done | bytes 407584 | tf_op jit(solution)/shard_map/ppermute | solution.py:67
  83.2 3.5 %collective-permute-done.27.refs_4_ = bf16[197,1024]{1,0:T(8,128)(2,1)S(1)} collective-permute-done((bf16[197,1024]{1,0:T(8,128)(2,1)S(1)}, bf16[197,1024]{1,0:T(8,128)(2,1)S(1)}, u32[]{:S(2)}, u32[]{:S(2)}) %collective-permute-start.27) | collective-permute-done | bytes 403488 | tf_op jit(solution)/shard_map/ppermute | solution.py:67
  86.6 3.2 %collective-permute-done.28.refs_3_ = bf16[197,1024]{1,0:T(8,128)(2,1)S(1)} collective-permute-done((bf16[197,1024]{1,0:T(8,128)(2,1)S(1)}, bf16[197,1024]{1,0:T(8,128)(2,1)S(1)}, u32[]{:S(2)}, u32[]{:S(2)}) %collective-permute-start.28) | collective-permute-done | bytes 403488 | tf_op jit(solution)/shard_map/ppermute | solution.py:67
  93.6 1.8 collective-permute-done.34.refs_4_
  99.1 8.3 %collective-permute-done.32.refs_5_ = bf16[199,1024]{1,0:T(8,128)(2,1)S(1)} collective-permute-done((bf16[199,1024]{1,0:T(8,128)(2,1)S(1)}, bf16[199,1024]{1,0:T(8,128)(2,1)S(1)}, u32[]{:S(2)}, u32[]{:S(2)}) %collective-permute-start.32) | collective-permute-done | bytes 407584 | tf_op jit(solution)/shard_map/ppermute | solution.py:67
  109.4 3.9 %collective-permute-done.30.refs_6_ = bf16[197,1024]{1,0:T(8,128)(2,1)S(1)} collective-permute-done((bf16[197,1024]{1,0:T(8,128)(2,1)S(1)}, bf16[197,1024]{1,0:T(8,128)(2,1)S(1)}, u32[]{:S(2)}, u32[]{:S(2)}) %collective-permute-start.30) | collective-permute-done | bytes 403488 | tf_op jit(solution)/shard_map/ppermute | solution.py:67
  113.3 2.8 %collective-permute-done.31.refs_5_ = bf16[197,1024]{1,0:T(8,128)(2,1)S(1)} collective-permute-done((bf16[197,1024]{1,0:T(8,128)(2,1)S(1)}, bf16[197,1024]{1,0:T(8,128)(2,1)S(1)}, u32[]{:S(2)}, u32[]{:S(2)}) %collective-permute-start.31) | collective-permute-done | bytes 403488 | tf_op jit(solution)/shard_map/ppermute | solution.py:67
  118.6 3.0 %collective-permute-done.37.refs_6_ = bf16[200,1024]{1,0:T(8,128)(2,1)S(1)} collective-permute-done((bf16[200,1024]{1,0:T(8,128)(2,1)S(1)}, bf16[200,1024]{1,0:T(8,128)(2,1)S(1)}, u32[]{:S(2)}, u32[]{:S(2)}) %collective-permute-start.37) | collective-permute-done | bytes 409632 | tf_op jit(solution)/shard_map/ppermute | solution.py:67
  121.5 3.4 %collective-permute-done.38.refs_5_ = bf16[200,1024]{1,0:T(8,128)(2,1)S(1)} collective-permute-done((bf16[200,1024]{1,0:T(8,128)(2,1)S(1)}, bf16[200,1024]{1,0:T(8,128)(2,1)S(1)}, u32[]{:S(2)}, u32[]{:S(2)}) %collective-permute-start.38) | collective-permute-done | bytes 409632 | tf_op jit(solution)/shard_map/ppermute | solution.py:67
  127.5 2.2 collective-permute-done.41.refs_7_
  129.7 2.7 collective-permute-done.40.refs_7_
  135.6 4.7 %shard_map.242 = (bf16[512,1024]{1,0:T(8,128)(2,1)S(1)}, f32[512,2048]{1,0:T(8,128)S(1)}) custom-call(bf16[512,1536]{1,0:T(8,128)(2,1)S(1)} %get-tuple-element.341.x_ref.left_ref, bf16[1536,1024]{1,0:T(8,128)(2,1)S(1)} %shard_map.240.gate_ref.refs_0_, bf16[1536,1024]{1,0:T(8,128)(2,1)S(1)} %shard_map.241.up_ref.refs_1_), custom_call_target="tpu_custom_call" | custom-call | tf_op jit(solution)/shard_map/pallas_call | solution.py:338
  141.5 2.1 shard_map.243.blocks_ref
  145.7 2.2 shard_map.246.left_ref.right_ref
  147.9 4.7 %shard_map.247 = (f32[256,1536]{1,0:T(8,128)S(1)}, bf16[256,1536]{1,0:T(8,128)(2,1)S(1)}) custom-call(bf16[512,2048]{1,0:T(8,128)(2,1)S(1)} %shard_map.246.left_ref.right_ref, bf16[1536,1024]{1,0:T(8,128)(2,1)S(1)} %shard_map.240.gate_ref.refs_0_, bf16[1536,1024]{1,0:T(8,128)(2,1)S(1)} %shard_map.241.up_ref.refs_1_), custom_call_target="tpu_custom_call" | custom-call | tf_op jit(solution)/shard_map/pallas_call | solution.py:338
  152.6 2.7 collective-permute-done.44.refs_0_
  155.4 2.5 shard_map.249
  160.5 2.0 shard_map.250.blocks_ref
  162.6 2.0 shard_map.252.blocks_ref
  168.6 2.2 collective-permute-done.50.refs_0_
  173.6 6.0 %collective-permute-done.49.refs_0_ = bf16[198,1024]{1,0:T(8,128)(2,1)S(1)} collective-permute-done((bf16[198,1024]{1,0:T(8,128)(2,1)S(1)}, bf16[198,1024]{1,0:T(8,128)(2,1)S(1)}, u32[]{:S(2)}, u32[]{:S(2)}) %collective-permute-start.49) | collective-permute-done | bytes 405536 | tf_op jit(solution)/shard_map/ppermute | solution.py:67
  182.3 6.1 %collective-permute-done.56.refs_0_ = bf16[198,1024]{1,0:T(8,128)(2,1)S(1)} collective-permute-done((bf16[198,1024]{1,0:T(8,128)(2,1)S(1)}, bf16[198,1024]{1,0:T(8,128)(2,1)S(1)}, u32[]{:S(2)}, u32[]{:S(2)}) %collective-permute-start.56) | collective-permute-done | bytes 405536 | tf_op jit(solution)/shard_map/ppermute | solution.py:67
  191.4 5.7 %collective-permute-done.53.refs_0_ = bf16[196,1024]{1,0:T(8,128)(2,1)S(1)} collective-permute-done((bf16[196,1024]{1,0:T(8,128)(2,1)S(1)}, bf16[196,1024]{1,0:T(8,128)(2,1)S(1)}, u32[]{:S(2)}, u32[]{:S(2)}) %collective-permute-start.53) | collective-permute-done | bytes 401440 | tf_op jit(solution)/shard_map/ppermute | solution.py:67
  200.3 2.1 shard_map.262
  202.4 5.8 %shard_map.263 = (bf16[512,192]{1,0:T(8,128)(2,1)S(1)}, bf16[1,512,192]{2,1,0:T(8,128)(2,1)S(1)}, bf16[1,512,192]{2,1,0:T(8,128)(2,1)S(1)}, f32[1,768]{1,0:T(1,128)S(1)}) custom-call(bf16[512,192]{1,0:T(8,128)(2,1)S(1)} %get-tuple-element.311.q_ref, bf16[1,512,192]{2,1,0:T(8,128)(2,1)S(1)} %bitcast.19, bf16[1,512,192]{2,1,0:T(8,128)(2,1)S(1)} %bitcast.21, ...), custom_call_target="tpu_custom_call" | custom-call | tf_op jit(solution)/shard_map/pallas_call | solution.py:338
  208.2 3.9 %shard_map.264 = (bf16[8,200,768]{2,1,0:T(8,128)(2,1)S(1)}, f32[256,1536]{1,0:T(8,128)S(1)}, bf16[256,1536]{1,0:T(8,128)(2,1)S(1)}) custom-call(bf16[512,1536]{1,0:T(8,128)(2,1)S(1)} %get-tuple-element.407.n_ref, bf16[512,1536]{1,0:T(8,128)(2,1)S(1)} %constant_dynamic-update-slice_fusion.x_ref, f32[512,128]{1,0:T(8,128)S(1)} %get-tuple-element.408.rsq_ref, ...), custom_call_target="tpu_custom_call" | custom-call | tf_op jit(solution)/shard_map/pallas_call | solution.py:338
  218.4 4.2 %collective-permute-done.58.refs_0_ = bf16[196,1024]{1,0:T(8,128)(2,1)S(1)} collective-permute-done((bf16[196,1024]{1,0:T(8,128)(2,1)S(1)}, bf16[196,1024]{1,0:T(8,128)(2,1)S(1)}, u32[]{:S(2)}, u32[]{:S(2)}) %collective-permute-start.58) | collective-permute-done | bytes 401440 | tf_op jit(solution)/shard_map/ppermute | solution.py:67
  222.6 2.0 collective-permute-done.59.refs_1_
  226.9 4.3 %collective-permute-done.66.refs_0_ = bf16[200,768]{1,0:T(8,128)(2,1)S(1)} collective-permute-done((bf16[200,768]{1,0:T(8,128)(2,1)S(1)}, bf16[200,768]{1,0:T(8,128)(2,1)S(1)}, u32[]{:S(2)}, u32[]{:S(2)}) %collective-permute-start.66) | collective-permute-done | bytes 307232 | tf_op jit(solution)/shard_map/ppermute | solution.py:67
  233.4 3.1 %collective-permute-done.70.refs_0_ = bf16[196,1024]{1,0:T(8,128)(2,1)S(1)} collective-permute-done((bf16[196,1024]{1,0:T(8,128)(2,1)S(1)}, bf16[196,1024]{1,0:T(8,128)(2,1)S(1)}, u32[]{:S(2)}, u32[]{:S(2)}) %collective-permute-start.70) | collective-permute-done | bytes 401440 | tf_op jit(solution)/shard_map/ppermute | solution.py:67
  240.2 2.8 collective-permute-done.75.refs_0_
  243.0 3.5 %collective-permute-done.76.refs_1_ = bf16[200,768]{1,0:T(8,128)(2,1)S(1)} collective-permute-done((bf16[200,768]{1,0:T(8,128)(2,1)S(1)}, bf16[200,768]{1,0:T(8,128)(2,1)S(1)}, u32[]{:S(2)}, u32[]{:S(2)}) %collective-permute-start.76) | collective-permute-done | bytes 307232 | tf_op jit(solution)/shard_map/ppermute | solution.py:67
  251.8 2.7 collective-permute-done.73.refs_2_
  256.8 2.4 collective-permute-start.67
  262.8 4.3 %collective-permute-done.77.refs_0_ = bf16[198,1024]{1,0:T(8,128)(2,1)S(1)} collective-permute-done((bf16[198,1024]{1,0:T(8,128)(2,1)S(1)}, bf16[198,1024]{1,0:T(8,128)(2,1)S(1)}, u32[]{:S(2)}, u32[]{:S(2)}) %collective-permute-start.77) | collective-permute-done | bytes 405536 | tf_op jit(solution)/shard_map/ppermute | solution.py:67
  267.0 2.3 collective-permute-done.78.refs_1_
  269.5 2.9 %collective-permute-start.84 = (bf16[48,1024]{1,0:T(8,128)(2,1)S(1)}, bf16[48,1024]{1,0:T(8,128)(2,1)S(1)}, u32[]{:S(2)}, u32[]{:S(2)}) collective-permute-start(bf16[48,1024]{1,0:T(8,128)(2,1)S(1)} %get-tuple-element.481), channel_id=1, source_target_pairs={{0,2},{1,3},{2,0},{3,1},{4,6},{5,7},{6,4},{7,5},{8,10},{9,11},{10,... | collective-permute-start | bytes 294920 | tf_op jit(solution)/shard_map/ppermute | solution.py:70
  272.7 2.7 collective-permute-done.82.refs_1_
  (215 shorter events, 110.3 us)
Async XLA Ops:
  13.9 13.9 %collective-permute-start.2 = (bf16[48,3072]{1,0:T(8,128)(2,1)S(1)}, bf16[48,3072]{1,0:T(8,128)(2,1)S(1)}, u32[]{:S(2)}, u32[]{:S(2)}) collective-permute-start(bf16[48,3072]{1,0:T(8,128)(2,1)S(1)} %get-tuple-element.274), channel_id=1, source_target_pairs={{0,2},{1,3},{2,0},{3,1},{4,6},{5,7},{6,4},{7,5},{8,10},{9,11},{10,... | collective-permute-start | bytes 884744 | tf_op jit(solution)/shard_map/ppermute | solution.py:70
  27.9 12.5 %collective-permute-start.10 = (bf16[199,1024]{1,0:T(8,128)(2,1)S(1)}, bf16[199,1024]{1,0:T(8,128)(2,1)}, u32[]{:S(2)}, u32[]{:S(2)}) collective-permute-start(bf16[199,1024]{1,0:T(8,128)(2,1)S(1)} %get-tuple-element.288.refs_0_), channel_id=1, source_target_pairs={{0,4},{8,0},{16,8},{24,16},{28,24},{20,28},{12,20},{4,12},{1,5},{9... | collective-permute-start | bytes 1222664 | tf_op jit(solution)/shard_map/ppermute | solution.py:67
  29.6 12.5 %collective-permute-start.9 = (bf16[199,1024]{1,0:T(8,128)(2,1)S(1)}, bf16[199,1024]{1,0:T(8,128)(2,1)}, u32[]{:S(2)}, u32[]{:S(2)}) collective-permute-start(bf16[199,1024]{1,0:T(8,128)(2,1)S(1)} %get-tuple-element.288.refs_0_), channel_id=1, source_target_pairs={{0,8},{8,16},{16,24},{24,28},{28,20},{20,12},{12,4},{4,0},{1,9},{9... | collective-permute-start | bytes 1222664 | tf_op jit(solution)/shard_map/ppermute | solution.py:67
  31.7 17.0 %collective-permute-start.15 = (bf16[200,768]{1,0:T(8,128)(2,1)S(1)}, bf16[200,768]{1,0:T(8,128)(2,1)S(1)}, u32[]{:S(2)}, u32[]{:S(2)}) collective-permute-start(bf16[200,768]{1,0:T(8,128)(2,1)S(1)} %collective-permute-done.11.refs_3_), channel_id=1, source_target_pairs={{0,8},{8,16},{16,24},{24,28},{28,20},{20,12},{12,4},{4,0},{1,9},{9... | collective-permute-start | bytes 921608 | tf_op jit(solution)/shard_map/ppermute | solution.py:67
  33.3 15.4 %collective-permute-start.16 = (bf16[200,768]{1,0:T(8,128)(2,1)S(1)}, bf16[200,768]{1,0:T(8,128)(2,1)S(1)}, u32[]{:S(2)}, u32[]{:S(2)}) collective-permute-start(bf16[200,768]{1,0:T(8,128)(2,1)S(1)} %collective-permute-done.12.refs_4_), channel_id=1, source_target_pairs={{0,4},{8,0},{16,8},{24,16},{28,24},{20,28},{12,20},{4,12},{1,5},{9... | collective-permute-start | bytes 921608 | tf_op jit(solution)/shard_map/ppermute | solution.py:67
  40.5 23.9 %collective-permute-start.14 = (bf16[128,1536]{1,0:T(8,128)(2,1)}, bf16[128,1536]{1,0:T(8,128)(2,1)}, u32[]{:S(2)}, u32[]{:S(2)}) collective-permute-start(bf16[128,1536]{1,0:T(8,128)(2,1)} %bitcast.26), channel_id=1, source_target_pairs={{0,2},{1,3},{2,0},{3,1},{4,6},{5,7},{6,4},{7,5},{8,10},{9,11},{10,... | collective-permute-start | bytes 1179656 | tf_op jit(solution)/shard_map/ppermute | solution.py:70
  43.7 13.8 %collective-permute-start.19 = (bf16[200,1024]{1,0:T(8,128)(2,1)S(1)}, bf16[200,1024]{1,0:T(8,128)(2,1)}, u32[]{:S(2)}, u32[]{:S(2)}) collective-permute-start(bf16[200,1024]{1,0:T(8,128)(2,1)S(1)} %get-tuple-element.298.refs_0_), channel_id=1, source_target_pairs={{0,8},{8,16},{16,24},{24,28},{28,20},{20,12},{12,4},{4,0},{1,9},{9... | collective-permute-start | bytes 1228808 | tf_op jit(solution)/shard_map/ppermute | solution.py:67
  48.6 17.4 %collective-permute-start.13 = (bf16[128,1536]{1,0:T(8,128)(2,1)}, bf16[128,1536]{1,0:T(8,128)(2,1)}, u32[]{:S(2)}, u32[]{:S(2)}) collective-permute-start(bf16[128,1536]{1,0:T(8,128)(2,1)} %bitcast), channel_id=1, source_target_pairs={{0,1},{1,0},{2,3},{3,2},{4,5},{5,4},{6,7},{7,6},{8,9},{9,8},{10,11... | collective-permute-start | bytes 1179656 | tf_op jit(solution)/shard_map/ppermute | solution.py:70
  48.6 15.4 %collective-permute-start.17 = (bf16[200,768]{1,0:T(8,128)(2,1)S(1)}, bf16[200,768]{1,0:T(8,128)(2,1)S(1)}, u32[]{:S(2)}, u32[]{:S(2)}) collective-permute-start(bf16[200,768]{1,0:T(8,128)(2,1)S(1)} %collective-permute-done.15.refs_5_), channel_id=1, source_target_pairs={{0,8},{8,16},{16,24},{24,28},{28,20},{20,12},{12,4},{4,0},{1,9},{9... | collective-permute-start | bytes 921608 | tf_op jit(solution)/shard_map/ppermute | solution.py:67
  54.4 19.4 %collective-permute-start.21 = (bf16[197,1024]{1,0:T(8,128)(2,1)}, bf16[197,1024]{1,0:T(8,128)(2,1)S(1)}, u32[]{:S(2)}, u32[]{:S(2)}) collective-permute-start(bf16[197,1024]{1,0:T(8,128)(2,1)} %copy-done.2), channel_id=1, source_target_pairs={{0,4},{8,0},{16,8},{24,16},{28,24},{20,28},{12,20},{4,12},{1,5},{9... | collective-permute-start | bytes 1210376 | tf_op jit(solution)/shard_map/ppermute | solution.py:67
  57.5 16.2 %collective-permute-start.22 = (bf16[197,1024]{1,0:T(8,128)(2,1)}, bf16[197,1024]{1,0:T(8,128)(2,1)S(1)}, u32[]{:S(2)}, u32[]{:S(2)}) collective-permute-start(bf16[197,1024]{1,0:T(8,128)(2,1)} %copy-done.2), channel_id=1, source_target_pairs={{0,8},{8,16},{16,24},{24,28},{28,20},{20,12},{12,4},{4,0},{1,9},{9... | collective-permute-start | bytes 1210376 | tf_op jit(solution)/shard_map/ppermute | solution.py:67
  64.0 17.1 %collective-permute-start.24 = (bf16[199,1024]{1,0:T(8,128)(2,1)}, bf16[199,1024]{1,0:T(8,128)(2,1)S(1)}, u32[]{:S(2)}, u32[]{:S(2)}) collective-permute-start(bf16[199,1024]{1,0:T(8,128)(2,1)} %collective-permute-done.9.refs_1_), channel_id=1, source_target_pairs={{0,8},{8,16},{16,24},{24,28},{28,20},{20,12},{12,4},{4,0},{1,9},{9... | collective-permute-start | bytes 1222664 | tf_op jit(solution)/shard_map/ppermute | solution.py:67
  64.4 16.7 %collective-permute-start.25 = (bf16[199,1024]{1,0:T(8,128)(2,1)}, bf16[199,1024]{1,0:T(8,128)(2,1)S(1)}, u32[]{:S(2)}, u32[]{:S(2)}) collective-permute-start(bf16[199,1024]{1,0:T(8,128)(2,1)} %collective-permute-done.10.refs_2_), channel_id=1, source_target_pairs={{0,4},{8,0},{16,8},{24,16},{28,24},{20,28},{12,20},{4,12},{1,5},{9... | collective-permute-start | bytes 1222664 | tf_op jit(solution)/shard_map/ppermute | solution.py:67
  75.9 13.9 %collective-permute-start.28 = (bf16[197,1024]{1,0:T(8,128)(2,1)S(1)}, bf16[197,1024]{1,0:T(8,128)(2,1)S(1)}, u32[]{:S(2)}, u32[]{:S(2)}) collective-permute-start(bf16[197,1024]{1,0:T(8,128)(2,1)S(1)} %collective-permute-done.22.refs_1_), channel_id=1, source_target_pairs={{0,8},{8,16},{16,24},{24,28},{28,20},{20,12},{12,4},{4,0},{1,9},{9... | collective-permute-start | bytes 1210376 | tf_op jit(solution)/shard_map/ppermute | solution.py:67
  81.1 14.4 %collective-permute-start.34 = (bf16[200,1024]{1,0:T(8,128)(2,1)}, bf16[200,1024]{1,0:T(8,128)(2,1)S(1)}, u32[]{:S(2)}, u32[]{:S(2)}) collective-permute-start(bf16[200,1024]{1,0:T(8,128)(2,1)} %collective-permute-done.18.refs_2_), channel_id=1, source_target_pairs={{0,4},{8,0},{16,8},{24,16},{28,24},{20,28},{12,20},{4,12},{1,5},{9... | collective-permute-start | bytes 1228808 | tf_op jit(solution)/shard_map/ppermute | solution.py:67
  82.7 15.9 %collective-permute-start.35 = (bf16[200,1024]{1,0:T(8,128)(2,1)}, bf16[200,1024]{1,0:T(8,128)(2,1)S(1)}, u32[]{:S(2)}, u32[]{:S(2)}) collective-permute-start(bf16[200,1024]{1,0:T(8,128)(2,1)} %collective-permute-done.19.refs_1_), channel_id=1, source_target_pairs={{0,8},{8,16},{16,24},{24,28},{28,20},{20,12},{12,4},{4,0},{1,9},{9... | collective-permute-start | bytes 1228808 | tf_op jit(solution)/shard_map/ppermute | solution.py:67
  90.0 26.1 %collective-permute-start.29 = (bf16[256,1536]{1,0:T(8,128)(2,1)S(1)}, bf16[256,1536]{1,0:T(8,128)(2,1)S(1)}, u32[]{:S(2)}, u32[]{:S(2)}) collective-permute-start(bf16[256,1536]{1,0:T(8,128)(2,1)S(1)} %shard_map.237.left_ref), channel_id=1, source_target_pairs={{0,2},{1,3},{2,0},{3,1},{4,6},{5,7},{6,4},{7,5},{8,10},{9,11},{10,... | collective-permute-start | bytes 2359304 | tf_op jit(solution)/shard_map/ppermute | solution.py:70
  91.6 15.8 %collective-permute-start.32 = (bf16[199,1024]{1,0:T(8,128)(2,1)S(1)}, bf16[199,1024]{1,0:T(8,128)(2,1)S(1)}, u32[]{:S(2)}, u32[]{:S(2)}) collective-permute-start(bf16[199,1024]{1,0:T(8,128)(2,1)S(1)} %collective-permute-done.24.refs_3_), channel_id=1, source_target_pairs={{0,8},{8,16},{16,24},{24,28},{28,20},{20,12},{12,4},{4,0},{1,9},{9... | collective-permute-start | bytes 1222664 | tf_op jit(solution)/shard_map/ppermute | solution.py:67
  92.1 16.8 %collective-permute-start.33 = (bf16[199,1024]{1,0:T(8,128)(2,1)S(1)}, bf16[199,1024]{1,0:T(8,128)(2,1)S(1)}, u32[]{:S(2)}, u32[]{:S(2)}) collective-permute-start(bf16[199,1024]{1,0:T(8,128)(2,1)S(1)} %collective-permute-done.25.refs_4_), channel_id=1, source_target_pairs={{0,4},{8,0},{16,8},{24,16},{28,24},{20,28},{12,20},{4,12},{1,5},{9... | collective-permute-start | bytes 1222664 | tf_op jit(solution)/shard_map/ppermute | solution.py:67
  95.4 17.9 %collective-permute-start.30 = (bf16[197,1024]{1,0:T(8,128)(2,1)S(1)}, bf16[197,1024]{1,0:T(8,128)(2,1)S(1)}, u32[]{:S(2)}, u32[]{:S(2)}) collective-permute-start(bf16[197,1024]{1,0:T(8,128)(2,1)S(1)} %collective-permute-done.27.refs_4_), channel_id=1, source_target_pairs={{0,4},{8,0},{16,8},{24,16},{28,24},{20,28},{12,20},{4,12},{1,5},{9... | collective-permute-start | bytes 1210376 | tf_op jit(solution)/shard_map/ppermute | solution.py:67
  98.6 17.6 %collective-permute-start.31 = (bf16[197,1024]{1,0:T(8,128)(2,1)S(1)}, bf16[197,1024]{1,0:T(8,128)(2,1)S(1)}, u32[]{:S(2)}, u32[]{:S(2)}) collective-permute-start(bf16[197,1024]{1,0:T(8,128)(2,1)S(1)} %collective-permute-done.28.refs_3_), channel_id=1, source_target_pairs={{0,8},{8,16},{16,24},{24,28},{28,20},{20,12},{12,4},{4,0},{1,9},{9... | collective-permute-start | bytes 1210376 | tf_op jit(solution)/shard_map/ppermute | solution.py:67
  107.4 14.2 %collective-permute-start.37 = (bf16[200,1024]{1,0:T(8,128)(2,1)S(1)}, bf16[200,1024]{1,0:T(8,128)(2,1)S(1)}, u32[]{:S(2)}, u32[]{:S(2)}) collective-permute-start(bf16[200,1024]{1,0:T(8,128)(2,1)S(1)} %collective-permute-done.34.refs_4_), channel_id=1, source_target_pairs={{0,4},{8,0},{16,8},{24,16},{28,24},{20,28},{12,20},{4,12},{1,5},{9... | collective-permute-start | bytes 1228808 | tf_op jit(solution)/shard_map/ppermute | solution.py:67
  109.0 16.0 %collective-permute-start.38 = (bf16[200,1024]{1,0:T(8,128)(2,1)S(1)}, bf16[200,1024]{1,0:T(8,128)(2,1)S(1)}, u32[]{:S(2)}, u32[]{:S(2)}) collective-permute-start(bf16[200,1024]{1,0:T(8,128)(2,1)S(1)} %collective-permute-done.35.refs_3_), channel_id=1, source_target_pairs={{0,8},{8,16},{16,24},{24,28},{28,20},{20,12},{12,4},{4,0},{1,9},{9... | collective-permute-start | bytes 1228808 | tf_op jit(solution)/shard_map/ppermute | solution.py:67
  116.5 15.9 %collective-permute-start.40 = (bf16[199,1024]{1,0:T(8,128)(2,1)S(1)}, bf16[199,1024]{1,0:T(8,128)(2,1)S(1)}, u32[]{:S(2)}, u32[]{:S(2)}) collective-permute-start(bf16[199,1024]{1,0:T(8,128)(2,1)S(1)} %collective-permute-done.32.refs_5_), channel_id=1, source_target_pairs={{0,8},{8,16},{16,24},{24,28},{28,20},{20,12},{12,4},{4,0},{1,9},{9... | collective-permute-start | bytes 1222664 | tf_op jit(solution)/shard_map/ppermute | solution.py:67
  117.0 12.6 %collective-permute-start.41 = (bf16[197,1024]{1,0:T(8,128)(2,1)S(1)}, bf16[197,1024]{1,0:T(8,128)(2,1)S(1)}, u32[]{:S(2)}, u32[]{:S(2)}) collective-permute-start(bf16[197,1024]{1,0:T(8,128)(2,1)S(1)} %collective-permute-done.30.refs_6_), channel_id=1, source_target_pairs={{0,4},{8,0},{16,8},{24,16},{28,24},{20,28},{12,20},{4,12},{1,5},{9... | collective-permute-start | bytes 1210376 | tf_op jit(solution)/shard_map/ppermute | solution.py:67
  165.1 24.0 %collective-permute-start.55 = (bf16[256,1536]{1,0:T(8,128)(2,1)S(1)}, bf16[256,1536]{1,0:T(8,128)(2,1)S(1)}, u32[]{:S(2)}, u32[]{:S(2)}) collective-permute-start(bf16[256,1536]{1,0:T(8,128)(2,1)S(1)} %shard_map.255.left_ref), channel_id=1, source_target_pairs={{0,2},{1,3},{2,0},{3,1},{4,6},{5,7},{6,4},{7,5},{8,10},{9,11},{10,... | collective-permute-start | bytes 2359304 | tf_op jit(solution)/shard_map/ppermute | solution.py:70
  166.6 13.0 %collective-permute-start.49 = (bf16[198,1024]{1,0:T(8,128)(2,1)S(1)}, bf16[198,1024]{1,0:T(8,128)(2,1)S(1)}, u32[]{:S(2)}, u32[]{:S(2)}) collective-permute-start(bf16[198,1024]{1,0:T(8,128)(2,1)S(1)} %shard_map.254), channel_id=1, source_target_pairs={{0,8},{8,16},{16,24},{24,28},{28,20},{20,12},{12,4},{4,0},{1,9},{9... | collective-permute-start | bytes 1216520 | tf_op jit(solution)/shard_map/ppermute | solution.py:67
  167.1 13.0 %collective-permute-start.48 = (bf16[196,1024]{1,0:T(8,128)(2,1)S(1)}, bf16[196,1024]{1,0:T(8,128)(2,1)S(1)}, u32[]{:S(2)}, u32[]{:S(2)}) collective-permute-start(bf16[196,1024]{1,0:T(8,128)(2,1)S(1)} %shard_map.251), channel_id=1, source_target_pairs={{0,4},{8,0},{16,8},{24,16},{28,24},{20,28},{12,20},{4,12},{1,5},{9... | collective-permute-start | bytes 1204232 | tf_op jit(solution)/shard_map/ppermute | solution.py:67
  171.5 16.9 %collective-permute-start.56 = (bf16[198,1024]{1,0:T(8,128)(2,1)S(1)}, bf16[198,1024]{1,0:T(8,128)(2,1)S(1)}, u32[]{:S(2)}, u32[]{:S(2)}) collective-permute-start(bf16[198,1024]{1,0:T(8,128)(2,1)S(1)} %get-tuple-element.382), channel_id=1, source_target_pairs={{0,8},{8,16},{16,24},{24,28},{28,20},{20,12},{12,4},{4,0},{1,9},{9... | collective-permute-start | bytes 1216520 | tf_op jit(solution)/shard_map/ppermute | solution.py:67
  172.0 16.9 %collective-permute-start.57 = (bf16[198,1024]{1,0:T(8,128)(2,1)S(1)}, bf16[198,1024]{1,0:T(8,128)(2,1)S(1)}, u32[]{:S(2)}, u32[]{:S(2)}) collective-permute-start(bf16[198,1024]{1,0:T(8,128)(2,1)S(1)} %get-tuple-element.392), channel_id=1, source_target_pairs={{0,4},{8,0},{16,8},{24,16},{28,24},{20,28},{12,20},{4,12},{1,5},{9... | collective-permute-start | bytes 1216520 | tf_op jit(solution)/shard_map/ppermute | solution.py:67
  180.2 16.9 %collective-permute-start.53 = (bf16[196,1024]{1,0:T(8,128)(2,1)S(1)}, bf16[196,1024]{1,0:T(8,128)(2,1)S(1)}, u32[]{:S(2)}, u32[]{:S(2)}) collective-permute-start(bf16[196,1024]{1,0:T(8,128)(2,1)S(1)} %get-tuple-element.390), channel_id=1, source_target_pairs={{0,8},{8,16},{16,24},{24,28},{28,20},{20,12},{12,4},{4,0},{1,9},{9... | collective-permute-start | bytes 1204232 | tf_op jit(solution)/shard_map/ppermute | solution.py:67
  180.7 16.9 %collective-permute-start.54 = (bf16[196,1024]{1,0:T(8,128)(2,1)S(1)}, bf16[196,1024]{1,0:T(8,128)(2,1)S(1)}, u32[]{:S(2)}, u32[]{:S(2)}) collective-permute-start(bf16[196,1024]{1,0:T(8,128)(2,1)S(1)} %get-tuple-element.391), channel_id=1, source_target_pairs={{0,4},{8,0},{16,8},{24,16},{28,24},{20,28},{12,20},{4,12},{1,5},{9... | collective-permute-start | bytes 1204232 | tf_op jit(solution)/shard_map/ppermute | solution.py:67
  189.3 22.8 %collective-permute-start.63 = (bf16[198,1024]{1,0:T(8,128)(2,1)S(1)}, bf16[198,1024]{1,0:T(8,128)(2,1)S(1)}, u32[]{:S(2)}, u32[]{:S(2)}) collective-permute-start(bf16[198,1024]{1,0:T(8,128)(2,1)S(1)} %get-tuple-element.386), channel_id=1, source_target_pairs={{0,8},{8,16},{16,24},{24,28},{28,20},{20,12},{12,4},{4,0},{1,9},{9... | collective-permute-start | bytes 1216520 | tf_op jit(solution)/shard_map/ppermute | solution.py:67
  189.8 23.9 %collective-permute-start.64 = (bf16[198,1024]{1,0:T(8,128)(2,1)S(1)}, bf16[198,1024]{1,0:T(8,128)(2,1)S(1)}, u32[]{:S(2)}, u32[]{:S(2)}) collective-permute-start(bf16[198,1024]{1,0:T(8,128)(2,1)S(1)} %get-tuple-element.425), channel_id=1, source_target_pairs={{0,4},{8,0},{16,8},{24,16},{28,24},{20,28},{12,20},{4,12},{1,5},{9... | collective-permute-start | bytes 1216520 | tf_op jit(solution)/shard_map/ppermute | solution.py:67
  197.1 17.6 %collective-permute-start.61 = (bf16[198,1024]{1,0:T(8,128)(2,1)S(1)}, bf16[198,1024]{1,0:T(8,128)(2,1)S(1)}, u32[]{:S(2)}, u32[]{:S(2)}) collective-permute-start(bf16[198,1024]{1,0:T(8,128)(2,1)S(1)} %get-tuple-element.397), channel_id=1, source_target_pairs={{0,8},{8,16},{16,24},{24,28},{28,20},{20,12},{12,4},{4,0},{1,9},{9... | collective-permute-start | bytes 1216520 | tf_op jit(solution)/shard_map/ppermute | solution.py:67
  197.6 17.6 %collective-permute-start.62 = (bf16[198,1024]{1,0:T(8,128)(2,1)S(1)}, bf16[198,1024]{1,0:T(8,128)(2,1)S(1)}, u32[]{:S(2)}, u32[]{:S(2)}) collective-permute-start(bf16[198,1024]{1,0:T(8,128)(2,1)S(1)} %get-tuple-element.424), channel_id=1, source_target_pairs={{0,4},{8,0},{16,8},{24,16},{28,24},{20,28},{12,20},{4,12},{1,5},{9... | collective-permute-start | bytes 1216520 | tf_op jit(solution)/shard_map/ppermute | solution.py:67
  199.6 23.0 %collective-permute-start.58 = (bf16[196,1024]{1,0:T(8,128)(2,1)S(1)}, bf16[196,1024]{1,0:T(8,128)(2,1)S(1)}, u32[]{:S(2)}, u32[]{:S(2)}) collective-permute-start(bf16[196,1024]{1,0:T(8,128)(2,1)S(1)} %get-tuple-element.405), channel_id=1, source_target_pairs={{0,8},{8,16},{16,24},{24,28},{28,20},{20,12},{12,4},{4,0},{1,9},{9... | collective-permute-start | bytes 1204232 | tf_op jit(solution)/shard_map/ppermute | solution.py:67
  212.1 12.5 %collective-permute-start.59 = (bf16[196,1024]{1,0:T(8,128)(2,1)S(1)}, bf16[196,1024]{1,0:T(8,128)(2,1)S(1)}, u32[]{:S(2)}, u32[]{:S(2)}) collective-permute-start(bf16[196,1024]{1,0:T(8,128)(2,1)S(1)} %get-tuple-element.406), channel_id=1, source_target_pairs={{0,4},{8,0},{16,8},{24,16},{28,24},{20,28},{12,20},{4,12},{1,5},{9... | collective-permute-start | bytes 1204232 | tf_op jit(solution)/shard_map/ppermute | solution.py:67
  215.2 21.7 %collective-permute-start.65 = (bf16[256,1536]{1,0:T(8,128)(2,1)S(1)}, bf16[256,1536]{1,0:T(8,128)(2,1)S(1)}, u32[]{:S(2)}, u32[]{:S(2)}) collective-permute-start(bf16[256,1536]{1,0:T(8,128)(2,1)S(1)} %get-tuple-element.432), channel_id=1, source_target_pairs={{0,1},{1,0},{2,3},{3,2},{4,5},{5,4},{6,7},{7,6},{8,9},{9,8},{10,11... | collective-permute-start | bytes 2359304 | tf_op jit(solution)/shard_map/ppermute | solution.py:70
  216.8 14.3 %collective-permute-start.66 = (bf16[200,768]{1,0:T(8,128)(2,1)S(1)}, bf16[200,768]{1,0:T(8,128)(2,1)S(1)}, u32[]{:S(2)}, u32[]{:S(2)}) collective-permute-start(bf16[200,768]{1,0:T(8,128)(2,1)S(1)} %shard_map.265), channel_id=1, source_target_pairs={{0,4},{8,0},{16,8},{24,16},{28,24},{20,28},{12,20},{4,12},{1,5},{9... | collective-permute-start | bytes 921608 | tf_op jit(solution)/shard_map/ppermute | solution.py:67
  225.3 14.7 %collective-permute-start.71 = (bf16[196,1024]{1,0:T(8,128)(2,1)S(1)}, bf16[196,1024]{1,0:T(8,128)(2,1)S(1)}, u32[]{:S(2)}, u32[]{:S(2)}) collective-permute-start(bf16[196,1024]{1,0:T(8,128)(2,1)S(1)} %get-tuple-element.449), channel_id=1, source_target_pairs={{0,4},{8,0},{16,8},{24,16},{28,24},{20,28},{12,20},{4,12},{1,5},{9... | collective-permute-start | bytes 1204232 | tf_op jit(solution)/shard_map/ppermute | solution.py:67
  231.8 14.7 %collective-permute-start.76 = (bf16[200,768]{1,0:T(8,128)(2,1)S(1)}, bf16[200,768]{1,0:T(8,128)(2,1)S(1)}, u32[]{:S(2)}, u32[]{:S(2)}) collective-permute-start(bf16[200,768]{1,0:T(8,128)(2,1)S(1)} %get-tuple-element.458), channel_id=1, source_target_pairs={{0,4},{8,0},{16,8},{24,16},{28,24},{20,28},{12,20},{4,12},{1,5},{9... | collective-permute-start | bytes 921608 | tf_op jit(solution)/shard_map/ppermute | solution.py:67
  236.4 18.0 %collective-permute-start.68 = (bf16[198,1024]{1,0:T(8,128)(2,1)S(1)}, bf16[198,1024]{1,0:T(8,128)(2,1)S(1)}, u32[]{:S(2)}, u32[]{:S(2)}) collective-permute-start(bf16[198,1024]{1,0:T(8,128)(2,1)S(1)} %get-tuple-element.430), channel_id=1, source_target_pairs={{0,8},{8,16},{16,24},{24,28},{28,20},{20,12},{12,4},{4,0},{1,9},{9... | collective-permute-start | bytes 1216520 | tf_op jit(solution)/shard_map/ppermute | solution.py:67
  236.9 17.5 %collective-permute-start.69 = (bf16[198,1024]{1,0:T(8,128)(2,1)S(1)}, bf16[198,1024]{1,0:T(8,128)(2,1)S(1)}, u32[]{:S(2)}, u32[]{:S(2)}) collective-permute-start(bf16[198,1024]{1,0:T(8,128)(2,1)S(1)} %get-tuple-element.447), channel_id=1, source_target_pairs={{0,4},{8,0},{16,8},{24,16},{28,24},{20,28},{12,20},{4,12},{1,5},{9... | collective-permute-start | bytes 1216520 | tf_op jit(solution)/shard_map/ppermute | solution.py:67
  254.7 12.4 %collective-permute-start.77 = (bf16[198,1024]{1,0:T(8,128)(2,1)S(1)}, bf16[198,1024]{1,0:T(8,128)(2,1)S(1)}, u32[]{:S(2)}, u32[]{:S(2)}) collective-permute-start(bf16[198,1024]{1,0:T(8,128)(2,1)S(1)} %get-tuple-element.469), channel_id=1, source_target_pairs={{0,8},{8,16},{16,24},{24,28},{28,20},{20,12},{12,4},{4,0},{1,9},{9... | collective-permute-start | bytes 1216520 | tf_op jit(solution)/shard_map/ppermute | solution.py:67
  255.1 14.2 %collective-permute-start.78 = (bf16[198,1024]{1,0:T(8,128)(2,1)S(1)}, bf16[198,1024]{1,0:T(8,128)(2,1)S(1)}, u32[]{:S(2)}, u32[]{:S(2)}) collective-permute-start(bf16[198,1024]{1,0:T(8,128)(2,1)S(1)} %get-tuple-element.470), channel_id=1, source_target_pairs={{0,4},{8,0},{16,8},{24,16},{28,24},{20,28},{12,20},{4,12},{1,5},{9... | collective-permute-start | bytes 1216520 | tf_op jit(solution)/shard_map/ppermute | solution.py:67
  256.8 15.6 %collective-permute-start.67 = (bf16[128,1536]{1,0:T(8,128)(2,1)S(1)}, bf16[128,1536]{1,0:T(8,128)(2,1)S(1)}, u32[]{:S(2)}, u32[]{:S(2)}) collective-permute-start(bf16[128,1536]{1,0:T(8,128)(2,1)S(1)} %get-tuple-element.516), channel_id=1, source_target_pairs={{0,2},{1,3},{2,0},{3,1},{4,6},{5,7},{6,4},{7,5},{8,10},{9,11},{10,... | collective-permute-start | bytes 1179656 | tf_op jit(solution)/shard_map/ppermute | solution.py:70
  261.3 14.1 %collective-permute-start.82 = (bf16[200,768]{1,0:T(8,128)(2,1)S(1)}, bf16[200,768]{1,0:T(8,128)(2,1)S(1)}, u32[]{:S(2)}, u32[]{:S(2)}) collective-permute-start(bf16[200,768]{1,0:T(8,128)(2,1)S(1)} %get-tuple-element.485), channel_id=1, source_target_pairs={{0,4},{8,0},{16,8},{24,16},{28,24},{20,28},{12,20},{4,12},{1,5},{9... | collective-permute-start | bytes 921608 | tf_op jit(solution)/shard_map/ppermute | solution.py:67
  (49 other events, 546.3 us)
